TPU v7x, 32 devices: a whole 2x2x4 slice. The times are simulated.
32 devices in a mesh: azim: 8 (over z, y), axial: 4 (over x, core).
Axes of the slice: x: 2, y: 2, z: 4, core: 2. Of those that a mesh axis runs over, the one named last changes fastest.
Arguments:
- observed_heights: bfloat16 [4, 8, 1024, 1024], P('axial', 'azim'), may hold values from -6 to 6
- ref_map: float32 [1024, 1024], P(('azim', 'axial')), may hold values from -3 to 3
- coefs: float32 [4, 8, 4], P('axial', 'azim'), may hold values from -1.8 to 1.8
- shifts: float32 [4, 8], P('axial', 'azim'), may hold values from 0.1 to 0.9
- pair_offset: int32 [4, 8, 16], P('axial', 'azim'), may hold values from 0 to 255
- pair_width: int32 [4, 8, 16], P('axial', 'azim'), may hold values from 128 to 512
Outputs:
- refined_map: float32 [1024, 1024], P(('azim', 'axial'))
- refined_coefs: float32 [4, 8, 4], P('axial', 'azim')
All inputs are finite; a program needn't handle non-finite values.
Results may differ from a plain program's by a relative error of at most 0.0041.
Values may be sent and summed in bfloat16 or wider, within the bound.
No kernel may reach another device: no remote copies, remote signals or barrier semaphores. Data moves between devices by JAX's collectives and lax.ppermute only.
A program may use at most 64 MiB of HBM per device.

v0:
```python
import math

import jax
import jax.numpy as jnp
from jax import lax
from jax.sharding import PartitionSpec as P

PASSES = 2


window_width = 16.0


def from_behind(block, axis, distance):
    devices = range(lax.axis_size(axis))
    route = [((i - distance) % len(devices), i) for i in devices]
    return lax.ppermute(block, axis, route)


def grid_terms(row_total, col_total):
    lengthwise = (jnp.arange(row_total, dtype=jnp.float32) - 0.5 * (row_total - 1)) * (
        2.0 / row_total
    )
    angular_place = (jnp.arange(col_total, dtype=jnp.float32) - 0.5 * (col_total - 1)) * (
        2.0 / col_total
    )
    return (lengthwise[:, None], angular_place[None, :])


def registration(coef_vec, lengthwise, angular_place):
    return (
        coef_vec[0]
        + coef_vec[1] * angular_place
        + coef_vec[2] * lengthwise
        + coef_vec[3] * (angular_place * angular_place + lengthwise * lengthwise - 2.0 / 3.0)
    )


def resampler(shift_value, col_total):
    source = jnp.arange(col_total, dtype=jnp.float32)[:, None]
    target = jnp.arange(col_total, dtype=jnp.float32)[None, :]
    offset = source - target - shift_value
    return (jnp.sinc(offset) * jnp.exp(-(offset * offset) / (window_width * window_width))).astype(
        jnp.bfloat16
    )


def coef_gradient(pulled, lengthwise, angular_place):
    return jnp.stack(
        [
            jnp.sum(pulled),
            jnp.sum(pulled * angular_place),
            jnp.sum(pulled * lengthwise),
            jnp.sum(pulled * (angular_place * angular_place + lengthwise * lengthwise - 2.0 / 3.0)),
        ]
    )


def seam_residual(own_strip, next_strip, lower, extent):
    columns = jnp.arange(own_strip.shape[-1], dtype=jnp.int32)
    low_edge = lower[..., None, None]
    window_mask = (columns >= low_edge) & (columns < low_edge + extent[..., None, None])
    difference = own_strip.astype(jnp.float32) - next_strip.astype(jnp.float32)
    return jnp.where(window_mask, difference, 0.0).astype(jnp.bfloat16)


def reduce_share(pulled):
    return lax.psum_scatter(pulled, ("azim", "axial"), scatter_dimension=0, tiled=True)


def local(observed_heights, ref_map, coefs, shifts, pair_offset, pair_width):
    height_map_solo = observed_heights[0, 0]
    lengthwise_tally, angular_tally = height_map_solo.shape
    half_cols = angular_tally // 2
    pair_count = pair_offset.shape[2]
    band_rows = lengthwise_tally // pair_count
    device_count = lax.axis_size("azim") * lax.axis_size("axial")
    mixer = resampler(shifts[0, 0], angular_tally)
    axial_all, angular_place = grid_terms(lengthwise_tally, angular_tally)
    offsets = pair_offset[0, 0]
    widths = pair_width[0, 0]

    def banded(strip):
        return strip.reshape(pair_count, band_rows, half_cols)

    coef_now = coefs[0, 0]
    ref_rows = ref_map
    for pass_index in range(PASSES):
        row_block = lax.all_gather(
            ref_rows.astype(jnp.bfloat16), ("azim", "axial"), axis=0, tiled=True
        )
        tile_lines = row_block.shape[0]
        height_lines = lax.slice_in_dim(height_map_solo, 0, tile_lines, axis=0)
        axial_rows = lax.slice_in_dim(axial_all, 0, tile_lines, axis=0)
        repaired_heights = (
            height_lines.astype(jnp.float32)
            - row_block.astype(jnp.float32)
            - registration(coef_now, axial_rows, angular_place)
        ).astype(jnp.bfloat16)
        regridded = jnp.dot(repaired_heights, mixer, preferred_element_type=jnp.float32).astype(
            jnp.bfloat16
        )
        own_left = regridded[:, :half_cols]
        own_right = regridded[:, half_cols:]
        next_left = from_behind(own_left, "azim", -1)
        seam_rows = seam_residual(banded(own_right), banded(next_left), offsets, widths).reshape(
            lengthwise_tally, half_cols
        )
        from_left = from_behind(seam_rows, "azim", 1)
        upstream = jnp.concatenate([-from_left, seam_rows], axis=1)
        pulled = lax.dot_general(
            upstream, mixer, (((1,), (1,)), ((), ())), preferred_element_type=jnp.float32
        )
        new_coef = coef_now + coef_gradient(pulled, axial_all, angular_place) / (
            lengthwise_tally * angular_tally
        )
        pulled, coef_now = (pulled, new_coef)
        ref_rows = ref_rows + reduce_share(pulled) / math.sqrt(device_count)
    return (ref_rows, coef_now.reshape(1, 1, coef_now.shape[0]))


def solution(mesh):
    in_specs = (
        P("axial", "azim", None, None),
        P(("azim", "axial"), None),
        P("axial", "azim", None),
        P("axial", "azim"),
        P("axial", "azim", None),
        P("axial", "azim", None),
    )
    out_specs = (P(("azim", "axial"), None), P("axial", "azim", None))
    return jax.shard_map(local, mesh=mesh, in_specs=in_specs, out_specs=out_specs, check_vma=False)
```

profile of v0, /device:TPU:0, one launch (start us, length us, event | category | flops | bytes accessed | tf_op | source)
XLA Modules:
  0.0 565.7 jit_solution(2285652827476224226)
XLA Ops:
  7.2 1.5 convert_element_type.65
  9.5 1.4 fusion.122
  12.1 0.6 multiply_add_fusion.4
  12.7 57.8 %all-gather.3.cloned.1.call-done = bf16[1024,1024]{1,0:T(8,128)(2,1)} async-done(((bf16[32,1024]{1,0:T(8,128)(2,1)}), bf16[1024,1024]{1,0:T(8,128)(2,1)}) %all-gather.3.cloned.1.call-update) | async-done | bytes 2097168 | tf_op jit(solution)/shard_map/all_gather | solution.py:89
  70.5 10.9 %fusion.48 = bf16[1024,1024]{0,1:T(8,128)(2,1)S(1)} fusion(f32[]{:T(128)} %bitcast.42, bf16[1024,1024]{1,0:T(8,128)(2,1)} %all-gather.3.cloned.1.call-done, bf16[1,1,1024,1024]{3,2,1,0:T(8,128)(2,1)} %param.6, f32[1024]{0:T(1024)S(1)} %fusion.63, f32[]{:T(128)} %bitcast.7, f32[1024]{0:T(1024)S(1)} %get-tuple-element.25, f32[1024]{0:T(1024)S(1)} %get-tuple-element.24), kind=kOutput, calls=%fused_computation.64 | convolution fusion | flops 2200961024 | bytes 6303752 | tf_op jit(solution)/shard_map/dot_general | solution.py:100
  81.5 1.1 slice.53
  82.5 3.1 collective-permute-start
  85.9 0.9 copy.8
  86.8 22.0 %collective-permute-done = bf16[1024,512]{0,1:T(8,128)(2,1)} collective-permute-done((bf16[1024,512]{0,1:T(8,128)(2,1)}, bf16[1024,512]{0,1:T(8,128)(2,1)}, u32[]{:S(2)}, u32[]{:S(2)}) %collective-permute-start) | collective-permute-done | bytes 1048608 | tf_op jit(solution)/shard_map/ppermute | solution.py:17
  108.8 1.8 select_convert_fusion.1
  110.6 2.0 collective-permute-start.1
  112.6 26.2 %collective-permute-done.1 = bf16[1024,512]{0,1:T(8,128)(2,1)S(1)} collective-permute-done((bf16[1024,512]{0,1:T(8,128)(2,1)S(1)}, bf16[1024,512]{0,1:T(8,128)(2,1)S(1)}, u32[]{:S(2)}, u32[]{:S(2)}) %collective-permute-start.1) | collective-permute-done | bytes 1048608 | tf_op jit(solution)/shard_map/ppermute | solution.py:17
  138.8 0.2 neg.15
  139.0 10.1 %fusion.120 = (f32[]{:T(128)}, f32[]{:T(128)}, f32[]{:T(128)}, f32[]{:T(128)}, f32[1024,1024]{1,0:T(8,128)}) fusion(f32[1024]{0:T(1024)S(1)} %fusion.63, f32[1024]{0:T(1024)S(1)} %fusion.61, f32[]{:T(128)} %bitcast.45, bf16[1024,512]{0,1:T(8,128)(2,1)S(1)} %select_convert_fusion.1, bf16[1024,512]{0,1:T(8,128)(2,1)S(1)} %neg.15), kind=kOutput, calls=%fused_computation.139 | convolution fusion | flops 2203058176 | bytes 6299668 | tf_op jit(solution)/shard_map/dot_general | solution.py:111
  149.2 138.6 %reduce-scatter.3.cloned.1.call-done = f32[32,1024]{1,0:T(8,128)} async-done(((f32[1024,1024]{1,0:T(8,128)}), f32[32,1024]{1,0:T(8,128)}) %reduce-scatter.3.cloned.1.call-update) | async-done | bytes 131088 | tf_op jit(solution)/shard_map/reduce_scatter | solution.py:68
  287.8 1.6 fusion.58
  289.3 0.3 reduce-scatter.5.cloned.1.call-start
  289.6 2.6 fusion.64
  292.2 0.6 fusion.121
  294.0 0.6 multiply_add_fusion.3
  294.6 48.9 %all-gather.5.cloned.1.call-done = bf16[1024,1024]{1,0:T(8,128)(2,1)} async-done(((bf16[32,1024]{1,0:T(8,128)(2,1)}), bf16[1024,1024]{1,0:T(8,128)(2,1)}) %all-gather.5.cloned.1.call-update) | async-done | bytes 2097168 | tf_op jit(solution)/shard_map/all_gather | solution.py:89
  343.5 10.3 %fusion.53 = bf16[1024,1024]{0,1:T(8,128)(2,1)S(1)} fusion(f32[]{:T(128)} %bitcast.44, bf16[1024,1024]{1,0:T(8,128)(2,1)} %all-gather.5.cloned.1.call-done, bf16[1,1,1024,1024]{3,2,1,0:T(8,128)(2,1)S(1)} %copy-done.4, f32[]{:T(128)} %bitcast.18, f32[1024]{0:T(1024)S(1)} %fusion.60, f32[1024]{0:T(1024)S(1)} %multiply_add_fusion.3, f32[1024]{0:T(1024)S(1)} %fusion.63), kind=kOutput, calls=%fused_computation.65 | convolution fusion | flops 2200961024 | bytes 6303752 | tf_op jit(solution)/shard_map/dot_general | solution.py:100
  353.9 3.1 collective-permute-start.2
  357.0 22.8 %collective-permute-done.2 = bf16[1024,512]{0,1:T(8,128)(2,1)S(1)} collective-permute-done((bf16[1024,512]{0,1:T(8,128)(2,1)S(1)}, bf16[1024,512]{0,1:T(8,128)(2,1)S(1)}, u32[]{:S(2)}, u32[]{:S(2)}) %collective-permute-start.2) | collective-permute-done | bytes 1048608 | tf_op jit(solution)/shard_map/ppermute | solution.py:17
  379.8 0.6 select_convert_fusion
  380.4 2.1 collective-permute-start.3
  382.5 26.2 %collective-permute-done.3 = bf16[1024,512]{0,1:T(8,128)(2,1)S(1)} collective-permute-done((bf16[1024,512]{0,1:T(8,128)(2,1)S(1)}, bf16[1024,512]{0,1:T(8,128)(2,1)S(1)}, u32[]{:S(2)}, u32[]{:S(2)}) %collective-permute-start.3) | collective-permute-done | bytes 1048608 | tf_op jit(solution)/shard_map/ppermute | solution.py:17
  408.7 0.2 neg.16
  408.9 10.1 %fusion.119 = (f32[]{:T(128)}, f32[]{:T(128)}, f32[]{:T(128)}, f32[]{:T(128)}, f32[1024,1024]{1,0:T(8,128)}) fusion(f32[1024]{0:T(1024)S(1)} %fusion.63, f32[1024]{0:T(1024)S(1)} %fusion.61, f32[]{:T(128)} %bitcast.43, bf16[1024,512]{0,1:T(8,128)(2,1)S(1)} %select_convert_fusion, bf16[1024,512]{0,1:T(8,128)(2,1)S(1)} %neg.16), kind=kOutput, calls=%fused_computation.138 | convolution fusion | flops 2203058176 | bytes 6299668 | tf_op jit(solution)/shard_map/dot_general | solution.py:111
  419.0 5.7 %fusion.66 = f32[1,1,4]{2,1,0:T(1,128)} fusion(f32[1,1,4]{2,1,0:T(1,128)S(1)} %copy-done.2, f32[1,1,1]{2,1,0:T(1,128)} %bitcast.22, f32[1,1,1]{2,1,0:T(1,128)} %bitcast.21, f32[1,1,1]{2,1,0:T(1,128)} %bitcast.20, f32[1,1,1]{2,1,0:T(1,128)} %bitcast.19, f32[1,1,1]{2,1,0:T(1,128)} %bitcast.26, f32[1,1,1]{2,1,0:T(1,128)} %bitcast.25, f32[1,1,1]{2,1,0:T(1,128)} %bitcast.24, ...), kind=kLoop, calls=%fused_computation.83 | loop fusion | flops 40 | bytes 64 | tf_op jit(solution)/shard_map/add | solution.py:114
  424.8 132.9 %reduce-scatter.5.cloned.1.call-done = f32[32,1024]{1,0:T(8,128)} async-done(((f32[1024,1024]{1,0:T(8,128)}), f32[32,1024]{1,0:T(8,128)}) %reduce-scatter.5.cloned.1.call-update) | async-done | bytes 131088 | tf_op jit(solution)/shard_map/reduce_scatter | solution.py:68
  557.6 1.6 multiply_add_fusion.1
  (26 shorter events, 0.5 us)
Async XLA Ops:
  7.2 63.4 %all-gather.3.cloned.1.call-start = ((), (), s32[]{:S(2)}) async-start(), calls=%async_computation.2 | async-start | bytes 2162688 | tf_op jit(solution)/shard_map/all_gather | solution.py:89
  8.8 279.0 %reduce-scatter.3.cloned.1.call-start = ((), (), s32[]{:S(2)}) async-start(), calls=%async_computation.3 | async-start | bytes 4325376 | tf_op jit(solution)/shard_map/reduce_scatter | solution.py:68
  70.5 15.1 %copy-start.3 = (s32[1,1,16]{2,1,0:T(1,128)S(1)}, s32[1,1,16]{2,1,0:T(1,128)}, u32[]{:S(2)}) copy-start(s32[1,1,16]{2,1,0:T(1,128)} %param.10) | copy-start | bytes 196
  70.5 15.1 %copy-start.5 = (s32[1,1,16]{2,1,0:T(1,128)S(1)}, s32[1,1,16]{2,1,0:T(1,128)}, u32[]{:S(2)}) copy-start(s32[1,1,16]{2,1,0:T(1,128)} %param.11) | copy-start | bytes 196
  82.5 26.2 %collective-permute-start = (bf16[1024,512]{0,1:T(8,128)(2,1)}, bf16[1024,512]{0,1:T(8,128)(2,1)}, u32[]{:S(2)}, u32[]{:S(2)}) collective-permute-start(bf16[1024,512]{0,1:T(8,128)(2,1)} %slice.53), channel_id=1, source_target_pairs={{4,0},{8,4},{12,8},{16,12},{20,16},{24,20},{28,24},{0,28},{5,1},{9... | collective-permute-start | bytes 3145736 | tf_op jit(solution)/shard_map/ppermute | solution.py:17
  110.6 28.2 %collective-permute-start.1 = (bf16[1024,512]{0,1:T(8,128)(2,1)S(1)}, bf16[1024,512]{0,1:T(8,128)(2,1)S(1)}, u32[]{:S(2)}, u32[]{:S(2)}) collective-permute-start(bf16[1024,512]{0,1:T(8,128)(2,1)S(1)} %select_convert_fusion.1), channel_id=1, source_target_pairs={{28,0},{0,4},{4,8},{8,12},{12,16},{16,20},{20,24},{24,28},{29,1},{... | collective-permute-start | bytes 3145736 | tf_op jit(solution)/shard_map/ppermute | solution.py:17
  149.1 138.7 %copy-start = (f32[32,1024]{1,0:T(8,128)S(1)}, f32[32,1024]{1,0:T(8,128)}, u32[]{:S(2)}) copy-start(f32[32,1024]{1,0:T(8,128)} %param.7) | copy-start | bytes 393220
  149.1 140.5 %copy-start.2 = (f32[1,1,4]{2,1,0:T(1,128)S(1)}, f32[1,1,4]{2,1,0:T(1,128)}, u32[]{:S(2)}) copy-start(f32[1,1,4]{2,1,0:T(1,128)} %param.8) | copy-start | bytes 52
  149.1 194.4 %copy-start.4 = (bf16[1,1,1024,1024]{3,2,1,0:T(8,128)(2,1)S(1)}, bf16[1,1,1024,1024]{3,2,1,0:T(8,128)(2,1)}, u32[]{:S(2)}) copy-start(bf16[1,1,1024,1024]{3,2,1,0:T(8,128)(2,1)} %param.6) | copy-start | bytes 6291460
  149.1 194.4 %all-gather.5.cloned.1.call-start = ((), (), s32[]{:S(2)}) async-start(), calls=%async_computation.4 | async-start | bytes 2162688 | tf_op jit(solution)/shard_map/all_gather | solution.py:89
  289.3 268.3 %reduce-scatter.5.cloned.1.call-start = ((), (), s32[]{:S(2)}) async-start(), calls=%async_computation.5 | async-start | bytes 4325376 | tf_op jit(solution)/shard_map/reduce_scatter | solution.py:68
  353.9 26.0 %collective-permute-start.2 = (bf16[1024,512]{0,1:T(8,128)(2,1)S(1)}, bf16[1024,512]{0,1:T(8,128)(2,1)S(1)}, u32[]{:S(2)}, u32[]{:S(2)}) collective-permute-start(bf16[1024,512]{0,1:T(8,128)(2,1)S(1)} %slice.55), channel_id=1, source_target_pairs={{4,0},{8,4},{12,8},{16,12},{20,16},{24,20},{28,24},{0,28},{5,1},{9... | collective-permute-start | bytes 3145736 | tf_op jit(solution)/shard_map/ppermute | solution.py:17
  380.4 28.3 %collective-permute-start.3 = (bf16[1024,512]{0,1:T(8,128)(2,1)S(1)}, bf16[1024,512]{0,1:T(8,128)(2,1)S(1)}, u32[]{:S(2)}, u32[]{:S(2)}) collective-permute-start(bf16[1024,512]{0,1:T(8,128)(2,1)S(1)} %select_convert_fusion), channel_id=1, source_target_pairs={{28,0},{0,4},{4,8},{8,12},{12,16},{16,20},{20,24},{24,28},{29,1},{... | collective-permute-start | bytes 3145736 | tf_op jit(solution)/shard_map/ppermute | solution.py:17
  419.0 138.6 %copy-start.1 = (f32[32,1024]{1,0:T(8,128)S(1)}, f32[32,1024]{1,0:T(8,128)}, u32[]{:S(2)}) copy-start(f32[32,1024]{1,0:T(8,128)} %reduce-scatter.3.cloned.1.call-done) | copy-start | bytes 393220
Sparse Core Ops, SparseCore 0:
  11.4 59.0 all-gather.2
  149.2 138.4 reduce-scatter.2
  291.2 52.2 all-gather.4
  419.2 138.4 reduce-scatter.4
where the time goes:
time: 566 us
  waiting for transfers between devices  475 us (84%)
  matrix products  41.4 us (7%)
  other arithmetic  17.1 us (3%)
  between operations  16.8 us (3%)
  starting transfers between devices  10.7 us (2%)
    reduce_scatter x2, waiting for transfers between devices, reduce_share(): lax.psum_scatter(pulled, ('azim', 'axial'), scatter_dimension=0, tiled=True)  271 us
    all_gather x2, waiting for transfers between devices, local(): lax.all_gather(ref_rows.astype(jnp.bfloat16), ('azim', 'axial'), axis=0,...  107 us
    ppermute x4, waiting for transfers between devices, from_behind(): return lax.ppermute(block, axis, route)  97.2 us
    dot_general x2, matrix products, local(): jnp.dot(repaired_heights, mixer, preferred_element_type=jnp.float32)  21.2 us
    dot_general x2, matrix products, local(): lax.dot_general(upstream, mixer, (((1,), (1,)), ((), ())), preferred_elem...  20.2 us
  transfers between devices with their start and end apart: 8, of which 8 were waited for; matrix products, arithmetic and copies ran while one was open for 2% of the time, Pallas kernels for 0%

commit v1 on v0

v1 whole, which is shorter than its diff:
```python
import functools
import math

import jax
import jax.numpy as jnp
from jax import lax
from jax.experimental import pallas as pl
from jax.experimental.pallas import tpu as pltpu
from jax.sharding import PartitionSpec as P

PASSES = 2
AXES = ("azim", "axial")
WINDOW = 16.0
LANE = 128
WIDE = 256
REACH = 2
SPAN = 512


def tap_tables(shifts):
    place = jnp.arange(2 * SPAN, dtype=jnp.float32) - SPAN
    lag = jnp.stack([-place, place])[None]
    offset = lag - shifts[:, None, None]
    return jnp.sinc(offset) * jnp.exp(-(offset * offset) / (WINDOW * WINDOW))


def butterfly_sum(value):
    for axis in ("axial", "azim"):
        size = lax.axis_size(axis)
        step = 1
        while step < size:
            value = value + lax.ppermute(value, axis, [(i, i ^ step) for i in range(size)])
            step *= 2
    return value


def build_bands(tap_ref, band_ref, tiles):
    def one(s, carry):
        for way in range(2):
            taps = jnp.broadcast_to(tap_ref[s, way : way + 1, :], (LANE, 2 * SPAN))
            skewed = pltpu.roll(taps, 0, 1, stride=1, stride_axis=0)
            first = SPAN - REACH * LANE
            band_ref[s, way] = skewed[:, first : first + (2 * REACH + 1) * LANE].astype(jnp.bfloat16)
        return carry

    lax.fori_loop(0, tiles, one, 0)


def wide_matrix(band_ref, s, way):
    def block(distance):
        if abs(distance) > REACH:
            return jnp.zeros((LANE, LANE), jnp.bfloat16)
        start = (REACH - distance) * LANE
        return band_ref[s, way, :, start : start + LANE]

    rows = []
    for row in range(-2, 4):
        rows.append(jnp.concatenate([block(row - col) for col in range(2)], axis=1))
    return jnp.concatenate(rows, axis=0)


def spread(stacked, rows):
    if rows % 16:
        stacked = stacked.astype(jnp.float32)
    edge = jnp.zeros((rows, WIDE), stacked.dtype)
    before = jnp.concatenate([edge, stacked[:-rows]], axis=0)
    after = jnp.concatenate([stacked[rows:], edge], axis=0)
    return jnp.concatenate([before, stacked, after], axis=1).astype(jnp.bfloat16)


def stack_blocks(value):
    return jnp.concatenate(
        [value[:, k : k + WIDE] for k in range(0, value.shape[1], WIDE)], axis=0
    )


def pass_kernel(
    tiles, neighbour, scale, height_ref, ref_ref, tap_ref, col_ref, row_ref, coef_ref, low_ref, high_ref,
    map_ref, grad_ref, band_ref, resampled_ref, total_ref, ref_low_ref
):
    rows, cols = ref_ref.shape
    build_bands(tap_ref, band_ref, tiles)
    ref_low_ref[...] = ref_ref[...].astype(jnp.bfloat16).astype(jnp.float32)

    def forward(s, carry):
        az = col_ref[0:1, :]
        ax = row_ref[:, 0:1]
        shape = (
            coef_ref[4 * s]
            + coef_ref[4 * s + 1] * az
            + coef_ref[4 * s + 2] * ax
            + coef_ref[4 * s + 3] * (az * az + ax * ax - 2.0 / 3.0)
        )
        corrected = height_ref[s].astype(jnp.float32) - ref_low_ref[...] - shape
        stacked = stack_blocks(corrected).astype(jnp.bfloat16)
        out = jnp.dot(
            spread(stacked, rows), wide_matrix(band_ref, s, 0), preferred_element_type=jnp.float32
        )
        resampled_ref[s] = out.astype(jnp.bfloat16)
        return carry

    lax.fori_loop(0, tiles, forward, 0)
    total_ref[...] = jnp.zeros_like(total_ref)
    column = lax.broadcasted_iota(jnp.int32, (2 * rows, WIDE), 1) + jnp.where(
        lax.broadcasted_iota(jnp.int32, (2 * rows, WIDE), 0) >= rows, WIDE, 0
    )

    def seam(left, right):
        difference = resampled_ref[left, 2 * rows :, :].astype(jnp.float32) - resampled_ref[
            right, : 2 * rows, :
        ].astype(jnp.float32)
        inside = (column >= low_ref[left]) & (column < high_ref[left])
        return jnp.where(inside, difference, 0.0)

    def backward(s, carry):
        before = jnp.where(s >= neighbour, s - neighbour, s - neighbour + tiles)
        after = jnp.where(s + neighbour < tiles, s + neighbour, s + neighbour - tiles)
        upstream = jnp.concatenate([-seam(before, s), seam(s, after)], axis=0).astype(jnp.bfloat16)
        pulled = jnp.dot(
            spread(upstream, rows), wide_matrix(band_ref, s, 1), preferred_element_type=jnp.float32
        )
        total_ref[...] += pulled
        ax = row_ref[:, :]
        plain, tilted, bent = [], [], []
        for k in range(cols // WIDE):
            block = pulled[k * rows : (k + 1) * rows].reshape(rows // 8, 8, WIDE)
            weight = jnp.concatenate([ax, ax], axis=1).reshape(rows // 8, 8, WIDE)
            first = block * weight
            plain.append(jnp.sum(block, axis=0))
            tilted.append(jnp.sum(first, axis=0))
            bent.append(jnp.sum(first * weight, axis=0))
        plain = jnp.concatenate(plain, axis=1)
        tilted = jnp.concatenate(tilted, axis=1)
        bent = jnp.concatenate(bent, axis=1)
        az = col_ref[0:1, :]
        leaning = plain * az
        sums = [plain, leaning, tilted, leaning * az + bent - plain * (2.0 / 3.0)]
        folded = [
            sum(value[:, k : k + LANE] for k in range(0, cols, LANE)) for value in sums
        ]
        grad_ref[s] = jnp.concatenate([jnp.sum(v, axis=0, keepdims=True) for v in folded], axis=0)
        return carry

    lax.fori_loop(0, tiles, backward, 0)
    for k in range(cols // WIDE):
        part = slice(k * WIDE, (k + 1) * WIDE)
        map_ref[:, part] = ref_ref[:, part] + total_ref[k * rows : (k + 1) * rows, :] / scale


def one_pass(heights, ref_rows, taps, col_terms, row_terms, coefs, low, high, neighbour):
    tiles, rows, cols = heights.shape
    vmem = pl.BlockSpec(memory_space=pltpu.VMEM)
    smem = pl.BlockSpec(memory_space=pltpu.SMEM)
    body = functools.partial(pass_kernel, tiles, neighbour, math.sqrt(tiles))
    return pl.pallas_call(
        body,
        out_shape=(
            jax.ShapeDtypeStruct((rows, cols), jnp.float32),
            jax.ShapeDtypeStruct((tiles, 4, LANE), jnp.float32),
        ),
        in_specs=[vmem] * 5 + [smem] * 3,
        out_specs=(vmem, vmem),
        scratch_shapes=[
            pltpu.VMEM((tiles, 2, LANE, (2 * REACH + 1) * LANE), jnp.bfloat16),
            pltpu.VMEM((tiles, 4 * rows, WIDE), jnp.bfloat16),
            pltpu.VMEM((4 * rows, WIDE), jnp.float32),
            pltpu.VMEM((rows, cols), jnp.float32),
        ],
        compiler_params=pltpu.CompilerParams(vmem_limit_bytes=56 * 1024 * 1024),
    )(heights, ref_rows, taps, col_terms, row_terms, coefs.reshape(-1), low, high)


def local(observed_heights, ref_map, coefs, shifts, pair_offset, pair_width):
    rows, cols = ref_map.shape
    axial_size = lax.axis_size("axial")
    tiles = lax.axis_size("azim") * axial_size
    me = lax.axis_index(AXES)
    row_total = observed_heights.shape[2]
    pair_count = pair_offset.shape[2]
    pair = me * rows // (row_total // pair_count)

    words = jnp.concatenate(
        [
            coefs[0, 0],
            shifts[0],
            pair_offset[0, 0].astype(jnp.float32),
            pair_width[0, 0].astype(jnp.float32),
        ]
    )
    words = jnp.pad(words, (0, LANE - words.shape[0]))[None]
    table = lax.all_gather(words, AXES, axis=0, tiled=True)
    heights = lax.all_to_all(
        observed_heights[0, 0].reshape(tiles, rows, cols), AXES, 0, 0, tiled=True
    )
    coef_now = table[:, :4]
    taps = tap_tables(table[:, 4])
    low = lax.dynamic_index_in_dim(table, 5 + pair, 1, keepdims=False).astype(jnp.int32)
    width = lax.dynamic_index_in_dim(table, 5 + pair_count + pair, 1, keepdims=False)
    high = low + width.astype(jnp.int32)

    row_place = (me * rows).astype(jnp.float32) + jnp.arange(rows, dtype=jnp.float32)
    row_terms = (row_place - 0.5 * (row_total - 1)) * (2.0 / row_total)
    row_terms = jnp.broadcast_to(row_terms[:, None], (rows, LANE))
    col_terms = (jnp.arange(cols, dtype=jnp.float32) - 0.5 * (cols - 1)) * (2.0 / cols)
    col_terms = jnp.broadcast_to(col_terms[None], (8, cols))

    ref_rows = ref_map
    for _ in range(PASSES):
        ref_rows, partial = one_pass(
            heights, ref_rows, taps, col_terms, row_terms, coef_now, low, high, axial_size
        )
        grads = butterfly_sum(jnp.sum(partial, axis=2))
        coef_now = coef_now + grads / (row_total * cols)
    mine = lax.dynamic_slice_in_dim(coef_now, me, 1, axis=0)
    return (ref_rows, mine[None])


def solution(mesh):
    in_specs = (
        P("axial", "azim", None, None),
        P(("azim", "axial"), None),
        P("axial", "azim", None),
        P("axial", "azim"),
        P("axial", "azim", None),
        P("axial", "azim", None),
    )
    out_specs = (P(("azim", "axial"), None), P("axial", "azim", None))
    return jax.shard_map(local, mesh=mesh, in_specs=in_specs, out_specs=out_specs, check_vma=False)
```

time: 566 us -> 173 us (0.31)
  waiting for transfers between devices: 475 us -> 21.5 us
  blocking collectives: 0 us -> 68.7 us
  Pallas kernels: 0 us -> 48.8 us
  matrix products: 41.4 us -> 0 us
  between operations: 16.8 us -> 1.43 us
  starting transfers between devices: 10.7 us -> 23.2 us
  other arithmetic: 17.1 us -> 6.59 us
    reduce_scatter x2 -> x0, waiting for transfers between devices: 271 us -> none  [reduce_share(): lax.psum_scatter(pulled, ('azim', 'axial'), scatter_dimension=0, tiled=True)]
    all_gather x2 -> x0, waiting for transfers between devices: 107 us -> none  [local(): lax.all_gather(ref_rows.astype(jnp.bfloat16), ('azim', 'axial'), axis=0,...]
    ppermute x4 -> x10, waiting for transfers between devices: 97.2 us -> 21.5 us  [butterfly_sum(): lax.ppermute(value, axis, [(i, i ^ step) for i in range(size)])]
    all_gather x0 -> x1, blocking collectives: none -> 68.7 us  [local(): table = lax.all_gather(words, AXES, axis=0, tiled=True)]
    pallas_call x0 -> x2, Pallas kernels: none -> 48.8 us  [one_pass(): pl.pallas_call(body, out_shape=(jax.ShapeDtypeStruct((rows, cols), jnp.fl...]
    dot_general x4 -> x0, matrix products: 41.4 us -> none  [the longest x2 21.2 us: local(): jnp.dot(repaired_heights, mixer, preferred_element_type=jnp.float32)]
    add x6 -> x10, other arithmetic: 11.2 us -> 0.62 us  [the longest x1 0.58 us: local(): high = low + width.astype(jnp.int32)]
    all_to_all x0 -> x1, starting transfers between devices: none -> 7.3 us  [local(): lax.all_to_all(observed_heights[0, 0].reshape(tiles, rows, cols), AXES, 0...]
  transfers between devices with their start and end apart: 8 -> 11, of which waited for: 8 -> 10; matrix products, arithmetic and copies ran while one was open for 2% -> 3% of each run, Pallas kernels for 0% -> 0%
where the time goes in v1:
time: 173 us
  blocking collectives  68.7 us (40%)
  Pallas kernels  48.8 us (28%)
  starting transfers between devices  23.2 us (13%)
  waiting for transfers between devices  21.5 us (12%)
  other arithmetic  6.59 us (4%)
  local copies, waits for them, and re-layouts  2.78 us (2%)
    all_gather x1, blocking collectives, local(): table = lax.all_gather(words, AXES, axis=0, tiled=True)  68.7 us
    pallas_call x2, Pallas kernels, one_pass(): pl.pallas_call(body, out_shape=(jax.ShapeDtypeStruct((rows, cols), jnp.fl...  48.8 us
    ppermute x10, waiting for transfers between devices, butterfly_sum(): lax.ppermute(value, axis, [(i, i ^ step) for i in range(size)])  21.5 us
    ppermute x10, starting transfers between devices, butterfly_sum(): lax.ppermute(value, axis, [(i, i ^ step) for i in range(size)])  15.9 us
    all_to_all x1, starting transfers between devices, local(): lax.all_to_all(observed_heights[0, 0].reshape(tiles, rows, cols), AXES, 0...  7.3 us
  transfers between devices with their start and end apart: 11, of which 10 were waited for; matrix products, arithmetic and copies ran while one was open for 3% of the time, Pallas kernels for 0%

profile of v1, /device:TPU:0, one launch (start us, length us, event | category | flops | bytes accessed | tf_op | source)
XLA Modules:
  0.0 173.0 jit_solution(6955820600082953557)
XLA Ops:
  0.7 7.3 %all-to-all-start = ((bf16[32,32,1024]{2,1,0:T(8,128)(2,1)}), bf16[32,32,1024]{2,1,0:T(8,128)(2,1)S(1)}, u32[]{:S(2)}, u32[]{:S(2)}) async-start(bf16[32,32,1024]{2,1,0:T(8,128)(2,1)} %bitcast.14), calls=%async_computation | async-start | bytes 4194304 | tf_op jit(solution)/shard_map/all_to_all | solution.py:192
  8.8 68.7 %all-gather.1 = f32[32,1,128]{2,1,0:T(1,128)S(1)} all-gather(f32[1,1,128]{2,1,0:T(1,128)S(1)} %fusion.15), channel_id=2, replica_groups=mesh['azim'=8,'axial'=4] {'azim','axial'}, dimensions={0}, use_global_device_ids=true | all-gather | bytes 16896 | tf_op jit(solution)/shard_map/all_gather | solution.py:191
  77.5 0.6 reshape.38.coef_ref
  78.1 1.3 convert_reduce_fusion
  79.4 0.6 add.161.high_ref
  80.2 2.1 %fusion.9.tap_ref = f32[32,2,1024]{2,1,0:T(2,128)} fusion(f32[2,1024]{1,0:T(2,128)S(1)} %pad_maximum_fusion, f32[32]{0:T(128)S(1)} %slice_reduce_fusion), kind=kLoop, calls=%fused_computation.19 | loop fusion | flops 2490368 | bytes 270464 | tf_op jit(solution)/shard_map/mul | solution.py:24
  82.4 0.7 broadcast_in_dim.28.row_ref
  83.1 0.6 broadcast_in_dim.27.col_ref
  83.7 24.4 %shard_map.77 = (f32[32,1024]{1,0:T(8,128)}, f32[32,4,128]{2,1,0:T(4,128)}) custom-call(bf16[32,32,1024]{2,1,0:T(8,128)(2,1)} %copy-done, f32[32,1024]{1,0:T(8,128)} %ref_ref.1, f32[32,2,1024]{2,1,0:T(2,128)} %fusion.9.tap_ref, f32[8,1024]{1,0:T(8,128)} %broadcast_in_dim.27.col_ref, f32[32,128]{1,0:T(8,128)} %broadcast_in_dim.28.row_ref, ...), custom_call_target="tpu_custom_call" | custom-call | tf_op jit(solution)/shard_map/pallas_call | solution.py:155
  108.1 0.9 reduce_sum.18
  109.1 0.4 collective-permute-start
  109.4 0.9 collective-permute-done
  110.3 1.4 collective-permute-start.1
  111.7 2.3 %collective-permute-done.1 = f32[32,4]{1,0:T(8,128)S(1)} collective-permute-done((f32[32,4]{1,0:T(8,128)S(1)}, f32[32,4]{1,0:T(8,128)S(1)}, u32[]{:S(2)}, u32[]{:S(2)}) %collective-permute-start.1) | collective-permute-done | bytes 544 | tf_op jit(solution)/shard_map/ppermute | solution.py:32
  114.1 1.6 collective-permute-start.2
  115.7 2.1 %collective-permute-done.2 = f32[32,4]{1,0:T(8,128)S(1)} collective-permute-done((f32[32,4]{1,0:T(8,128)S(1)}, f32[32,4]{1,0:T(8,128)S(1)}, u32[]{:S(2)}, u32[]{:S(2)}) %collective-permute-start.2) | collective-permute-done | bytes 544 | tf_op jit(solution)/shard_map/ppermute | solution.py:32
  117.8 3.4 %collective-permute-start.3 = (f32[32,4]{1,0:T(8,128)S(1)}, f32[32,4]{1,0:T(8,128)S(1)}, u32[]{:S(2)}, u32[]{:S(2)}) collective-permute-start(f32[32,4]{1,0:T(8,128)S(1)} %add.164), channel_id=1, source_target_pairs={{0,8},{4,12},{8,0},{12,4},{16,24},{20,28},{24,16},{28,20},{1,9},{5... | collective-permute-start | bytes 1544 | tf_op jit(solution)/shard_map/ppermute | solution.py:32
  121.2 1.7 collective-permute-done.3
  123.0 4.7 %collective-permute-start.4 = (f32[32,4]{1,0:T(8,128)S(1)}, f32[32,4]{1,0:T(8,128)S(1)}, u32[]{:S(2)}, u32[]{:S(2)}) collective-permute-start(f32[32,4]{1,0:T(8,128)S(1)} %add.165), channel_id=1, source_target_pairs={{0,16},{4,20},{8,24},{12,28},{16,0},{20,4},{24,8},{28,12},{1,17},{... | collective-permute-start | bytes 1544 | tf_op jit(solution)/shard_map/ppermute | solution.py:32
  127.7 1.7 collective-permute-done.4
  129.4 0.6 reshape.39.coef_ref
  130.0 24.4 %shard_map.78 = (f32[32,1024]{1,0:T(8,128)}, f32[32,4,128]{2,1,0:T(4,128)}) custom-call(bf16[32,32,1024]{2,1,0:T(8,128)(2,1)} %copy-done, f32[32,1024]{1,0:T(8,128)} %get-tuple-element.6.ref_ref, f32[32,2,1024]{2,1,0:T(2,128)} %fusion.9.tap_ref, f32[8,1024]{1,0:T(8,128)} %broadcast_in_dim.27.col_ref, f32[32,128]{1,0:T(8,128)} %broadcast_in_dim.28.row_ref, ...), custom_call_target="tpu_custom_call" | custom-call | tf_op jit(solution)/shard_map/pallas_call | solution.py:155
  154.4 0.9 reduce_sum.19
  155.5 1.2 collective-permute-done.5
  156.6 1.1 collective-permute-start.6
  157.8 2.6 %collective-permute-done.6 = f32[32,4]{1,0:T(8,128)S(1)} collective-permute-done((f32[32,4]{1,0:T(8,128)S(1)}, f32[32,4]{1,0:T(8,128)S(1)}, u32[]{:S(2)}, u32[]{:S(2)}) %collective-permute-start.6) | collective-permute-done | bytes 544 | tf_op jit(solution)/shard_map/ppermute | solution.py:32
  160.4 3.7 %collective-permute-done.7 = f32[32,4]{1,0:T(8,128)S(1)} collective-permute-done((f32[32,4]{1,0:T(8,128)S(1)}, f32[32,4]{1,0:T(8,128)S(1)}, u32[]{:S(2)}, u32[]{:S(2)}) %collective-permute-start.7) | collective-permute-done | bytes 544 | tf_op jit(solution)/shard_map/ppermute | solution.py:32
  164.1 0.2 collective-permute-start.8
  164.4 3.5 %collective-permute-done.8 = f32[32,4]{1,0:T(8,128)S(1)} collective-permute-done((f32[32,4]{1,0:T(8,128)S(1)}, f32[32,4]{1,0:T(8,128)S(1)}, u32[]{:S(2)}, u32[]{:S(2)}) %collective-permute-start.8) | collective-permute-done | bytes 544 | tf_op jit(solution)/shard_map/ppermute | solution.py:32
  167.9 2.9 %collective-permute-start.9 = (f32[32,4]{1,0:T(8,128)S(1)}, f32[32,4]{1,0:T(8,128)S(1)}, u32[]{:S(2)}, u32[]{:S(2)}) collective-permute-start(f32[32,4]{1,0:T(8,128)S(1)} %add.171), channel_id=1, source_target_pairs={{0,16},{4,20},{8,24},{12,28},{16,0},{20,4},{24,8},{28,12},{1,17},{... | collective-permute-start | bytes 1544 | tf_op jit(solution)/shard_map/ppermute | solution.py:32
  170.8 1.7 collective-permute-done.9
  172.5 0.5 fusion.16
  (29 shorter events, 0.4 us)
Async XLA Ops:
  0.6 8.0 %copy-start.3 = (s32[1,1,16]{2,1,0:T(1,128)S(1)}, s32[1,1,16]{2,1,0:T(1,128)}, u32[]{:S(2)}) copy-start(s32[1,1,16]{2,1,0:T(1,128)} %param.11) | copy-start | bytes 196
  0.6 8.0 %copy-start.4 = (s32[1,1,16]{2,1,0:T(1,128)S(1)}, s32[1,1,16]{2,1,0:T(1,128)}, u32[]{:S(2)}) copy-start(s32[1,1,16]{2,1,0:T(1,128)} %param.10) | copy-start | bytes 196
  0.7 8.0 %copy-start.2 = (f32[1,1,4]{2,1,0:T(1,128)S(1)}, f32[1,1,4]{2,1,0:T(1,128)}, u32[]{:S(2)}) copy-start(f32[1,1,4]{2,1,0:T(1,128)} %param.8) | copy-start | bytes 52
  0.7 81.7 %all-to-all-start = ((bf16[32,32,1024]{2,1,0:T(8,128)(2,1)}), bf16[32,32,1024]{2,1,0:T(8,128)(2,1)S(1)}, u32[]{:S(2)}, u32[]{:S(2)}) async-start(bf16[32,32,1024]{2,1,0:T(8,128)(2,1)} %bitcast.14), calls=%async_computation | async-start | bytes 4194304 | tf_op jit(solution)/shard_map/all_to_all | solution.py:192
  79.4 4.3 %copy-start.1 = (s32[32]{0:T(128)}, s32[32]{0:T(128)S(1)}, u32[]{:S(2)}) copy-start(s32[32]{0:T(128)S(1)} %get-tuple-element.11.low_ref) | copy-start | bytes 388
  82.4 1.4 copy-start
  109.1 1.2 collective-permute-start
  110.3 3.7 %collective-permute-start.1 = (f32[32,4]{1,0:T(8,128)S(1)}, f32[32,4]{1,0:T(8,128)S(1)}, u32[]{:S(2)}, u32[]{:S(2)}) collective-permute-start(f32[32,4]{1,0:T(8,128)S(1)} %add.162), channel_id=1, source_target_pairs={{0,2},{1,3},{2,0},{3,1},{4,6},{5,7},{6,4},{7,5},{8,10},{9,11},{10,... | collective-permute-start | bytes 1544 | tf_op jit(solution)/shard_map/ppermute | solution.py:32
  114.1 3.7 %collective-permute-start.2 = (f32[32,4]{1,0:T(8,128)S(1)}, f32[32,4]{1,0:T(8,128)S(1)}, u32[]{:S(2)}, u32[]{:S(2)}) collective-permute-start(f32[32,4]{1,0:T(8,128)S(1)} %add.163), channel_id=1, source_target_pairs={{0,4},{4,0},{8,12},{12,8},{16,20},{20,16},{24,28},{28,24},{1,5},{5... | collective-permute-start | bytes 1544 | tf_op jit(solution)/shard_map/ppermute | solution.py:32
  117.8 5.1 %collective-permute-start.3 = (f32[32,4]{1,0:T(8,128)S(1)}, f32[32,4]{1,0:T(8,128)S(1)}, u32[]{:S(2)}, u32[]{:S(2)}) collective-permute-start(f32[32,4]{1,0:T(8,128)S(1)} %add.164), channel_id=1, source_target_pairs={{0,8},{4,12},{8,0},{12,4},{16,24},{20,28},{24,16},{28,20},{1,9},{5... | collective-permute-start | bytes 1544 | tf_op jit(solution)/shard_map/ppermute | solution.py:32
  123.0 6.4 %collective-permute-start.4 = (f32[32,4]{1,0:T(8,128)S(1)}, f32[32,4]{1,0:T(8,128)S(1)}, u32[]{:S(2)}, u32[]{:S(2)}) collective-permute-start(f32[32,4]{1,0:T(8,128)S(1)} %add.165), channel_id=1, source_target_pairs={{0,16},{4,20},{8,24},{12,28},{16,0},{20,4},{24,8},{28,12},{1,17},{... | collective-permute-start | bytes 1544 | tf_op jit(solution)/shard_map/ppermute | solution.py:32
  155.4 1.2 collective-permute-start.5
  156.6 3.7 %collective-permute-start.6 = (f32[32,4]{1,0:T(8,128)S(1)}, f32[32,4]{1,0:T(8,128)S(1)}, u32[]{:S(2)}, u32[]{:S(2)}) collective-permute-start(f32[32,4]{1,0:T(8,128)S(1)} %add.168), channel_id=1, source_target_pairs={{0,2},{1,3},{2,0},{3,1},{4,6},{5,7},{6,4},{7,5},{8,10},{9,11},{10,... | collective-permute-start | bytes 1544 | tf_op jit(solution)/shard_map/ppermute | solution.py:32
  160.4 3.7 %collective-permute-start.7 = (f32[32,4]{1,0:T(8,128)S(1)}, f32[32,4]{1,0:T(8,128)S(1)}, u32[]{:S(2)}, u32[]{:S(2)}) collective-permute-start(f32[32,4]{1,0:T(8,128)S(1)} %add.169), channel_id=1, source_target_pairs={{0,4},{4,0},{8,12},{12,8},{16,20},{20,16},{24,28},{28,24},{1,5},{5... | collective-permute-start | bytes 1544 | tf_op jit(solution)/shard_map/ppermute | solution.py:32
  164.1 3.7 %collective-permute-start.8 = (f32[32,4]{1,0:T(8,128)S(1)}, f32[32,4]{1,0:T(8,128)S(1)}, u32[]{:S(2)}, u32[]{:S(2)}) collective-permute-start(f32[32,4]{1,0:T(8,128)S(1)} %add.170), channel_id=1, source_target_pairs={{0,8},{4,12},{8,0},{12,4},{16,24},{20,28},{24,16},{28,20},{1,9},{5... | collective-permute-start | bytes 1544 | tf_op jit(solution)/shard_map/ppermute | solution.py:32
  167.9 4.6 %collective-permute-start.9 = (f32[32,4]{1,0:T(8,128)S(1)}, f32[32,4]{1,0:T(8,128)S(1)}, u32[]{:S(2)}, u32[]{:S(2)}) collective-permute-start(f32[32,4]{1,0:T(8,128)S(1)} %add.171), channel_id=1, source_target_pairs={{0,16},{4,20},{8,24},{12,28},{16,0},{20,4},{24,8},{28,12},{1,17},{... | collective-permute-start | bytes 1544 | tf_op jit(solution)/shard_map/ppermute | solution.py:32

commit v2 on v1

v2 whole, which is shorter than its diff:
```python
import functools
import math

import jax
import jax.numpy as jnp
from jax import lax
from jax.experimental import pallas as pl
from jax.experimental.pallas import tpu as pltpu
from jax.sharding import PartitionSpec as P

AXES = ("azim", "axial")
WINDOW = 16.0
LANE = 128
WIDE = 256
REACH = 2
BAND = (2 * REACH + 1) * LANE
SPAN = 512
GROUP = 4
HALF_LANE = 64
VMEM_MAIN = 56 * 1024 * 1024
EXACT = lax.Precision.HIGHEST


def exchange(value, axis, steps):
    size = lax.axis_size(axis)
    return sum(lax.ppermute(value, axis, [(i, i ^ k) for i in range(size)]) for k in steps)


def gather_rows(value):
    azim, axial = lax.axis_size("azim"), lax.axis_size("axial")
    value = value + exchange(value, "azim", range(2, azim, 2))
    value = value + exchange(value, "azim", [1])
    step = axial // 2
    while step:
        value = value + exchange(value, "axial", [step])
        step //= 2
    return value


def tap_values(offset):
    centre = offset == 0.0
    angle = jnp.where(centre, 1.0, math.pi * offset)
    sinc = jnp.where(centre, 1.0, jnp.sin(angle) / angle)
    return sinc * jnp.exp(-(offset * offset) / (WINDOW * WINDOW))


def wide_matrix(band_ref, s, way):
    def block(distance):
        if abs(distance) > REACH:
            return jnp.zeros((LANE, LANE), jnp.bfloat16)
        start = (REACH - distance) * LANE
        return band_ref[s, way, :, start : start + LANE]

    rows = []
    for row in range(-2, 4):
        rows.append(jnp.concatenate([block(row - col) for col in range(2)], axis=1))
    return jnp.concatenate(rows, axis=0)


def spread(stacked, rows):
    if rows % 16:
        stacked = stacked.astype(jnp.float32)
    edge = jnp.zeros((rows, WIDE), stacked.dtype)
    before = jnp.concatenate([edge, stacked[:-rows]], axis=0)
    after = jnp.concatenate([stacked[rows:], edge], axis=0)
    return jnp.concatenate([before, stacked, after], axis=1).astype(jnp.bfloat16)


def stack_blocks(value):
    return jnp.concatenate(
        [value[:, k : k + WIDE] for k in range(0, value.shape[1], WIDE)], axis=0
    )


def mixed(stacked, rows, band_ref, s, way):
    return jnp.dot(
        spread(stacked, rows), wide_matrix(band_ref, s, way), preferred_element_type=jnp.float32
    )


def neighbours(s, tiles, stride):
    before = jnp.where(s >= stride, s - stride, s - stride + tiles)
    after = jnp.where(s + stride < tiles, s + stride, s + stride - tiles)
    return before, after


def two_parts(value):
    high = value.astype(jnp.bfloat16).astype(jnp.float32)
    return high, value - high


def prepare_kernel(
    tiles, stride, pair_count, pair_ref, words_ref, table_ref, col_ref,
    band_ref, effect_ref, moment_ref, tap_ref, seen_ref, base_ref
):
    cols = col_ref.shape[1]
    blocks = cols // WIDE
    pair = pair_ref[0]
    place = lax.broadcasted_iota(jnp.int32, (tiles, 2 * SPAN), 1).astype(jnp.float32) - SPAN
    shift = table_ref[:, 4:5]
    tap_ref[0] = tap_values(-place - shift)
    tap_ref[1] = tap_values(place - shift)
    az = col_ref[0:1, :]
    row = lax.broadcasted_iota(jnp.int32, (8, cols), 0)
    base = jnp.where(row == 0, 1.0, jnp.where(row == 1, az, jnp.where(row == 2, az * az, 0.0)))
    high, low = two_parts(base)
    base = jnp.concatenate([high, low], axis=0)
    base_ref[...] = spread(stack_blocks(base).astype(jnp.bfloat16), 16)
    effect_ref[...] = jnp.zeros_like(effect_ref)

    def build(s, carry):
        for way in range(2):
            taps = jnp.broadcast_to(tap_ref[way, pl.ds(s, 1), :], (LANE, 2 * SPAN))
            skewed = pltpu.roll(taps, 0, 1, stride=1, stride_axis=0)
            first = SPAN - REACH * LANE
            band_ref[s, way] = skewed[:, first : first + BAND].astype(jnp.bfloat16)
        out = jnp.dot(
            base_ref[...], wide_matrix(band_ref, s, 0), preferred_element_type=jnp.float32
        )
        seen_ref[s] = jnp.sum(out.reshape(blocks, 2, 8, WIDE), axis=1)
        return carry

    lax.fori_loop(0, tiles, build, 0)
    column = lax.broadcasted_iota(jnp.int32, (2, 8, WIDE), 2) + WIDE * lax.broadcasted_iota(
        jnp.int32, (2, 8, WIDE), 0
    )
    column = column.astype(jnp.float32)
    lanes = lax.broadcasted_iota(jnp.int32, (8, LANE), 1)
    az_blocks = [az[:, k : k + LANE] for k in range(0, cols, LANE)]

    def inside(s):
        start = words_ref[s, 5 + pair]
        return (column >= start) & (column < start + words_ref[s, 5 + pair_count + pair])

    def respond(s, carry):
        before, after = neighbours(s, tiles, stride)
        mask_before, mask_own = inside(before), inside(s)
        half = blocks // 2
        own = seen_ref[s]
        zero = jnp.zeros((half, 8, WIDE), jnp.float32)
        parts = [
            jnp.concatenate(
                [jnp.where(mask_before, own[:half], 0.0), jnp.where(mask_own, own[half:], 0.0)], axis=0
            ),
            jnp.concatenate([jnp.where(mask_before, -seen_ref[before][half:], 0.0), zero], axis=0),
            jnp.concatenate([zero, jnp.where(mask_own, -seen_ref[after][:half], 0.0)], axis=0),
        ]
        rows = []
        for block in range(blocks):
            for part in parts:
                rows.extend(two_parts(part[block]))
        out = mixed(jnp.concatenate(rows, axis=0).astype(jnp.bfloat16), 48, band_ref, s, 1)
        out = jnp.sum(out.reshape(blocks, 3, 2, 8, WIDE), axis=2)
        for source, target in enumerate((s, before, after)):
            effect_ref[target] += out[:, source]
            flat = [out[k // 2, source][:, (k % 2) * LANE : (k % 2 + 1) * LANE] for k in range(2 * blocks)]
            first = [f * a for f, a in zip(flat, az_blocks)]
            second = [f * a for f, a in zip(first, az_blocks)]
            sums = [jnp.sum(sum(v), axis=1, keepdims=True) for v in (flat, first, second)]
            moment_ref[s, source] = jnp.where(
                lanes == 0, sums[0], jnp.where(lanes == 1, sums[1], jnp.where(lanes == 2, sums[2], 0.0))
            )
        return carry

    lax.fori_loop(0, tiles, respond, 0)


def prepare(pair, table, col_terms, stride, pair_count):
    tiles = table.shape[0]
    cols = col_terms.shape[1]
    blocks = cols // WIDE
    vmem = pl.BlockSpec(memory_space=pltpu.VMEM)
    smem = pl.BlockSpec(memory_space=pltpu.SMEM)
    return pl.pallas_call(
        functools.partial(prepare_kernel, tiles, stride, pair_count),
        out_shape=(
            jax.ShapeDtypeStruct((tiles, 2, LANE, BAND), jnp.bfloat16),
            jax.ShapeDtypeStruct((tiles, blocks, 8, WIDE), jnp.float32),
            jax.ShapeDtypeStruct((tiles, 3, 8, LANE), jnp.float32),
        ),
        in_specs=[smem, smem, vmem, vmem],
        out_specs=(vmem, vmem, vmem),
        scratch_shapes=[
            pltpu.VMEM((2, tiles, 2 * SPAN), jnp.float32),
            pltpu.VMEM((tiles, blocks, 8, WIDE), jnp.float32),
            pltpu.VMEM((16 * blocks, 3 * WIDE), jnp.bfloat16),
        ],
        compiler_params=pltpu.CompilerParams(vmem_limit_bytes=VMEM_MAIN),
    )(pair, table, table, col_terms)


def passes_kernel(
    tiles, stride, pair_count, scale, pair_ref, words_ref, height_hbm, band_hbm, ref_ref, col_ref, row_ref, extra_ref,
    map_ref, message_ref, height_ref, band_ref, resampled_ref, total_ref, ref_low_ref, sums_ref, sems
):
    rows, cols = ref_ref.shape
    blocks = cols // WIDE
    groups = tiles // GROUP
    pair = pair_ref[0]

    def copies(g):
        part = pl.ds(g * GROUP, GROUP)
        return (
            pltpu.make_async_copy(height_hbm.at[part], height_ref.at[part], sems.at[0, g]),
            pltpu.make_async_copy(band_hbm.at[part], band_ref.at[part], sems.at[1, g]),
        )

    for g in range(groups):
        for copy in copies(g):
            copy.start()

    az = col_ref[0:1, :]
    column = lax.broadcasted_iota(jnp.int32, (2 * rows, WIDE), 1) + jnp.where(
        lax.broadcasted_iota(jnp.int32, (2 * rows, WIDE), 0) >= rows, WIDE, 0
    )
    column = column.astype(jnp.float32)

    def forward(s):
        ax = row_ref[:, 0:1]
        shape = (
            words_ref[s, 0]
            + words_ref[s, 1] * az
            + words_ref[s, 2] * ax
            + words_ref[s, 3] * (az * az + ax * ax - 2.0 / 3.0)
        )
        corrected = height_ref[s].astype(jnp.float32) - ref_low_ref[...] - shape
        out = mixed(stack_blocks(corrected).astype(jnp.bfloat16), rows, band_ref, s, 0)
        resampled_ref[s] = out.astype(jnp.bfloat16)

    def seam(left, right):
        difference = resampled_ref[left, 2 * rows :, :].astype(jnp.float32) - resampled_ref[
            right, : 2 * rows, :
        ].astype(jnp.float32)
        start = words_ref[left, 5 + pair]
        inside = (column >= start) & (column < start + words_ref[left, 5 + pair_count + pair])
        return jnp.where(inside, difference, 0.0)

    def backward(s):
        before, after = neighbours(s, tiles, stride)
        upstream = jnp.concatenate([-seam(before, s), seam(s, after)], axis=0).astype(jnp.bfloat16)
        pulled = mixed(upstream, rows, band_ref, s, 1)
        total_ref[...] += pulled
        plain, tilted, bent = [], [], []
        weight = row_ref[...]
        weight = jnp.concatenate([weight, weight], axis=1).reshape(rows // 8, 8, WIDE)
        for k in range(blocks):
            block = pulled[k * rows : (k + 1) * rows].reshape(rows // 8, 8, WIDE)
            first = block * weight
            plain.append(jnp.sum(block, axis=0))
            tilted.append(jnp.sum(first, axis=0))
            bent.append(jnp.sum(first * weight, axis=0))
        plain = jnp.concatenate(plain, axis=1)
        tilted = jnp.concatenate(tilted, axis=1)
        bent = jnp.concatenate(bent, axis=1)
        leaning = plain * az
        sums = [plain, leaning, tilted, leaning * az + bent - plain * (2.0 / 3.0)]
        folded = [sum(v[:, k : k + LANE] for k in range(0, cols, LANE)) for v in sums]
        return [jnp.sum(v, axis=0, keepdims=True) for v in folded]

    def add_map(source_ref):
        for k in range(blocks):
            part = slice(k * WIDE, (k + 1) * WIDE)
            map_ref[:, part] = source_ref[:, part] + total_ref[k * rows : (k + 1) * rows, :] / scale

    def first_forward(g, carry):
        for copy in copies(g):
            copy.wait()
        for k in range(GROUP):
            forward(g * GROUP + k)
        return carry

    def first_backward(g, carry):
        for k in range(GROUP):
            s = g * GROUP + k
            for term, value in enumerate(backward(s)):
                sums_ref[term, pl.ds(s, 1), :] = value
        return carry

    ref_low_ref[...] = ref_ref[...].astype(jnp.bfloat16).astype(jnp.float32)
    lax.fori_loop(0, groups, first_forward, 0)
    total_ref[...] = jnp.zeros_like(total_ref)
    lax.fori_loop(0, groups, first_backward, 0)
    add_map(ref_ref)

    ones = jnp.ones((8, LANE), jnp.float32)
    turned = []
    for term in range(4):
        line = lax.dot_general(
            ones, sums_ref[term], (((1,), (1,)), ((), ())),
            precision=EXACT, preferred_element_type=jnp.float32,
        )[0:1]
        if tiles < LANE:
            line = jnp.concatenate([line, jnp.zeros((1, LANE - tiles), jnp.float32)], axis=1)
        turned.append(line)
    turned = jnp.concatenate(turned, axis=0)
    low_lanes = lax.broadcasted_iota(jnp.int32, (4, LANE), 1) < HALF_LANE

    def second_forward(g, carry):
        for k in range(GROUP):
            forward(g * GROUP + k)
        return carry

    def second_backward(g, carry):
        for k in range(GROUP):
            s = g * GROUP + k
            value = jnp.concatenate(backward(s), axis=0)
            value = value + pltpu.roll(value, HALF_LANE, 1)
            value = jnp.where(low_lanes, value, extra_ref[s])
            message_ref[s] = jnp.concatenate([turned, value], axis=0)
        return carry

    ref_low_ref[...] = map_ref[...].astype(jnp.bfloat16).astype(jnp.float32)
    lax.fori_loop(0, groups, second_forward, 0)
    total_ref[...] = jnp.zeros_like(total_ref)
    lax.fori_loop(0, groups, second_backward, 0)
    add_map(map_ref)


def passes(pair, table, heights, bands, ref_rows, col_terms, row_terms, extra, stride, pair_count):
    tiles, rows, cols = heights.shape
    vmem = pl.BlockSpec(memory_space=pltpu.VMEM)
    smem = pl.BlockSpec(memory_space=pltpu.SMEM)
    anywhere = pl.BlockSpec(memory_space=pl.ANY)
    return pl.pallas_call(
        functools.partial(passes_kernel, tiles, stride, pair_count, math.sqrt(tiles)),
        out_shape=(
            jax.ShapeDtypeStruct((rows, cols), jnp.float32),
            jax.ShapeDtypeStruct((tiles, 8, LANE), jnp.float32),
        ),
        in_specs=[smem, smem, anywhere, anywhere, vmem, vmem, vmem, vmem],
        out_specs=(vmem, vmem),
        scratch_shapes=[
            pltpu.VMEM((tiles, rows, cols), jnp.bfloat16),
            pltpu.VMEM((tiles, 2, LANE, BAND), jnp.bfloat16),
            pltpu.VMEM((tiles, 4 * rows, WIDE), jnp.bfloat16),
            pltpu.VMEM((4 * rows, WIDE), jnp.float32),
            pltpu.VMEM((rows, cols), jnp.float32),
            pltpu.VMEM((4, tiles, LANE), jnp.float32),
            pltpu.SemaphoreType.DMA((2, tiles // GROUP)),
        ],
        compiler_params=pltpu.CompilerParams(vmem_limit_bytes=VMEM_MAIN),
    )(pair, table, heights, bands, ref_rows, col_terms, row_terms, extra)


def finish_kernel(
    tiles, stride, scale, pixels, me_ref, got_ref, map_ref, effect_ref, row_ref, coef_ref, out_map_ref, out_coef_ref
):
    total = jnp.sum(got_ref[...], axis=0)
    step = total[0:4] / pixels
    later = total[4:8]
    lines = lax.broadcasted_iota(jnp.int32, (8, LANE), 0)
    wide = [jnp.broadcast_to(step[k : k + 1], (8, LANE))[:, :tiles] for k in range(4)]
    lines = lines[:, :tiles]
    flat = jnp.where(
        lines == 0, wide[0] - wide[3] * (2.0 / 3.0),
        jnp.where(lines == 1, wide[2], jnp.where(lines == 2, wide[3], 0.0)),
    )
    only = lines == 0

    def weigh(weights, term):
        return jnp.dot(weights, effect_ref[term], precision=EXACT, preferred_element_type=jnp.float32)

    level = weigh(flat, 0)
    level = level + weigh(jnp.where(only, wide[1], 0.0), 1) + weigh(jnp.where(only, wide[3], 0.0), 2)
    ax = row_ref[:, 0:1]
    change = level[0:1] + ax * (level[1:2] + ax * level[2:3])
    out_map_ref[...] = map_ref[...] - change / scale

    me = me_ref[0]
    before, after = neighbours(me, tiles, stride)
    lane = lax.broadcasted_iota(jnp.int32, (4, LANE), 1)
    reach = jnp.zeros((4, 1), jnp.float32)
    own = None
    for source, target in enumerate((me, before, after)):
        at = jnp.sum(jnp.where(lane == target, step, 0.0), axis=1, keepdims=True)
        own = at if source == 0 else own
        for k in range(4):
            place = HALF_LANE + 4 * source + k
            reach = reach + at[k : k + 1] * later[:, place : place + 1]
    fresh = jnp.sum(jnp.where(lane < HALF_LANE, later, 0.0), axis=1, keepdims=True)
    gain = own + (fresh - reach) / pixels
    line = lax.broadcasted_iota(jnp.int32, (4, LANE), 0)
    gain = jnp.sum(jnp.where(line == lane, gain, 0.0), axis=0, keepdims=True)
    out_coef_ref[...] = coef_ref[...] + gain[:, :4]


def finish(me, got, map_rows, effects, row_terms, coefs, stride, pixels):
    tiles = got.shape[0]
    vmem = pl.BlockSpec(memory_space=pltpu.VMEM)
    smem = pl.BlockSpec(memory_space=pltpu.SMEM)
    return pl.pallas_call(
        functools.partial(finish_kernel, tiles, stride, math.sqrt(tiles), pixels),
        out_shape=(
            jax.ShapeDtypeStruct(map_rows.shape, jnp.float32),
            jax.ShapeDtypeStruct(coefs.shape, jnp.float32),
        ),
        in_specs=[smem] + [vmem] * 5,
        out_specs=(vmem, vmem),
    )(me, got, map_rows, effects, row_terms, coefs)


def response_sums(moments, ax):
    zero, one = jnp.zeros_like(ax), jnp.ones_like(ax)
    in_terms = jnp.stack(
        [
            jnp.stack([one, zero, zero]),
            jnp.stack([zero, one, zero]),
            jnp.stack([ax, zero, zero]),
            jnp.stack([ax * ax - 2.0 / 3.0, zero, one]),
        ]
    )
    pairs = jnp.sum(in_terms[:, :, None, None, :] * in_terms[None, None, :, :, :], axis=-1)
    spreaded = moments[:, :, None, None, :, :]
    weights = pairs.transpose(0, 2, 3, 1)
    summed = jnp.sum(spreaded * weights, axis=(-1, -2))
    return summed.transpose(0, 2, 1, 3).reshape(moments.shape[0], 4, 12)


def local(observed_heights, ref_map, coefs, shifts, pair_offset, pair_width):
    rows, cols = ref_map.shape
    stride = lax.axis_size("axial")
    tiles = lax.axis_size("azim") * stride
    me = lax.axis_index(AXES)
    row_total = observed_heights.shape[2]
    pair_count = pair_offset.shape[2]
    pair = (me * rows // (row_total // pair_count)).reshape(1)

    words = jnp.concatenate(
        [
            coefs[0, 0],
            shifts[0],
            pair_offset[0, 0].astype(jnp.float32),
            pair_width[0, 0].astype(jnp.float32),
        ]
    )
    words = jnp.pad(words, (0, LANE - words.shape[0]))[None]
    owner = lax.broadcasted_iota(jnp.int32, (tiles, LANE), 0) == me
    table = gather_rows(jnp.where(owner, words, 0.0))
    heights = lax.all_to_all(
        observed_heights[0, 0].reshape(tiles, rows, cols), AXES, 0, 0, tiled=True
    )

    row_place = (me * rows).astype(jnp.float32) + jnp.arange(rows, dtype=jnp.float32)
    ax = (row_place - 0.5 * (row_total - 1)) * (2.0 / row_total)
    row_terms = jnp.broadcast_to(ax[:, None], (rows, LANE))
    col_terms = (jnp.arange(cols, dtype=jnp.float32) - 0.5 * (cols - 1)) * (2.0 / cols)
    col_terms = jnp.broadcast_to(col_terms[None], (8, cols))

    bands, effects, moments = prepare(pair, table, col_terms, stride, pair_count)
    effects = effects[:, :, :3].transpose(2, 0, 1, 3).reshape(3, tiles, cols)
    extra = response_sums(moments[:, :, :3, :3], ax)
    extra = jnp.pad(extra, ((0, 0), (0, 0), (HALF_LANE, LANE - HALF_LANE - 12)))

    map_rows, message = passes(
        pair, table, heights, bands, ref_map, col_terms, row_terms, extra, stride, pair_count
    )
    got = lax.all_to_all(message, AXES, 0, 0, tiled=True)
    new_map, new_coefs = finish(
        me.reshape(1), got, map_rows, effects, row_terms, coefs[0], stride, row_total * cols
    )
    return (new_map, new_coefs[None])


def solution(mesh):
    in_specs = (
        P("axial", "azim", None, None),
        P(("azim", "axial"), None),
        P("axial", "azim", None),
        P("axial", "azim"),
        P("axial", "azim", None),
        P("axial", "azim", None),
    )
    out_specs = (P(("azim", "axial"), None), P("axial", "azim", None))
    return jax.shard_map(local, mesh=mesh, in_specs=in_specs, out_specs=out_specs, check_vma=False)
```

time: 173 us -> 132 us (0.76)
  blocking collectives: 68.7 us -> 0 us
  waiting for transfers between devices: 21.5 us -> 57.4 us
  other arithmetic: 6.59 us -> 1.23 us
  starting transfers between devices: 23.2 us -> 18.3 us
  local copies, waits for them, and re-layouts: 2.78 us -> 5.92 us
  Pallas kernels: 48.8 us -> 47 us
    all_gather x1 -> x0, blocking collectives: 68.7 us -> none  [local(): table = lax.all_gather(words, AXES, axis=0, tiled=True)]
    ppermute x10 -> x6, waiting for transfers between devices: 21.5 us -> 50.4 us  [exchange(): lax.ppermute(value, axis, [(i, i ^ k) for i in range(size)])]
    ppermute x10 -> x6, starting transfers between devices: 15.9 us -> 7.07 us  [exchange(): lax.ppermute(value, axis, [(i, i ^ k) for i in range(size)])]
    all_to_all x0 -> x1, waiting for transfers between devices: none -> 7.06 us  [local(): got = lax.all_to_all(message, AXES, 0, 0, tiled=True)]
    all_to_all x0 -> x1, starting transfers between devices: none -> 3.92 us  [local(): got = lax.all_to_all(message, AXES, 0, 0, tiled=True)]
    mul x2 -> x1, other arithmetic: 2.14 us -> 0.01 us  [local(): ax = (row_place - 0.5 * (row_total - 1)) * (2.0 / row_total)]
    pallas_call x2 -> x3, Pallas kernels: 48.8 us -> 47 us  [the longest x1 27 us: prepare(): pl.pallas_call(functools.partial(prepare_kernel, tiles, stride, pair_coun...]
  transfers between devices with their start and end apart: 11 -> 8, of which waited for: 10 -> 6; matrix products, arithmetic and copies ran while one was open for 3% -> 4% of each run, Pallas kernels for 0% -> 21%
where the time goes in v2:
time: 132 us; the launch traced here: 131 us
  waiting for transfers between devices  57.4 us (43%)
  Pallas kernels  47 us (36%)
  starting transfers between devices  18.3 us (14%)
  local copies, waits for them, and re-layouts  5.92 us (4%)
  between operations  1.5 us (1%)
    ppermute x6, waiting for transfers between devices, exchange(): lax.ppermute(value, axis, [(i, i ^ k) for i in range(size)])  50.4 us
    pallas_call x1, Pallas kernels, prepare(): pl.pallas_call(functools.partial(prepare_kernel, tiles, stride, pair_coun...  27 us
    pallas_call x1, Pallas kernels, passes(): pl.pallas_call(functools.partial(passes_kernel, tiles, stride, pair_count...  17.8 us
    all_to_all x1, starting transfers between devices, local(): lax.all_to_all(observed_heights[0, 0].reshape(tiles, rows, cols), AXES, 0...  7.3 us
    ppermute x6, starting transfers between devices, exchange(): lax.ppermute(value, axis, [(i, i ^ k) for i in range(size)])  7.07 us
    all_to_all x1, waiting for transfers between devices, local(): got = lax.all_to_all(message, AXES, 0, 0, tiled=True)  7.06 us
    all_to_all x1, starting transfers between devices, local(): got = lax.all_to_all(message, AXES, 0, 0, tiled=True)  3.92 us
  transfers between devices with their start and end apart: 8, of which 6 were waited for; matrix products, arithmetic and copies ran while one was open for 4% of the time, Pallas kernels for 21%

profile of v2, /device:TPU:0, one launch (start us, length us, event | category | flops | bytes accessed | tf_op | source)
XLA Modules:
  0.0 131.4 jit_solution(10840833250494786402)
XLA Ops:
  0.7 7.3 %all-to-all-start = ((bf16[32,32,1024]{2,1,0:T(8,128)(2,1)}), bf16[32,32,1024]{2,1,0:T(8,128)(2,1)S(1)}, u32[]{:S(2)}, u32[]{:S(2)}) async-start(bf16[32,32,1024]{2,1,0:T(8,128)(2,1)} %bitcast.23), calls=%async_computation | async-start | bytes 4194304 | tf_op jit(solution)/shard_map/all_to_all | solution.py:439
  8.7 0.1 select_maximum_fusion
  8.8 0.1 broadcast_select_fusion
  8.9 1.8 %collective-permute-start = (f32[32,128]{1,0:T(8,128)S(1)}, f32[32,128]{1,0:T(8,128)S(1)}, u32[]{:S(2)}, u32[]{:S(2)}) collective-permute-start(f32[32,128]{1,0:T(8,128)S(1)} %broadcast_select_fusion), channel_id=1, source_target_pairs={{0,8},{4,12},{8,0},{12,4},{16,24},{20,28},{24,16},{28,20},{1,9},{5... | collective-permute-start | bytes 49160 | tf_op jit(solution)/shard_map/ppermute | solution.py:26
  10.6 2.4 %collective-permute-start.1 = (f32[32,128]{1,0:T(8,128)S(1)}, f32[32,128]{1,0:T(8,128)S(1)}, u32[]{:S(2)}, u32[]{:S(2)}) collective-permute-start(f32[32,128]{1,0:T(8,128)S(1)} %broadcast_select_fusion), channel_id=1, source_target_pairs={{0,16},{4,20},{8,24},{12,28},{16,0},{20,4},{24,8},{28,12},{1,17},{... | collective-permute-start | bytes 49160 | tf_op jit(solution)/shard_map/ppermute | solution.py:26
  13.0 0.2 collective-permute-start.2
  13.5 30.2 %collective-permute-done = f32[32,128]{1,0:T(8,128)S(1)} collective-permute-done((f32[32,128]{1,0:T(8,128)S(1)}, f32[32,128]{1,0:T(8,128)S(1)}, u32[]{:S(2)}, u32[]{:S(2)}) %collective-permute-start) | collective-permute-done | bytes 16416 | tf_op jit(solution)/shard_map/ppermute | solution.py:26
  43.7 14.4 %collective-permute-done.1 = f32[32,128]{1,0:T(8,128)S(1)} collective-permute-done((f32[32,128]{1,0:T(8,128)S(1)}, f32[32,128]{1,0:T(8,128)S(1)}, u32[]{:S(2)}, u32[]{:S(2)}) %collective-permute-start.1) | collective-permute-done | bytes 16416 | tf_op jit(solution)/shard_map/ppermute | solution.py:26
  58.2 1.3 collective-permute-start.3
  59.5 0.1 multiply_reduce_fusion.1
  59.6 2.3 %collective-permute-done.3 = f32[32,128]{1,0:T(8,128)S(1)} collective-permute-done((f32[32,128]{1,0:T(8,128)S(1)}, f32[32,128]{1,0:T(8,128)S(1)}, u32[]{:S(2)}, u32[]{:S(2)}) %collective-permute-start.3) | collective-permute-done | bytes 16416 | tf_op jit(solution)/shard_map/ppermute | solution.py:26
  61.9 1.4 %collective-permute-start.4 = (f32[32,128]{1,0:T(8,128)S(1)}, f32[32,128]{1,0:T(8,128)S(1)}, u32[]{:S(2)}, u32[]{:S(2)}) collective-permute-start(f32[32,128]{1,0:T(8,128)S(1)} %add.86), channel_id=1, source_target_pairs={{0,2},{1,3},{2,0},{3,1},{4,6},{5,7},{6,4},{7,5},{8,10},{9,11},{10,... | collective-permute-start | bytes 49160 | tf_op jit(solution)/shard_map/ppermute | solution.py:26
  63.3 2.3 %collective-permute-done.4 = f32[32,128]{1,0:T(8,128)S(1)} collective-permute-done((f32[32,128]{1,0:T(8,128)S(1)}, f32[32,128]{1,0:T(8,128)S(1)}, u32[]{:S(2)}, u32[]{:S(2)}) %collective-permute-start.4) | collective-permute-done | bytes 16416 | tf_op jit(solution)/shard_map/ppermute | solution.py:26
  65.8 1.1 collective-permute-done.5
  66.9 0.6 add.88.words_ref.table_ref
  67.5 0.6 broadcast_in_dim.36.col_ref
  68.1 27.0 %shard_map.77 = (bf16[32,2,128,640]{3,2,1,0:T(8,128)(2,1)}, f32[32,4,8,256]{3,2,1,0:T(8,128)}, f32[32,3,8,128]{3,2,1,0:T(8,128)}) custom-call(s32[1]{0:T(128)} %bitcast.1.pair_ref, f32[32,128]{1,0:T(8,128)} %add.88.words_ref.table_ref, f32[32,128]{1,0:T(8,128)} %add.88.words_ref.table_ref, f32[8,1024]{1,0:T(8,128)} %broadcast_in_dim.36.col_ref), custom_call_target="tpu_custom_call" | custom-call | tf_op jit(solution)/shard_map/pallas_call | solution.py:174
  95.1 1.0 slice.6
  96.1 0.1 copy.11
  96.3 0.1 multiply_reduce_fusion
  96.4 0.1 copy.15
  96.5 0.7 pad.10.extra_ref
  97.3 0.8 broadcast_in_dim.37.row_ref
  98.0 0.6 copy-done
  98.6 17.8 %shard_map.78 = (f32[32,1024]{1,0:T(8,128)}, f32[32,8,128]{2,1,0:T(8,128)}) custom-call(s32[1]{0:T(128)} %bitcast.1.pair_ref, f32[32,128]{1,0:T(8,128)} %add.88.words_ref.table_ref, bf16[32,32,1024]{2,1,0:T(8,128)(2,1)} %copy-done, bf16[32,2,128,640]{3,2,1,0:T(8,128)(2,1)} %get-tuple-element.9.band_hbm, f32[32,1024]{1,0:T(8,128)} %ref_ref.1, ...), custom_call_target="tpu_custom_call" | custom-call | tf_op jit(solution)/shard_map/pallas_call | solution.py:324
  116.4 3.9 %all-to-all-start.1 = ((f32[32,8,128]{2,1,0:T(8,128)}), f32[32,8,128]{2,1,0:T(8,128)S(1)}, u32[]{:S(2)}, u32[]{:S(2)}) async-start(f32[32,8,128]{2,1,0:T(8,128)} %get-tuple-element.11), calls=%async_computation.1 | async-start | bytes 262144 | tf_op jit(solution)/shard_map/all_to_all | solution.py:457
  120.4 0.1 slice_bitcast_fusion
  120.5 0.1 copy.16
  120.6 1.0 reshape.57.effect_ref
  121.5 7.1 %all-to-all-done.1.got_ref = f32[32,8,128]{2,1,0:T(8,128)S(1)} async-done(((f32[32,8,128]{2,1,0:T(8,128)}), f32[32,8,128]{2,1,0:T(8,128)S(1)}, u32[]{:S(2)}, u32[]{:S(2)}) %all-to-all-start.1) | async-done | bytes 131104 | tf_op jit(solution)/shard_map/all_to_all | solution.py:457
  128.6 0.6 copy-done.1
  129.2 2.2 %shard_map.79 = (f32[32,1024]{1,0:T(8,128)}, f32[1,4]{1,0:T(1,128)}) custom-call(s32[1]{0:T(128)} %bitcast.me_ref, f32[32,8,128]{2,1,0:T(8,128)} %copy-done.1, f32[32,1024]{1,0:T(8,128)} %get-tuple-element.12.map_ref, f32[3,32,1024]{2,1,0:T(8,128)} %reshape.57.effect_ref, f32[32,128]{1,0:T(8,128)} %broadcast_in_dim.37.row_ref, f32[1,4]{1,0:T(1,128)} %bitcast.27), custom_call_target="tpu_custom_call" | custom-call | tf_op jit(solution)/shard_map/pallas_call | solution.py:391
  (33 shorter events, 0.4 us)
Async XLA Ops:
  0.6 8.0 %copy-start.6 = (s32[1,1,16]{2,1,0:T(1,128)S(1)}, s32[1,1,16]{2,1,0:T(1,128)}, u32[]{:S(2)}) copy-start(s32[1,1,16]{2,1,0:T(1,128)} %param.11) | copy-start | bytes 196
  0.6 8.0 %copy-start.7 = (s32[1,1,16]{2,1,0:T(1,128)S(1)}, s32[1,1,16]{2,1,0:T(1,128)}, u32[]{:S(2)}) copy-start(s32[1,1,16]{2,1,0:T(1,128)} %param.10) | copy-start | bytes 196
  0.6 8.0 %copy-start.5 = (f32[1,1,4]{2,1,0:T(1,128)S(1)}, f32[1,1,4]{2,1,0:T(1,128)}, u32[]{:S(2)}) copy-start(f32[1,1,4]{2,1,0:T(1,128)} %param.8) | copy-start | bytes 52
  0.7 12.8 %copy-start.3 = (f32[1,3,32]{2,1,0:T(4,128)S(1)}, f32[1,3,32]{2,1,0:T(4,128)}, u32[]{:S(2)}) copy-start(f32[1,3,32]{2,1,0:T(4,128)} %constant.48.clone.1) | copy-start | bytes 1156
  0.7 12.8 %copy-start.4 = (f32[1,3,32]{2,1,0:T(4,128)S(1)}, f32[1,3,32]{2,1,0:T(4,128)}, u32[]{:S(2)}) copy-start(f32[1,3,32]{2,1,0:T(4,128)} %constant.49.clone.1) | copy-start | bytes 1156
  0.7 96.6 %all-to-all-start = ((bf16[32,32,1024]{2,1,0:T(8,128)(2,1)}), bf16[32,32,1024]{2,1,0:T(8,128)(2,1)S(1)}, u32[]{:S(2)}, u32[]{:S(2)}) async-start(bf16[32,32,1024]{2,1,0:T(8,128)(2,1)} %bitcast.23), calls=%async_computation | async-start | bytes 4194304 | tf_op jit(solution)/shard_map/all_to_all | solution.py:439
  8.9 34.9 %collective-permute-start = (f32[32,128]{1,0:T(8,128)S(1)}, f32[32,128]{1,0:T(8,128)S(1)}, u32[]{:S(2)}, u32[]{:S(2)}) collective-permute-start(f32[32,128]{1,0:T(8,128)S(1)} %broadcast_select_fusion), channel_id=1, source_target_pairs={{0,8},{4,12},{8,0},{12,4},{16,24},{20,28},{24,16},{28,20},{1,9},{5... | collective-permute-start | bytes 49160 | tf_op jit(solution)/shard_map/ppermute | solution.py:26
  10.6 47.5 %collective-permute-start.1 = (f32[32,128]{1,0:T(8,128)S(1)}, f32[32,128]{1,0:T(8,128)S(1)}, u32[]{:S(2)}, u32[]{:S(2)}) collective-permute-start(f32[32,128]{1,0:T(8,128)S(1)} %broadcast_select_fusion), channel_id=1, source_target_pairs={{0,16},{4,20},{8,24},{12,28},{16,0},{20,4},{24,8},{28,12},{1,17},{... | collective-permute-start | bytes 49160 | tf_op jit(solution)/shard_map/ppermute | solution.py:26
  13.0 45.1 %collective-permute-start.2 = (f32[32,128]{1,0:T(8,128)S(1)}, f32[32,128]{1,0:T(8,128)S(1)}, u32[]{:S(2)}, u32[]{:S(2)}) collective-permute-start(f32[32,128]{1,0:T(8,128)S(1)} %broadcast_select_fusion), channel_id=1, source_target_pairs={{0,24},{4,28},{8,16},{12,20},{16,8},{20,12},{24,0},{28,4},{1,25},{... | collective-permute-start | bytes 49160 | tf_op jit(solution)/shard_map/ppermute | solution.py:26
  58.2 3.7 %collective-permute-start.3 = (f32[32,128]{1,0:T(8,128)S(1)}, f32[32,128]{1,0:T(8,128)S(1)}, u32[]{:S(2)}, u32[]{:S(2)}) collective-permute-start(f32[32,128]{1,0:T(8,128)S(1)} %add_add_fusion), channel_id=1, source_target_pairs={{0,4},{4,0},{8,12},{12,8},{16,20},{20,16},{24,28},{28,24},{1,5},{5... | collective-permute-start | bytes 49160 | tf_op jit(solution)/shard_map/ppermute | solution.py:26
  61.9 3.7 %collective-permute-start.4 = (f32[32,128]{1,0:T(8,128)S(1)}, f32[32,128]{1,0:T(8,128)S(1)}, u32[]{:S(2)}, u32[]{:S(2)}) collective-permute-start(f32[32,128]{1,0:T(8,128)S(1)} %add.86), channel_id=1, source_target_pairs={{0,2},{1,3},{2,0},{3,1},{4,6},{5,7},{6,4},{7,5},{8,10},{9,11},{10,... | collective-permute-start | bytes 49160 | tf_op jit(solution)/shard_map/ppermute | solution.py:26
  65.7 1.2 collective-permute-start.5
  97.3 1.3 %copy-start = (bf16[32,32,1024]{2,1,0:T(8,128)(2,1)}, bf16[32,32,1024]{2,1,0:T(8,128)(2,1)S(1)}, u32[]{:S(2)}) copy-start(bf16[32,32,1024]{2,1,0:T(8,128)(2,1)S(1)} %all-to-all-done.height_hbm) | copy-start | bytes 6291460
  98.6 21.8 %copy-start.2 = (f32[32,4,8,256]{3,2,1,0:T(8,128)S(1)}, f32[32,4,8,256]{3,2,1,0:T(8,128)}, u32[]{:S(2)}) copy-start(f32[32,4,8,256]{3,2,1,0:T(8,128)} %get-tuple-element.13) | copy-start | bytes 3145732
  116.4 12.2 %all-to-all-start.1 = ((f32[32,8,128]{2,1,0:T(8,128)}), f32[32,8,128]{2,1,0:T(8,128)S(1)}, u32[]{:S(2)}, u32[]{:S(2)}) async-start(f32[32,8,128]{2,1,0:T(8,128)} %get-tuple-element.11), calls=%async_computation.1 | async-start | bytes 262144 | tf_op jit(solution)/shard_map/all_to_all | solution.py:457
  128.6 0.6 copy-start.1

commit v3 on v2

--- a/solution.py
+++ b/solution.py
@@ -26,11 +26,13 @@
     return sum(lax.ppermute(value, axis, [(i, i ^ k) for i in range(size)]) for k in steps)
 
 
-def gather_rows(value):
-    azim, axial = lax.axis_size("azim"), lax.axis_size("axial")
-    value = value + exchange(value, "azim", range(2, azim, 2))
+def gather_far(value):
+    return value + exchange(value, "azim", range(2, lax.axis_size("azim"), 2))
+
+
+def gather_near(value):
     value = value + exchange(value, "azim", [1])
-    step = axial // 2
+    step = lax.axis_size("axial") // 2
     while step:
         value = value + exchange(value, "axial", [step])
         step //= 2
@@ -84,23 +86,27 @@
     return before, after
 
 
+def axis_terms(shape, dim, total, first=0):
+    place = lax.broadcasted_iota(jnp.int32, shape, dim).astype(jnp.float32) + first
+    return (place - 0.5 * (total - 1)) * (2.0 / total)
+
+
 def two_parts(value):
     high = value.astype(jnp.bfloat16).astype(jnp.float32)
     return high, value - high
 
 
 def prepare_kernel(
-    tiles, stride, pair_count, pair_ref, words_ref, table_ref, col_ref,
+    tiles, cols, stride, pair_count, pair_ref, words_ref, table_ref,
     band_ref, effect_ref, moment_ref, tap_ref, seen_ref, base_ref
 ):
-    cols = col_ref.shape[1]
     blocks = cols // WIDE
     pair = pair_ref[0]
     place = lax.broadcasted_iota(jnp.int32, (tiles, 2 * SPAN), 1).astype(jnp.float32) - SPAN
     shift = table_ref[:, 4:5]
     tap_ref[0] = tap_values(-place - shift)
     tap_ref[1] = tap_values(place - shift)
-    az = col_ref[0:1, :]
+    az = axis_terms((8, cols), 1, cols)
     row = lax.broadcasted_iota(jnp.int32, (8, cols), 0)
     base = jnp.where(row == 0, 1.0, jnp.where(row == 1, az, jnp.where(row == 2, az * az, 0.0)))
     high, low = two_parts(base)
@@ -126,7 +132,7 @@
     )
     column = column.astype(jnp.float32)
     lanes = lax.broadcasted_iota(jnp.int32, (8, LANE), 1)
-    az_blocks = [az[:, k : k + LANE] for k in range(0, cols, LANE)]
+    az_blocks = [az[0:1, k : k + LANE] for k in range(0, cols, LANE)]
 
     def inside(s):
         start = words_ref[s, 5 + pair]
@@ -165,20 +171,19 @@
     lax.fori_loop(0, tiles, respond, 0)
 
 
-def prepare(pair, table, col_terms, stride, pair_count):
+def prepare(pair, table, cols, stride, pair_count):
     tiles = table.shape[0]
-    cols = col_terms.shape[1]
     blocks = cols // WIDE
     vmem = pl.BlockSpec(memory_space=pltpu.VMEM)
     smem = pl.BlockSpec(memory_space=pltpu.SMEM)
     return pl.pallas_call(
-        functools.partial(prepare_kernel, tiles, stride, pair_count),
+        functools.partial(prepare_kernel, tiles, cols, stride, pair_count),
         out_shape=(
             jax.ShapeDtypeStruct((tiles, 2, LANE, BAND), jnp.bfloat16),
             jax.ShapeDtypeStruct((tiles, blocks, 8, WIDE), jnp.float32),
             jax.ShapeDtypeStruct((tiles, 3, 8, LANE), jnp.float32),
         ),
-        in_specs=[smem, smem, vmem, vmem],
+        in_specs=[smem, smem, vmem],
         out_specs=(vmem, vmem, vmem),
         scratch_shapes=[
             pltpu.VMEM((2, tiles, 2 * SPAN), jnp.float32),
@@ -186,17 +191,17 @@
             pltpu.VMEM((16 * blocks, 3 * WIDE), jnp.bfloat16),
         ],
         compiler_params=pltpu.CompilerParams(vmem_limit_bytes=VMEM_MAIN),
-    )(pair, table, table, col_terms)
+    )(pair, table, table)
 
 
 def passes_kernel(
-    tiles, stride, pair_count, scale, pair_ref, words_ref, height_hbm, band_hbm, ref_ref, col_ref, row_ref, extra_ref,
+    tiles, row_total, stride, pair_count, scale, place_ref, words_ref, height_hbm, band_hbm, ref_ref, extra_ref,
     map_ref, message_ref, height_ref, band_ref, resampled_ref, total_ref, ref_low_ref, sums_ref, sems
 ):
     rows, cols = ref_ref.shape
     blocks = cols // WIDE
     groups = tiles // GROUP
-    pair = pair_ref[0]
+    pair = place_ref[0]
 
     def copies(g):
         part = pl.ds(g * GROUP, GROUP)
@@ -209,19 +214,22 @@
         for copy in copies(g):
             copy.start()
 
-    az = col_ref[0:1, :]
+    az = axis_terms((1, cols), 1, cols)
+    first_row = place_ref[1].astype(jnp.float32)
+    ax = axis_terms((rows, LANE), 0, row_total, first_row)
+    ax_wide = axis_terms((rows, WIDE), 0, row_total, first_row).reshape(rows // 8, 8, WIDE)
     column = lax.broadcasted_iota(jnp.int32, (2 * rows, WIDE), 1) + jnp.where(
         lax.broadcasted_iota(jnp.int32, (2 * rows, WIDE), 0) >= rows, WIDE, 0
     )
     column = column.astype(jnp.float32)
 
     def forward(s):
-        ax = row_ref[:, 0:1]
+        tilt = ax[:, 0:1]
         shape = (
             words_ref[s, 0]
             + words_ref[s, 1] * az
-            + words_ref[s, 2] * ax
-            + words_ref[s, 3] * (az * az + ax * ax - 2.0 / 3.0)
+            + words_ref[s, 2] * tilt
+            + words_ref[s, 3] * (az * az + tilt * tilt - 2.0 / 3.0)
         )
         corrected = height_ref[s].astype(jnp.float32) - ref_low_ref[...] - shape
         out = mixed(stack_blocks(corrected).astype(jnp.bfloat16), rows, band_ref, s, 0)
@@ -241,14 +249,12 @@
         pulled = mixed(upstream, rows, band_ref, s, 1)
         total_ref[...] += pulled
         plain, tilted, bent = [], [], []
-        weight = row_ref[...]
-        weight = jnp.concatenate([weight, weight], axis=1).reshape(rows // 8, 8, WIDE)
         for k in range(blocks):
             block = pulled[k * rows : (k + 1) * rows].reshape(rows // 8, 8, WIDE)
-            first = block * weight
+            first = block * ax_wide
             plain.append(jnp.sum(block, axis=0))
             tilted.append(jnp.sum(first, axis=0))
-            bent.append(jnp.sum(first * weight, axis=0))
+            bent.append(jnp.sum(first * ax_wide, axis=0))
         plain = jnp.concatenate(plain, axis=1)
         tilted = jnp.concatenate(tilted, axis=1)
         bent = jnp.concatenate(bent, axis=1)
@@ -316,18 +322,18 @@
     add_map(map_ref)
 
 
-def passes(pair, table, heights, bands, ref_rows, col_terms, row_terms, extra, stride, pair_count):
+def passes(place, table, heights, bands, ref_rows, extra, row_total, stride, pair_count):
     tiles, rows, cols = heights.shape
     vmem = pl.BlockSpec(memory_space=pltpu.VMEM)
     smem = pl.BlockSpec(memory_space=pltpu.SMEM)
     anywhere = pl.BlockSpec(memory_space=pl.ANY)
     return pl.pallas_call(
-        functools.partial(passes_kernel, tiles, stride, pair_count, math.sqrt(tiles)),
+        functools.partial(passes_kernel, tiles, row_total, stride, pair_count, math.sqrt(tiles)),
         out_shape=(
             jax.ShapeDtypeStruct((rows, cols), jnp.float32),
             jax.ShapeDtypeStruct((tiles, 8, LANE), jnp.float32),
         ),
-        in_specs=[smem, smem, anywhere, anywhere, vmem, vmem, vmem, vmem],
+        in_specs=[smem, smem, anywhere, anywhere, vmem, vmem],
         out_specs=(vmem, vmem),
         scratch_shapes=[
             pltpu.VMEM((tiles, rows, cols), jnp.bfloat16),
@@ -339,11 +345,11 @@
             pltpu.SemaphoreType.DMA((2, tiles // GROUP)),
         ],
         compiler_params=pltpu.CompilerParams(vmem_limit_bytes=VMEM_MAIN),
-    )(pair, table, heights, bands, ref_rows, col_terms, row_terms, extra)
+    )(place, table, heights, bands, ref_rows, extra)
 
 
 def finish_kernel(
-    tiles, stride, scale, pixels, me_ref, got_ref, map_ref, effect_ref, row_ref, coef_ref, out_map_ref, out_coef_ref
+    tiles, row_total, stride, scale, pixels, place_ref, got_ref, map_ref, effect_ref, coef_ref, out_map_ref, out_coef_ref
 ):
     total = jnp.sum(got_ref[...], axis=0)
     step = total[0:4] / pixels
@@ -362,11 +368,11 @@
 
     level = weigh(flat, 0)
     level = level + weigh(jnp.where(only, wide[1], 0.0), 1) + weigh(jnp.where(only, wide[3], 0.0), 2)
-    ax = row_ref[:, 0:1]
+    ax = axis_terms((map_ref.shape[0], LANE), 0, row_total, place_ref[1].astype(jnp.float32))[:, 0:1]
     change = level[0:1] + ax * (level[1:2] + ax * level[2:3])
     out_map_ref[...] = map_ref[...] - change / scale
 
-    me = me_ref[0]
+    me = place_ref[2]
     before, after = neighbours(me, tiles, stride)
     lane = lax.broadcasted_iota(jnp.int32, (4, LANE), 1)
     reach = jnp.zeros((4, 1), jnp.float32)
@@ -384,19 +390,21 @@
     out_coef_ref[...] = coef_ref[...] + gain[:, :4]
 
 
-def finish(me, got, map_rows, effects, row_terms, coefs, stride, pixels):
+def finish(place, got, map_rows, effects, coefs, row_total, stride):
     tiles = got.shape[0]
     vmem = pl.BlockSpec(memory_space=pltpu.VMEM)
     smem = pl.BlockSpec(memory_space=pltpu.SMEM)
     return pl.pallas_call(
-        functools.partial(finish_kernel, tiles, stride, math.sqrt(tiles), pixels),
+        functools.partial(
+            finish_kernel, tiles, row_total, stride, math.sqrt(tiles), row_total * map_rows.shape[1]
+        ),
         out_shape=(
             jax.ShapeDtypeStruct(map_rows.shape, jnp.float32),
             jax.ShapeDtypeStruct(coefs.shape, jnp.float32),
         ),
-        in_specs=[smem] + [vmem] * 5,
+        in_specs=[smem] + [vmem] * 4,
         out_specs=(vmem, vmem),
-    )(me, got, map_rows, effects, row_terms, coefs)
+    )(place, got, map_rows, effects, coefs)
 
 
 def response_sums(moments, ax):
@@ -423,7 +431,7 @@
     me = lax.axis_index(AXES)
     row_total = observed_heights.shape[2]
     pair_count = pair_offset.shape[2]
-    pair = (me * rows // (row_total // pair_count)).reshape(1)
+    place = jnp.stack([me * rows // (row_total // pair_count), me * rows, me])
 
     words = jnp.concatenate(
         [
@@ -435,28 +443,25 @@
     )
     words = jnp.pad(words, (0, LANE - words.shape[0]))[None]
     owner = lax.broadcasted_iota(jnp.int32, (tiles, LANE), 0) == me
-    table = gather_rows(jnp.where(owner, words, 0.0))
+    table = gather_far(jnp.where(owner, words, 0.0))
+    table, own_heights = lax.optimization_barrier((table, observed_heights))
     heights = lax.all_to_all(
-        observed_heights[0, 0].reshape(tiles, rows, cols), AXES, 0, 0, tiled=True
-    )
-
-    row_place = (me * rows).astype(jnp.float32) + jnp.arange(rows, dtype=jnp.float32)
-    ax = (row_place - 0.5 * (row_total - 1)) * (2.0 / row_total)
-    row_terms = jnp.broadcast_to(ax[:, None], (rows, LANE))
-    col_terms = (jnp.arange(cols, dtype=jnp.float32) - 0.5 * (cols - 1)) * (2.0 / cols)
-    col_terms = jnp.broadcast_to(col_terms[None], (8, cols))
-
-    bands, effects, moments = prepare(pair, table, col_terms, stride, pair_count)
+        own_heights[0, 0].reshape(tiles, rows, cols), AXES, 0, 0, tiled=True
+    )
+    table = gather_near(table)
+
+    ax = axis_terms((rows,), 0, row_total, (me * rows).astype(jnp.float32))
+    bands, effects, moments = prepare(place, table, cols, stride, pair_count)
     effects = effects[:, :, :3].transpose(2, 0, 1, 3).reshape(3, tiles, cols)
     extra = response_sums(moments[:, :, :3, :3], ax)
     extra = jnp.pad(extra, ((0, 0), (0, 0), (HALF_LANE, LANE - HALF_LANE - 12)))
 
     map_rows, message = passes(
-        pair, table, heights, bands, ref_map, col_terms, row_terms, extra, stride, pair_count
+        place, table, heights, bands, ref_map, extra, row_total, stride, pair_count
     )
     got = lax.all_to_all(message, AXES, 0, 0, tiled=True)
     new_map, new_coefs = finish(
-        me.reshape(1), got, map_rows, effects, row_terms, coefs[0], stride, row_total * cols
+        place, got, map_rows, effects, coefs[0], row_total, stride
     )
     return (new_map, new_coefs[None])
 

time: 132 us -> 102 us (0.77)
  waiting for transfers between devices: 57.4 us -> 24.3 us
  starting transfers between devices: 18.3 us -> 20.8 us
  other arithmetic: 1.23 us -> 3.17 us
    ppermute x6, waiting for transfers between devices: 50.4 us -> 16 us  [exchange(): lax.ppermute(value, axis, [(i, i ^ k) for i in range(size)])]
    ppermute x6, starting transfers between devices: 7.07 us -> 11.9 us  [exchange(): lax.ppermute(value, axis, [(i, i ^ k) for i in range(size)])]
    all_to_all x1, starting transfers between devices: 7.3 us -> 2.86 us  [local(): lax.all_to_all(own_heights[0, 0].reshape(tiles, rows, cols), AXES, 0, 0,...]
    all_to_all x1, starting transfers between devices: 3.92 us -> 6.04 us  [local(): got = lax.all_to_all(message, AXES, 0, 0, tiled=True)]
    broadcast_in_dim x2 -> x0, local copies, waits for them, and re-layouts: 1.37 us -> none  [the longest x1 0.77 us: local(): row_terms = jnp.broadcast_to(ax[:, None], (rows, LANE))]
  transfers between devices with their start and end apart: 8 -> 8, of which waited for: 6 -> 7; matrix products, arithmetic and copies ran while one was open for 4% -> 5% of each run, Pallas kernels for 21% -> 27%
where the time goes in v3:
time: 102 us
  Pallas kernels  46.7 us (46%)
  waiting for transfers between devices  24.3 us (24%)
  starting transfers between devices  20.8 us (20%)
  local copies, waits for them, and re-layouts  5.27 us (5%)
  other arithmetic  3.17 us (3%)
  between operations  1.41 us (1%)
    pallas_call x1, Pallas kernels, prepare(): pl.pallas_call(functools.partial(prepare_kernel, tiles, cols, stride, pai...  27 us
    pallas_call x1, Pallas kernels, passes(): pl.pallas_call(functools.partial(passes_kernel, tiles, row_total, stride,...  17.5 us
    ppermute x6, waiting for transfers between devices, exchange(): lax.ppermute(value, axis, [(i, i ^ k) for i in range(size)])  16 us
    ppermute x6, starting transfers between devices, exchange(): lax.ppermute(value, axis, [(i, i ^ k) for i in range(size)])  11.9 us
    all_to_all x1, waiting for transfers between devices, local(): got = lax.all_to_all(message, AXES, 0, 0, tiled=True)  7.07 us
    all_to_all x1, starting transfers between devices, local(): got = lax.all_to_all(message, AXES, 0, 0, tiled=True)  6.04 us
    all_to_all x1, starting transfers between devices, local(): lax.all_to_all(own_heights[0, 0].reshape(tiles, rows, cols), AXES, 0, 0,...  2.86 us
    pallas_call x1, Pallas kernels, finish(): pl.pallas_call(functools.partial(finish_kernel, tiles, row_total, stride,...  2.16 us
  transfers between devices with their start and end apart: 8, of which 7 were waited for; matrix products, arithmetic and copies ran while one was open for 5% of the time, Pallas kernels for 27%

profile of v3, /device:TPU:0, one launch (start us, length us, event | category | flops | bytes accessed | tf_op | source)
XLA Modules:
  0.0 101.6 jit_solution(18420797367256475495)
XLA Ops:
  1.3 0.7 convert_bitcast_fusion
  2.0 0.7 select_maximum_fusion
  2.8 3.0 %collective-permute-start = (f32[32,128]{1,0:T(8,128)S(1)}, f32[32,128]{1,0:T(8,128)S(1)}, u32[]{:S(2)}, u32[]{:S(2)}) collective-permute-start(f32[32,128]{1,0:T(8,128)S(1)} %broadcast_select_fusion), channel_id=1, source_target_pairs={{0,8},{4,12},{8,0},{12,4},{16,24},{20,28},{24,16},{28,20},{1,9},{5... | collective-permute-start | bytes 49160 | tf_op jit(solution)/shard_map/ppermute | solution.py:26
  5.8 2.6 %collective-permute-start.1 = (f32[32,128]{1,0:T(8,128)S(1)}, f32[32,128]{1,0:T(8,128)S(1)}, u32[]{:S(2)}, u32[]{:S(2)}) collective-permute-start(f32[32,128]{1,0:T(8,128)S(1)} %broadcast_select_fusion), channel_id=1, source_target_pairs={{0,16},{4,20},{8,24},{12,28},{16,0},{20,4},{24,8},{28,12},{1,17},{... | collective-permute-start | bytes 49160 | tf_op jit(solution)/shard_map/ppermute | solution.py:26
  8.4 2.1 %collective-permute-done.1 = f32[32,128]{1,0:T(8,128)S(1)} collective-permute-done((f32[32,128]{1,0:T(8,128)S(1)}, f32[32,128]{1,0:T(8,128)S(1)}, u32[]{:S(2)}, u32[]{:S(2)}) %collective-permute-start.1) | collective-permute-done | bytes 16416 | tf_op jit(solution)/shard_map/ppermute | solution.py:26
  10.5 3.4 %collective-permute-done.2 = f32[32,128]{1,0:T(8,128)S(1)} collective-permute-done((f32[32,128]{1,0:T(8,128)S(1)}, f32[32,128]{1,0:T(8,128)S(1)}, u32[]{:S(2)}, u32[]{:S(2)}) %collective-permute-start.2) | collective-permute-done | bytes 16416 | tf_op jit(solution)/shard_map/ppermute | solution.py:26
  14.0 2.9 %all-to-all-start = ((bf16[32,32,1024]{2,1,0:T(8,128)(2,1)}), bf16[32,32,1024]{2,1,0:T(8,128)(2,1)S(1)}, u32[]{:S(2)}, u32[]{:S(2)}) async-start(bf16[32,32,1024]{2,1,0:T(8,128)(2,1)} %bitcast.24), calls=%async_computation | async-start | bytes 4194304 | tf_op jit(solution)/shard_map/all_to_all | solution.py:448
  16.9 0.1 pad.16.clone
  17.1 1.7 %collective-permute-start.3 = (f32[32,128]{1,0:T(8,128)S(1)}, f32[32,128]{1,0:T(8,128)S(1)}, u32[]{:S(2)}, u32[]{:S(2)}) collective-permute-start(f32[32,128]{1,0:T(8,128)S(1)} %add_add_fusion), channel_id=1, source_target_pairs={{0,4},{4,0},{8,12},{12,8},{16,20},{20,16},{24,28},{28,24},{1,5},{5... | collective-permute-start | bytes 49160 | tf_op jit(solution)/shard_map/ppermute | solution.py:26
  18.9 8.2 %collective-permute-done.3 = f32[32,128]{1,0:T(8,128)S(1)} collective-permute-done((f32[32,128]{1,0:T(8,128)S(1)}, f32[32,128]{1,0:T(8,128)S(1)}, u32[]{:S(2)}, u32[]{:S(2)}) %collective-permute-start.3) | collective-permute-done | bytes 16416 | tf_op jit(solution)/shard_map/ppermute | solution.py:26
  27.1 4.6 %collective-permute-start.4 = (f32[32,128]{1,0:T(8,128)S(1)}, f32[32,128]{1,0:T(8,128)S(1)}, u32[]{:S(2)}, u32[]{:S(2)}) collective-permute-start(f32[32,128]{1,0:T(8,128)S(1)} %add.69), channel_id=1, source_target_pairs={{0,2},{1,3},{2,0},{3,1},{4,6},{5,7},{6,4},{7,5},{8,10},{9,11},{10,... | collective-permute-start | bytes 49160 | tf_op jit(solution)/shard_map/ppermute | solution.py:26
  31.7 0.1 multiply_reduce_fusion.1
  31.8 1.7 %collective-permute-done.4 = f32[32,128]{1,0:T(8,128)S(1)} collective-permute-done((f32[32,128]{1,0:T(8,128)S(1)}, f32[32,128]{1,0:T(8,128)S(1)}, u32[]{:S(2)}, u32[]{:S(2)}) %collective-permute-start.4) | collective-permute-done | bytes 16416 | tf_op jit(solution)/shard_map/ppermute | solution.py:26
  33.5 0.6 pad_add_fusion.pair_ref.place_ref
  34.2 0.5 collective-permute-done.5
  34.7 0.6 add.71.words_ref.table_ref
  35.3 27.0 %shard_map.77 = (bf16[32,2,128,640]{3,2,1,0:T(8,128)(2,1)}, f32[32,4,8,256]{3,2,1,0:T(8,128)}, f32[32,3,8,128]{3,2,1,0:T(8,128)}) custom-call(s32[3]{0:T(128)} %pad_add_fusion.pair_ref.place_ref, f32[32,128]{1,0:T(8,128)} %add.71.words_ref.table_ref, f32[32,128]{1,0:T(8,128)} %add.71.words_ref.table_ref), custom_call_target="tpu_custom_call" | custom-call | tf_op jit(solution)/shard_map/pallas_call | solution.py:179
  62.3 1.0 %slice.6 = f32[32,3,3,3]{3,2,1,0:T(4,128)S(1)} slice(f32[32,3,8,128]{3,2,1,0:T(8,128)} %get-tuple-element.14), slice={[0:32], [0:3], [0:3], [0:3]} | slice | bytes 6912 | tf_op jit(solution)/shard_map/slice | solution.py:456
  63.4 0.1 copy.11
  63.5 0.1 multiply_reduce_fusion
  63.7 0.1 copy.15
  63.8 0.7 pad.10.extra_ref
  64.5 1.2 %all-to-all-done.height_hbm = bf16[32,32,1024]{2,1,0:T(8,128)(2,1)S(1)} async-done(((bf16[32,32,1024]{2,1,0:T(8,128)(2,1)}), bf16[32,32,1024]{2,1,0:T(8,128)(2,1)S(1)}, u32[]{:S(2)}, u32[]{:S(2)}) %all-to-all-start) | async-done | bytes 2097184 | tf_op jit(solution)/shard_map/all_to_all | solution.py:448
  65.7 1.3 %copy-done = bf16[32,32,1024]{2,1,0:T(8,128)(2,1)} copy-done((bf16[32,32,1024]{2,1,0:T(8,128)(2,1)}, bf16[32,32,1024]{2,1,0:T(8,128)(2,1)S(1)}, u32[]{:S(2)}) %copy-start) | copy-done | bytes 2097176
  67.1 17.5 %shard_map.78 = (f32[32,1024]{1,0:T(8,128)}, f32[32,8,128]{2,1,0:T(8,128)}) custom-call(s32[3]{0:T(128)} %pad_add_fusion.pair_ref.place_ref, f32[32,128]{1,0:T(8,128)} %add.71.words_ref.table_ref, bf16[32,32,1024]{2,1,0:T(8,128)(2,1)} %copy-done, bf16[32,2,128,640]{3,2,1,0:T(8,128)(2,1)} %get-tuple-element.13.band_hbm, f32[32,1024]{1,0:T(8,128)} %ref_ref.1, ...), custom_call_target="tpu_custom_call" | custom-call | tf_op jit(solution)/shard_map/pallas_call | solution.py:330
  84.5 6.0 %all-to-all-start.1 = ((f32[32,8,128]{2,1,0:T(8,128)}), f32[32,8,128]{2,1,0:T(8,128)S(1)}, u32[]{:S(2)}, u32[]{:S(2)}) async-start(f32[32,8,128]{2,1,0:T(8,128)} %get-tuple-element.15), calls=%async_computation.1 | async-start | bytes 262144 | tf_op jit(solution)/shard_map/all_to_all | solution.py:462
  90.6 0.1 slice_bitcast_fusion
  90.7 0.1 copy.16
  90.8 0.9 reshape.41.effect_ref
  91.7 7.1 %all-to-all-done.1.got_ref = f32[32,8,128]{2,1,0:T(8,128)S(1)} async-done(((f32[32,8,128]{2,1,0:T(8,128)}), f32[32,8,128]{2,1,0:T(8,128)S(1)}, u32[]{:S(2)}, u32[]{:S(2)}) %all-to-all-start.1) | async-done | bytes 131104 | tf_op jit(solution)/shard_map/all_to_all | solution.py:462
  98.8 0.6 copy-done.1
  99.5 2.2 %shard_map.79 = (f32[32,1024]{1,0:T(8,128)}, f32[1,4]{1,0:T(1,128)}) custom-call(s32[3]{0:T(128)} %pad_add_fusion.pair_ref.place_ref, f32[32,8,128]{2,1,0:T(8,128)} %copy-done.1, f32[32,1024]{1,0:T(8,128)} %get-tuple-element.16.map_ref, f32[3,32,1024]{2,1,0:T(8,128)} %reshape.41.effect_ref, f32[1,4]{1,0:T(1,128)} %bitcast.29), custom_call_target="tpu_custom_call" | custom-call | tf_op jit(solution)/shard_map/pallas_call | solution.py:397
  (24 shorter events, 0.4 us)
Async XLA Ops:
  2.8 5.6 %collective-permute-start = (f32[32,128]{1,0:T(8,128)S(1)}, f32[32,128]{1,0:T(8,128)S(1)}, u32[]{:S(2)}, u32[]{:S(2)}) collective-permute-start(f32[32,128]{1,0:T(8,128)S(1)} %broadcast_select_fusion), channel_id=1, source_target_pairs={{0,8},{4,12},{8,0},{12,4},{16,24},{20,28},{24,16},{28,20},{1,9},{5... | collective-permute-start | bytes 49160 | tf_op jit(solution)/shard_map/ppermute | solution.py:26
  5.8 4.7 %collective-permute-start.1 = (f32[32,128]{1,0:T(8,128)S(1)}, f32[32,128]{1,0:T(8,128)S(1)}, u32[]{:S(2)}, u32[]{:S(2)}) collective-permute-start(f32[32,128]{1,0:T(8,128)S(1)} %broadcast_select_fusion), channel_id=1, source_target_pairs={{0,16},{4,20},{8,24},{12,28},{16,0},{20,4},{24,8},{28,12},{1,17},{... | collective-permute-start | bytes 49160 | tf_op jit(solution)/shard_map/ppermute | solution.py:26
  8.4 5.5 %collective-permute-start.2 = (f32[32,128]{1,0:T(8,128)S(1)}, f32[32,128]{1,0:T(8,128)S(1)}, u32[]{:S(2)}, u32[]{:S(2)}) collective-permute-start(f32[32,128]{1,0:T(8,128)S(1)} %broadcast_select_fusion), channel_id=1, source_target_pairs={{0,24},{4,28},{8,16},{12,20},{16,8},{20,12},{24,0},{28,4},{1,25},{... | collective-permute-start | bytes 49160 | tf_op jit(solution)/shard_map/ppermute | solution.py:26
  14.0 4.8 %copy-start.3 = (f32[1,3,32]{2,1,0:T(4,128)S(1)}, f32[1,3,32]{2,1,0:T(4,128)}, u32[]{:S(2)}) copy-start(f32[1,3,32]{2,1,0:T(4,128)} %constant.43.clone.1) | copy-start | bytes 1156
  14.0 4.8 %copy-start.4 = (f32[1,3,32]{2,1,0:T(4,128)S(1)}, f32[1,3,32]{2,1,0:T(4,128)}, u32[]{:S(2)}) copy-start(f32[1,3,32]{2,1,0:T(4,128)} %constant.44.clone.1) | copy-start | bytes 1156
  14.0 51.7 %all-to-all-start = ((bf16[32,32,1024]{2,1,0:T(8,128)(2,1)}), bf16[32,32,1024]{2,1,0:T(8,128)(2,1)S(1)}, u32[]{:S(2)}, u32[]{:S(2)}) async-start(bf16[32,32,1024]{2,1,0:T(8,128)(2,1)} %bitcast.24), calls=%async_computation | async-start | bytes 4194304 | tf_op jit(solution)/shard_map/all_to_all | solution.py:448
  17.1 9.9 %collective-permute-start.3 = (f32[32,128]{1,0:T(8,128)S(1)}, f32[32,128]{1,0:T(8,128)S(1)}, u32[]{:S(2)}, u32[]{:S(2)}) collective-permute-start(f32[32,128]{1,0:T(8,128)S(1)} %add_add_fusion), channel_id=1, source_target_pairs={{0,4},{4,0},{8,12},{12,8},{16,20},{20,16},{24,28},{28,24},{1,5},{5... | collective-permute-start | bytes 49160 | tf_op jit(solution)/shard_map/ppermute | solution.py:26
  27.1 6.4 %collective-permute-start.4 = (f32[32,128]{1,0:T(8,128)S(1)}, f32[32,128]{1,0:T(8,128)S(1)}, u32[]{:S(2)}, u32[]{:S(2)}) collective-permute-start(f32[32,128]{1,0:T(8,128)S(1)} %add.69), channel_id=1, source_target_pairs={{0,2},{1,3},{2,0},{3,1},{4,6},{5,7},{6,4},{7,5},{8,10},{9,11},{10,... | collective-permute-start | bytes 49160 | tf_op jit(solution)/shard_map/ppermute | solution.py:26
  33.5 1.2 %collective-permute-start.5 = (f32[32,128]{1,0:T(8,128)S(1)}, f32[32,128]{1,0:T(8,128)S(1)}, u32[]{:S(2)}, u32[]{:S(2)}) collective-permute-start(f32[32,128]{1,0:T(8,128)S(1)} %add.70), channel_id=1, source_target_pairs={{0,1},{1,0},{2,3},{3,2},{4,5},{5,4},{6,7},{7,6},{8,9},{9,8},{10,11... | collective-permute-start | bytes 49160 | tf_op jit(solution)/shard_map/ppermute | solution.py:26
  65.7 1.3 %copy-start = (bf16[32,32,1024]{2,1,0:T(8,128)(2,1)}, bf16[32,32,1024]{2,1,0:T(8,128)(2,1)S(1)}, u32[]{:S(2)}) copy-start(bf16[32,32,1024]{2,1,0:T(8,128)(2,1)S(1)} %all-to-all-done.height_hbm) | copy-start | bytes 6291460
  67.0 23.5 %copy-start.2 = (f32[32,4,8,256]{3,2,1,0:T(8,128)S(1)}, f32[32,4,8,256]{3,2,1,0:T(8,128)}, u32[]{:S(2)}) copy-start(f32[32,4,8,256]{3,2,1,0:T(8,128)} %get-tuple-element.17) | copy-start | bytes 3145732
  84.5 14.3 %all-to-all-start.1 = ((f32[32,8,128]{2,1,0:T(8,128)}), f32[32,8,128]{2,1,0:T(8,128)S(1)}, u32[]{:S(2)}, u32[]{:S(2)}) async-start(f32[32,8,128]{2,1,0:T(8,128)} %get-tuple-element.15), calls=%async_computation.1 | async-start | bytes 262144 | tf_op jit(solution)/shard_map/all_to_all | solution.py:462
  98.8 0.6 copy-start.1

commit v4 on v3

--- a/solution.py
+++ b/solution.py
@@ -15,9 +15,10 @@
 REACH = 2
 BAND = (2 * REACH + 1) * LANE
 SPAN = 512
-GROUP = 4
+GROUP = 16
 HALF_LANE = 64
-VMEM_MAIN = 56 * 1024 * 1024
+VMEM_LARGE = 56 * 1024 * 1024
+VMEM_SMALL = 48 * 1024 * 1024
 EXACT = lax.Precision.HIGHEST
 
 
@@ -27,7 +28,11 @@
 
 
 def gather_far(value):
-    return value + exchange(value, "azim", range(2, lax.axis_size("azim"), 2))
+    step = 2
+    while step < lax.axis_size("azim"):
+        value = value + exchange(value, "azim", [step])
+        step *= 2
+    return value
 
 
 def gather_near(value):
@@ -84,6 +89,14 @@
     before = jnp.where(s >= stride, s - stride, s - stride + tiles)
     after = jnp.where(s + stride < tiles, s + stride, s + stride - tiles)
     return before, after
+
+
+def small(tiles):
+    return tiles <= HALF_LANE
+
+
+def vmem_params(tiles):
+    return pltpu.CompilerParams(vmem_limit_bytes=VMEM_SMALL if small(tiles) else VMEM_LARGE)
 
 
 def axis_terms(shape, dim, total, first=0):
@@ -126,7 +139,7 @@
         seen_ref[s] = jnp.sum(out.reshape(blocks, 2, 8, WIDE), axis=1)
         return carry
 
-    lax.fori_loop(0, tiles, build, 0)
+    lax.fori_loop(0, tiles, build, 0, unroll=4)
     column = lax.broadcasted_iota(jnp.int32, (2, 8, WIDE), 2) + WIDE * lax.broadcasted_iota(
         jnp.int32, (2, 8, WIDE), 0
     )
@@ -168,7 +181,7 @@
             )
         return carry
 
-    lax.fori_loop(0, tiles, respond, 0)
+    lax.fori_loop(0, tiles, respond, 0, unroll=4)
 
 
 def prepare(pair, table, cols, stride, pair_count):
@@ -190,32 +203,27 @@
             pltpu.VMEM((tiles, blocks, 8, WIDE), jnp.float32),
             pltpu.VMEM((16 * blocks, 3 * WIDE), jnp.bfloat16),
         ],
-        compiler_params=pltpu.CompilerParams(vmem_limit_bytes=VMEM_MAIN),
+        compiler_params=vmem_params(tiles),
     )(pair, table, table)
 
 
-def passes_kernel(
-    tiles, row_total, stride, pair_count, scale, place_ref, words_ref, height_hbm, band_hbm, ref_ref, extra_ref,
-    map_ref, message_ref, height_ref, band_ref, resampled_ref, total_ref, ref_low_ref, sums_ref, sems
+def band_copies(band_hbm, band_ref, sems, g, way):
+    part = pl.ds(g * GROUP, GROUP)
+    return pltpu.make_async_copy(band_hbm.at[part, way], band_ref.at[part, way], sems.at[way, g])
+
+
+def one_pass(
+    tiles, stride, pair_count, scale, first_row, pair, row_total,
+    words_ref, height_ref, band_hbm, ref_ref, map_ref, band_ref, resampled_ref, total_ref, ref_low_ref, sems, keep
 ):
     rows, cols = ref_ref.shape
     blocks = cols // WIDE
     groups = tiles // GROUP
-    pair = place_ref[0]
-
-    def copies(g):
-        part = pl.ds(g * GROUP, GROUP)
-        return (
-            pltpu.make_async_copy(height_hbm.at[part], height_ref.at[part], sems.at[0, g]),
-            pltpu.make_async_copy(band_hbm.at[part], band_ref.at[part], sems.at[1, g]),
-        )
-
-    for g in range(groups):
-        for copy in copies(g):
-            copy.start()
+    for way in range(2):
+        for g in range(groups):
+            band_copies(band_hbm, band_ref, sems, g, way).start()
 
     az = axis_terms((1, cols), 1, cols)
-    first_row = place_ref[1].astype(jnp.float32)
     ax = axis_terms((rows, LANE), 0, row_total, first_row)
     ax_wide = axis_terms((rows, WIDE), 0, row_total, first_row).reshape(rows // 8, 8, WIDE)
     column = lax.broadcasted_iota(jnp.int32, (2 * rows, WIDE), 1) + jnp.where(
@@ -246,8 +254,9 @@
     def backward(s):
         before, after = neighbours(s, tiles, stride)
         upstream = jnp.concatenate([-seam(before, s), seam(s, after)], axis=0).astype(jnp.bfloat16)
-        pulled = mixed(upstream, rows, band_ref, s, 1)
-        total_ref[...] += pulled
+        return mixed(upstream, rows, band_ref, s, 1)
+
+    def term_sums(pulled):
         plain, tilted, bent = [], [], []
         for k in range(blocks):
             block = pulled[k * rows : (k + 1) * rows].reshape(rows // 8, 8, WIDE)
@@ -263,89 +272,115 @@
         folded = [sum(v[:, k : k + LANE] for k in range(0, cols, LANE)) for v in sums]
         return [jnp.sum(v, axis=0, keepdims=True) for v in folded]
 
-    def add_map(source_ref):
-        for k in range(blocks):
-            part = slice(k * WIDE, (k + 1) * WIDE)
-            map_ref[:, part] = source_ref[:, part] + total_ref[k * rows : (k + 1) * rows, :] / scale
-
-    def first_forward(g, carry):
-        for copy in copies(g):
-            copy.wait()
+    def all_forward(g, carry):
+        band_copies(band_hbm, band_ref, sems, g, 0).wait()
         for k in range(GROUP):
             forward(g * GROUP + k)
         return carry
 
-    def first_backward(g, carry):
+    def all_backward(g, carry):
+        band_copies(band_hbm, band_ref, sems, g, 1).wait()
         for k in range(GROUP):
             s = g * GROUP + k
-            for term, value in enumerate(backward(s)):
-                sums_ref[term, pl.ds(s, 1), :] = value
+            pulled = backward(s)
+            total_ref[...] += pulled
+            if keep is not None:
+                for term, value in enumerate(term_sums(pulled)):
+                    keep[term, pl.ds(s, 1), :] = value
         return carry
 
     ref_low_ref[...] = ref_ref[...].astype(jnp.bfloat16).astype(jnp.float32)
-    lax.fori_loop(0, groups, first_forward, 0)
+    lax.fori_loop(0, groups, all_forward, 0)
     total_ref[...] = jnp.zeros_like(total_ref)
-    lax.fori_loop(0, groups, first_backward, 0)
-    add_map(ref_ref)
+    lax.fori_loop(0, groups, all_backward, 0)
+    for k in range(blocks):
+        part = slice(k * WIDE, (k + 1) * WIDE)
+        map_ref[:, part] = ref_ref[:, part] + total_ref[k * rows : (k + 1) * rows, :] / scale
+    return ax_wide
+
+
+def first_kernel(
+    tiles, row_total, stride, pair_count, scale,
+    place_ref, words_ref, height_ref, band_hbm, ref_ref, effect_ref, extra_ref, map_ref, message_ref,
+    band_ref, resampled_ref, total_ref, ref_low_ref, sums_ref, sems
+):
+    rows, cols = ref_ref.shape
+    ax_wide = one_pass(
+        tiles, stride, pair_count, scale, place_ref[1].astype(jnp.float32), place_ref[0], row_total,
+        words_ref, height_ref, band_hbm, ref_ref, map_ref, band_ref, resampled_ref, total_ref, ref_low_ref, sems, sums_ref
+    )
+
+    def lanes_dot(left, right):
+        return lax.dot_general(
+            left, right, (((1,), (1,)), ((), ())), precision=EXACT, preferred_element_type=jnp.float32
+        )
 
     ones = jnp.ones((8, LANE), jnp.float32)
-    turned = []
-    for term in range(4):
-        line = lax.dot_general(
-            ones, sums_ref[term], (((1,), (1,)), ((), ())),
-            precision=EXACT, preferred_element_type=jnp.float32,
-        )[0:1]
-        if tiles < LANE:
-            line = jnp.concatenate([line, jnp.zeros((1, LANE - tiles), jnp.float32)], axis=1)
-        turned.append(line)
-    turned = jnp.concatenate(turned, axis=0)
-    low_lanes = lax.broadcasted_iota(jnp.int32, (4, LANE), 1) < HALF_LANE
-
-    def second_forward(g, carry):
-        for k in range(GROUP):
-            forward(g * GROUP + k)
-        return carry
-
-    def second_backward(g, carry):
-        for k in range(GROUP):
-            s = g * GROUP + k
-            value = jnp.concatenate(backward(s), axis=0)
-            value = value + pltpu.roll(value, HALF_LANE, 1)
-            value = jnp.where(low_lanes, value, extra_ref[s])
-            message_ref[s] = jnp.concatenate([turned, value], axis=0)
-        return carry
-
-    ref_low_ref[...] = map_ref[...].astype(jnp.bfloat16).astype(jnp.float32)
-    lax.fori_loop(0, groups, second_forward, 0)
-    total_ref[...] = jnp.zeros_like(total_ref)
-    lax.fori_loop(0, groups, second_backward, 0)
-    add_map(map_ref)
-
-
-def passes(place, table, heights, bands, ref_rows, extra, row_total, stride, pair_count):
+    now = jnp.concatenate([lanes_dot(ones, sums_ref[term])[0:1] for term in range(4)], axis=0)
+
+    moments = [[], [], []]
+    for k in range(cols // WIDE):
+        block = total_ref[k * rows : (k + 1) * rows, :].reshape(rows // 8, 8, WIDE)
+        for power in range(3):
+            moments[power].append(jnp.sum(jnp.sum(block, axis=0), axis=0, keepdims=True))
+            block = block * ax_wide
+    moments = [jnp.concatenate(m, axis=1) for m in moments]
+    moments = jnp.concatenate(moments + [jnp.zeros((5, cols), jnp.float32)], axis=0)
+    level, lean, bend = [lanes_dot(moments, effect_ref[term]) for term in range(3)]
+    change = jnp.concatenate(
+        [level[0:1], lean[0:1], level[1:2], bend[0:1] + level[2:3] - level[0:1] * (2.0 / 3.0)], axis=0
+    )
+    later = now - change / scale
+    if small(tiles):
+        gap = jnp.zeros((4, HALF_LANE - tiles), jnp.float32)
+        shared = jnp.concatenate([now, gap, later, gap], axis=1)
+    else:
+        shared = jnp.concatenate([now, later], axis=0)
+    for s in range(tiles):
+        message_ref[s] = jnp.concatenate([shared, extra_ref[s]], axis=0)
+
+
+def second_kernel(
+    tiles, row_total, stride, pair_count, scale,
+    place_ref, words_ref, height_ref, band_hbm, ref_ref, map_ref,
+    band_ref, resampled_ref, total_ref, ref_low_ref, sems
+):
+    one_pass(
+        tiles, stride, pair_count, scale, place_ref[1].astype(jnp.float32), place_ref[0], row_total,
+        words_ref, height_ref, band_hbm, ref_ref, map_ref, band_ref, resampled_ref, total_ref, ref_low_ref, sems, None
+    )
+
+
+def in_vmem(value, tiles):
+    return pltpu.with_memory_space_constraint(value, pltpu.VMEM) if small(tiles) else value
+
+
+def run_pass(place, table, heights, bands, ref_rows, more, row_total, stride, pair_count):
     tiles, rows, cols = heights.shape
     vmem = pl.BlockSpec(memory_space=pltpu.VMEM)
     smem = pl.BlockSpec(memory_space=pltpu.SMEM)
-    anywhere = pl.BlockSpec(memory_space=pl.ANY)
+    anywhere = pl.BlockSpec(memory_space=pltpu.HBM)
+    out_shape = [jax.ShapeDtypeStruct((rows, cols), jnp.float32)]
+    scratch = [
+        pltpu.VMEM((tiles, 2, LANE, BAND), jnp.bfloat16),
+        pltpu.VMEM((tiles, 4 * rows, WIDE), jnp.bfloat16),
+        pltpu.VMEM((4 * rows, WIDE), jnp.float32),
+        pltpu.VMEM((rows, cols), jnp.float32),
+    ]
+    if more:
+        lines = 8 if small(tiles) else 12
+        out_shape.append(jax.ShapeDtypeStruct((tiles, lines, LANE), jnp.float32))
+        scratch.append(pltpu.VMEM((4, tiles, LANE), jnp.float32))
+    scratch.append(pltpu.SemaphoreType.DMA((2, tiles // GROUP)))
+    body = first_kernel if more else second_kernel
     return pl.pallas_call(
-        functools.partial(passes_kernel, tiles, row_total, stride, pair_count, math.sqrt(tiles)),
-        out_shape=(
-            jax.ShapeDtypeStruct((rows, cols), jnp.float32),
-            jax.ShapeDtypeStruct((tiles, 8, LANE), jnp.float32),
-        ),
-        in_specs=[smem, smem, anywhere, anywhere, vmem, vmem],
-        out_specs=(vmem, vmem),
-        scratch_shapes=[
-            pltpu.VMEM((tiles, rows, cols), jnp.bfloat16),
-            pltpu.VMEM((tiles, 2, LANE, BAND), jnp.bfloat16),
-            pltpu.VMEM((tiles, 4 * rows, WIDE), jnp.bfloat16),
-            pltpu.VMEM((4 * rows, WIDE), jnp.float32),
-            pltpu.VMEM((rows, cols), jnp.float32),
-            pltpu.VMEM((4, tiles, LANE), jnp.float32),
-            pltpu.SemaphoreType.DMA((2, tiles // GROUP)),
-        ],
-        compiler_params=pltpu.CompilerParams(vmem_limit_bytes=VMEM_MAIN),
-    )(place, table, heights, bands, ref_rows, extra)
+        functools.partial(body, tiles, row_total, stride, pair_count, math.sqrt(tiles)),
+        out_shape=out_shape,
+        in_specs=[smem, smem, vmem, anywhere, vmem] + [vmem] * len(more),
+        out_specs=[vmem] * len(out_shape),
+        scratch_shapes=scratch,
+        compiler_params=vmem_params(tiles),
+    )(place, table, heights, bands, ref_rows, *more)
 
 
 def finish_kernel(
@@ -353,7 +388,12 @@
 ):
     total = jnp.sum(got_ref[...], axis=0)
     step = total[0:4] / pixels
-    later = total[4:8]
+    if small(tiles):
+        later = pltpu.roll(total[0:4], HALF_LANE, 1)
+        links = total[4:8]
+    else:
+        later = total[4:8]
+        links = total[8:12]
     lines = lax.broadcasted_iota(jnp.int32, (8, LANE), 0)
     wide = [jnp.broadcast_to(step[k : k + 1], (8, LANE))[:, :tiles] for k in range(4)]
     lines = lines[:, :tiles]
@@ -375,16 +415,17 @@
     me = place_ref[2]
     before, after = neighbours(me, tiles, stride)
     lane = lax.broadcasted_iota(jnp.int32, (4, LANE), 1)
+
+    def pick(value, target):
+        return jnp.sum(jnp.where(lane == target, value, 0.0), axis=1, keepdims=True)
+
     reach = jnp.zeros((4, 1), jnp.float32)
-    own = None
     for source, target in enumerate((me, before, after)):
-        at = jnp.sum(jnp.where(lane == target, step, 0.0), axis=1, keepdims=True)
-        own = at if source == 0 else own
+        at = pick(step, target)
         for k in range(4):
-            place = HALF_LANE + 4 * source + k
-            reach = reach + at[k : k + 1] * later[:, place : place + 1]
-    fresh = jnp.sum(jnp.where(lane < HALF_LANE, later, 0.0), axis=1, keepdims=True)
-    gain = own + (fresh - reach) / pixels
+            place = 4 * source + k
+            reach = reach + at[k : k + 1] * links[:, place : place + 1]
+    gain = pick(step, me) + (pick(later, me) - reach) / pixels
     line = lax.broadcasted_iota(jnp.int32, (4, LANE), 0)
     gain = jnp.sum(jnp.where(line == lane, gain, 0.0), axis=0, keepdims=True)
     out_coef_ref[...] = coef_ref[...] + gain[:, :4]
@@ -404,6 +445,7 @@
         ),
         in_specs=[smem] + [vmem] * 4,
         out_specs=(vmem, vmem),
+        compiler_params=vmem_params(tiles),
     )(place, got, map_rows, effects, coefs)
 
 
@@ -454,15 +496,15 @@
     bands, effects, moments = prepare(place, table, cols, stride, pair_count)
     effects = effects[:, :, :3].transpose(2, 0, 1, 3).reshape(3, tiles, cols)
     extra = response_sums(moments[:, :, :3, :3], ax)
-    extra = jnp.pad(extra, ((0, 0), (0, 0), (HALF_LANE, LANE - HALF_LANE - 12)))
-
-    map_rows, message = passes(
-        place, table, heights, bands, ref_map, extra, row_total, stride, pair_count
-    )
-    got = lax.all_to_all(message, AXES, 0, 0, tiled=True)
-    new_map, new_coefs = finish(
-        place, got, map_rows, effects, coefs[0], row_total, stride
-    )
+    extra = jnp.pad(extra, ((0, 0), (0, 0), (0, LANE - 12)))
+
+    heights = in_vmem(heights, tiles)
+    map_rows, message = run_pass(
+        place, table, heights, bands, ref_map, (effects, extra), row_total, stride, pair_count
+    )
+    got = in_vmem(lax.all_to_all(message, AXES, 0, 0, tiled=True), tiles)
+    (map_rows,) = run_pass(place, table, heights, bands, map_rows, (), row_total, stride, pair_count)
+    new_map, new_coefs = finish(place, got, map_rows, effects, coefs[0], row_total, stride)
     return (new_map, new_coefs[None])
 
 

time: 102 us -> 90.3 us (0.89)
  Pallas kernels: 46.7 us -> 32.6 us
  waiting for transfers between devices: 24.3 us -> 30.4 us
  local copies, waits for them, and re-layouts: 5.27 us -> 0.86 us
  starting transfers between devices: 20.8 us -> 22.7 us
  other arithmetic: 3.17 us -> 2.08 us
    all_to_all x1, waiting for transfers between devices: 1.23 us -> 14.4 us  [local(): lax.all_to_all(own_heights[0, 0].reshape(tiles, rows, cols), AXES, 0, 0,...]
    pallas_call x1, Pallas kernels: 27 us -> 15.7 us  [prepare(): pl.pallas_call(functools.partial(prepare_kernel, tiles, cols, stride, pai...]
    all_to_all x1, waiting for transfers between devices: 7.07 us -> 1.58 us  [local(): got = in_vmem(lax.all_to_all(message, AXES, 0, 0, tiled=True), tiles)]
    all_to_all x1, starting transfers between devices: 2.86 us -> 6.24 us  [local(): lax.all_to_all(own_heights[0, 0].reshape(tiles, rows, cols), AXES, 0, 0,...]
    pallas_call x1 -> x2, Pallas kernels: 17.5 us -> 15.3 us  [run_pass(): pl.pallas_call(functools.partial(body, tiles, row_total, stride, pair_cou...]
    all_to_all x1, starting transfers between devices: 6.04 us -> 4.01 us  [local(): got = in_vmem(lax.all_to_all(message, AXES, 0, 0, tiled=True), tiles)]
    unnamed x10 -> x8, local copies, waits for them, and re-layouts: 1.98 us -> 0.02 us
    ppermute x6 -> x5, waiting for transfers between devices: 16 us -> 14.4 us  [exchange(): lax.ppermute(value, axis, [(i, i ^ k) for i in range(size)])]
  transfers between devices with their start and end apart: 8 -> 7, of which waited for: 7 -> 7; matrix products, arithmetic and copies ran while one was open for 5% -> 1% of each run, Pallas kernels for 27% -> 25%
where the time goes in v4:
time: 90.3 us; the launch traced here: 90.1 us
  Pallas kernels  32.6 us (36%)
  waiting for transfers between devices  30.4 us (34%)
  starting transfers between devices  22.7 us (25%)
  other arithmetic  2.08 us (2%)
  between operations  1.44 us (2%)
    pallas_call x1, Pallas kernels, prepare(): pl.pallas_call(functools.partial(prepare_kernel, tiles, cols, stride, pai...  15.7 us
    pallas_call x2, Pallas kernels, run_pass(): pl.pallas_call(functools.partial(body, tiles, row_total, stride, pair_cou...  15.3 us
    all_to_all x1, waiting for transfers between devices, local(): lax.all_to_all(own_heights[0, 0].reshape(tiles, rows, cols), AXES, 0, 0,...  14.4 us
    ppermute x5, waiting for transfers between devices, exchange(): lax.ppermute(value, axis, [(i, i ^ k) for i in range(size)])  14.4 us
    ppermute x5, starting transfers between devices, exchange(): lax.ppermute(value, axis, [(i, i ^ k) for i in range(size)])  12.4 us
    all_to_all x1, starting transfers between devices, local(): lax.all_to_all(own_heights[0, 0].reshape(tiles, rows, cols), AXES, 0, 0,...  6.24 us
    all_to_all x1, starting transfers between devices, local(): got = in_vmem(lax.all_to_all(message, AXES, 0, 0, tiled=True), tiles)  4.01 us
  transfers between devices with their start and end apart: 7, of which 7 were waited for; matrix products, arithmetic and copies ran while one was open for 1% of the time, Pallas kernels for 25%

profile of v4, /device:TPU:0, one launch (start us, length us, event | category | flops | bytes accessed | tf_op | source)
XLA Modules:
  0.0 90.1 jit_solution(8451694862525380136)
XLA Ops:
  1.3 0.7 convert_bitcast_fusion
  2.0 0.7 select_maximum_fusion
  2.7 0.1 broadcast_select_fusion
  2.8 3.0 %collective-permute-start = (f32[32,128]{1,0:T(8,128)S(1)}, f32[32,128]{1,0:T(8,128)S(1)}, u32[]{:S(2)}, u32[]{:S(2)}) collective-permute-start(f32[32,128]{1,0:T(8,128)S(1)} %broadcast_select_fusion), channel_id=1, source_target_pairs={{0,8},{4,12},{8,0},{12,4},{16,24},{20,28},{24,16},{28,20},{1,9},{5... | collective-permute-start | bytes 49160 | tf_op jit(solution)/shard_map/ppermute | solution.py:27
  5.8 1.7 %collective-permute-done = f32[32,128]{1,0:T(8,128)S(1)} collective-permute-done((f32[32,128]{1,0:T(8,128)S(1)}, f32[32,128]{1,0:T(8,128)S(1)}, u32[]{:S(2)}, u32[]{:S(2)}) %collective-permute-start) | collective-permute-done | bytes 16416 | tf_op jit(solution)/shard_map/ppermute | solution.py:27
  7.5 0.1 fusion
  7.6 3.0 %collective-permute-start.1 = (f32[32,128]{1,0:T(8,128)S(1)}, f32[32,128]{1,0:T(8,128)S(1)}, u32[]{:S(2)}, u32[]{:S(2)}) collective-permute-start(f32[32,128]{1,0:T(8,128)S(1)} %fusion), channel_id=1, source_target_pairs={{0,16},{4,20},{8,24},{12,28},{16,0},{20,4},{24,8},{28,12},{1,17},{... | collective-permute-start | bytes 49160 | tf_op jit(solution)/shard_map/ppermute | solution.py:27
  10.6 1.7 %collective-permute-done.1 = f32[32,128]{1,0:T(8,128)S(1)} collective-permute-done((f32[32,128]{1,0:T(8,128)S(1)}, f32[32,128]{1,0:T(8,128)S(1)}, u32[]{:S(2)}, u32[]{:S(2)}) %collective-permute-start.1) | collective-permute-done | bytes 16416 | tf_op jit(solution)/shard_map/ppermute | solution.py:27
  12.4 0.1 fusion.1
  12.4 6.2 %all-to-all-start = ((bf16[32,32,1024]{2,1,0:T(8,128)(2,1)}), bf16[32,32,1024]{2,1,0:T(8,128)(2,1)S(1)}, u32[]{:S(2)}, u32[]{:S(2)}) async-start(bf16[32,32,1024]{2,1,0:T(8,128)(2,1)} %bitcast.26), calls=%async_computation | async-start | bytes 4194304 | tf_op jit(solution)/shard_map/all_to_all | solution.py:490
  18.7 0.1 pad.16.clone
  18.8 0.1 pad.17.clone
  18.9 1.8 %collective-permute-start.2 = (f32[32,128]{1,0:T(8,128)S(1)}, f32[32,128]{1,0:T(8,128)S(1)}, u32[]{:S(2)}, u32[]{:S(2)}) collective-permute-start(f32[32,128]{1,0:T(8,128)S(1)} %fusion.1), channel_id=1, source_target_pairs={{0,4},{4,0},{8,12},{12,8},{16,20},{20,16},{24,28},{28,24},{1,5},{5... | collective-permute-start | bytes 49160 | tf_op jit(solution)/shard_map/ppermute | solution.py:27
  20.7 8.2 %collective-permute-done.2 = f32[32,128]{1,0:T(8,128)S(1)} collective-permute-done((f32[32,128]{1,0:T(8,128)S(1)}, f32[32,128]{1,0:T(8,128)S(1)}, u32[]{:S(2)}, u32[]{:S(2)}) %collective-permute-start.2) | collective-permute-done | bytes 16416 | tf_op jit(solution)/shard_map/ppermute | solution.py:27
  28.9 4.6 %collective-permute-start.3 = (f32[32,128]{1,0:T(8,128)S(1)}, f32[32,128]{1,0:T(8,128)S(1)}, u32[]{:S(2)}, u32[]{:S(2)}) collective-permute-start(f32[32,128]{1,0:T(8,128)S(1)} %add.65), channel_id=1, source_target_pairs={{0,2},{1,3},{2,0},{3,1},{4,6},{5,7},{6,4},{7,5},{8,10},{9,11},{10,... | collective-permute-start | bytes 49160 | tf_op jit(solution)/shard_map/ppermute | solution.py:27
  33.5 0.1 multiply_reduce_fusion.1
  33.6 1.7 %collective-permute-done.3 = f32[32,128]{1,0:T(8,128)S(1)} collective-permute-done((f32[32,128]{1,0:T(8,128)S(1)}, f32[32,128]{1,0:T(8,128)S(1)}, u32[]{:S(2)}, u32[]{:S(2)}) %collective-permute-start.3) | collective-permute-done | bytes 16416 | tf_op jit(solution)/shard_map/ppermute | solution.py:27
  35.4 0.1 pad_add_fusion.pair_ref.place_ref
  35.5 1.1 %collective-permute-done.4 = f32[32,128]{1,0:T(8,128)S(1)} collective-permute-done((f32[32,128]{1,0:T(8,128)S(1)}, f32[32,128]{1,0:T(8,128)S(1)}, u32[]{:S(2)}, u32[]{:S(2)}) %collective-permute-start.4) | collective-permute-done | bytes 16416 | tf_op jit(solution)/shard_map/ppermute | solution.py:27
  36.5 15.7 %shard_map.77 = (bf16[32,2,128,640]{3,2,1,0:T(8,128)(2,1)}, f32[32,4,8,256]{3,2,1,0:T(8,128)S(1)}, f32[32,3,8,128]{3,2,1,0:T(8,128)S(1)}) custom-call(s32[3]{0:T(128)S(1)} %pad_add_fusion.pair_ref.place_ref, f32[32,128]{1,0:T(8,128)S(1)} %add.67.words_ref.table_ref, f32[32,128]{1,0:T(8,128)S(1)} %add.67.words_ref.table_ref), custom_call_target="tpu_custom_call" | custom-call | tf_op jit(solution)/shard_map/pallas_call | solution.py:192
  52.3 0.1 slice_bitcast_fusion
  52.4 0.1 copy.11
  52.5 0.2 reshape.40.effect_ref
  52.7 0.1 copy.12
  52.9 0.1 multiply_reduce_fusion
  53.0 0.1 copy.16
  53.2 14.4 %all-to-all-done.height_ref = bf16[32,32,1024]{2,1,0:T(8,128)(2,1)S(1)} async-done(((bf16[32,32,1024]{2,1,0:T(8,128)(2,1)}), bf16[32,32,1024]{2,1,0:T(8,128)(2,1)S(1)}, u32[]{:S(2)}, u32[]{:S(2)}) %all-to-all-start) | async-done | bytes 2097184 | tf_op jit(solution)/shard_map/all_to_all | solution.py:490
  67.6 8.7 %shard_map.78 = (f32[32,1024]{1,0:T(8,128)S(1)}, f32[32,8,128]{2,1,0:T(8,128)}) custom-call(s32[3]{0:T(128)S(1)} %pad_add_fusion.pair_ref.place_ref, f32[32,128]{1,0:T(8,128)S(1)} %add.67.words_ref.table_ref, bf16[32,32,1024]{2,1,0:T(8,128)(2,1)S(1)} %all-to-all-done.height_ref, bf16[32,2,128,640]{3,2,1,0:T(8,128)(2,1)} %get-tuple-element.13.band_hbm, ...), custom_call_target="tpu_custom_call" | custom-call | tf_op jit(solution)/shard_map/pallas_call | solution.py:376
  76.2 4.0 %all-to-all-start.1 = ((f32[32,8,128]{2,1,0:T(8,128)}), f32[32,8,128]{2,1,0:T(8,128)S(1)}, u32[]{:S(2)}, u32[]{:S(2)}) async-start(f32[32,8,128]{2,1,0:T(8,128)} %get-tuple-element.16), calls=%async_computation.1 | async-start | bytes 262144 | tf_op jit(solution)/shard_map/all_to_all | solution.py:505
  80.3 6.6 %shard_map.79.map_ref = f32[32,1024]{1,0:T(8,128)S(1)} custom-call(s32[3]{0:T(128)S(1)} %pad_add_fusion.pair_ref.place_ref, f32[32,128]{1,0:T(8,128)S(1)} %add.67.words_ref.table_ref, bf16[32,32,1024]{2,1,0:T(8,128)(2,1)S(1)} %all-to-all-done.height_ref, bf16[32,2,128,640]{3,2,1,0:T(8,128)(2,1)} %get-tuple-element.13.band_hbm, ...), custom_call_target="tpu_custom_call" | custom-call | tf_op jit(solution)/shard_map/pallas_call | solution.py:376
  86.9 1.6 %all-to-all-done.1.got_ref = f32[32,8,128]{2,1,0:T(8,128)S(1)} async-done(((f32[32,8,128]{2,1,0:T(8,128)}), f32[32,8,128]{2,1,0:T(8,128)S(1)}, u32[]{:S(2)}, u32[]{:S(2)}) %all-to-all-start.1) | async-done | bytes 131104 | tf_op jit(solution)/shard_map/all_to_all | solution.py:505
  88.5 1.6 %shard_map.80 = (f32[32,1024]{1,0:T(8,128)}, f32[1,4]{1,0:T(1,128)}) custom-call(s32[3]{0:T(128)S(1)} %pad_add_fusion.pair_ref.place_ref, f32[32,8,128]{2,1,0:T(8,128)S(1)} %all-to-all-done.1.got_ref, f32[32,1024]{1,0:T(8,128)S(1)} %shard_map.79.map_ref, f32[3,32,1024]{2,1,0:T(8,128)S(1)} %reshape.40.effect_ref, f32[1,4]{1,0:T(1,128)S(1)} %bitcast.25), custom_call_target="tpu_custom_call" | custom-call | tf_op jit(solution)/shard_map/pallas_call | solution.py:438
  (22 shorter events, 0.2 us)
Async XLA Ops:
  2.8 4.7 %collective-permute-start = (f32[32,128]{1,0:T(8,128)S(1)}, f32[32,128]{1,0:T(8,128)S(1)}, u32[]{:S(2)}, u32[]{:S(2)}) collective-permute-start(f32[32,128]{1,0:T(8,128)S(1)} %broadcast_select_fusion), channel_id=1, source_target_pairs={{0,8},{4,12},{8,0},{12,4},{16,24},{20,28},{24,16},{28,20},{1,9},{5... | collective-permute-start | bytes 49160 | tf_op jit(solution)/shard_map/ppermute | solution.py:27
  7.6 4.8 %collective-permute-start.1 = (f32[32,128]{1,0:T(8,128)S(1)}, f32[32,128]{1,0:T(8,128)S(1)}, u32[]{:S(2)}, u32[]{:S(2)}) collective-permute-start(f32[32,128]{1,0:T(8,128)S(1)} %fusion), channel_id=1, source_target_pairs={{0,16},{4,20},{8,24},{12,28},{16,0},{20,4},{24,8},{28,12},{1,17},{... | collective-permute-start | bytes 49160 | tf_op jit(solution)/shard_map/ppermute | solution.py:27
  12.4 8.3 %copy-start.2 = (f32[1,3,32]{2,1,0:T(4,128)S(1)}, f32[1,3,32]{2,1,0:T(4,128)}, u32[]{:S(2)}) copy-start(f32[1,3,32]{2,1,0:T(4,128)} %constant.43.clone.1) | copy-start | bytes 1156
  12.4 8.3 %copy-start.3 = (f32[1,3,32]{2,1,0:T(4,128)S(1)}, f32[1,3,32]{2,1,0:T(4,128)}, u32[]{:S(2)}) copy-start(f32[1,3,32]{2,1,0:T(4,128)} %constant.44.clone.1) | copy-start | bytes 1156
  12.4 55.1 %all-to-all-start = ((bf16[32,32,1024]{2,1,0:T(8,128)(2,1)}), bf16[32,32,1024]{2,1,0:T(8,128)(2,1)S(1)}, u32[]{:S(2)}, u32[]{:S(2)}) async-start(bf16[32,32,1024]{2,1,0:T(8,128)(2,1)} %bitcast.26), calls=%async_computation | async-start | bytes 4194304 | tf_op jit(solution)/shard_map/all_to_all | solution.py:490
  18.7 48.9 %copy-start = (f32[32,1024]{1,0:T(8,128)S(1)}, f32[32,1024]{1,0:T(8,128)}, u32[]{:S(2)}) copy-start(f32[32,1024]{1,0:T(8,128)} %ref_ref.1) | copy-start | bytes 393220
  18.9 10.0 %collective-permute-start.2 = (f32[32,128]{1,0:T(8,128)S(1)}, f32[32,128]{1,0:T(8,128)S(1)}, u32[]{:S(2)}, u32[]{:S(2)}) collective-permute-start(f32[32,128]{1,0:T(8,128)S(1)} %fusion.1), channel_id=1, source_target_pairs={{0,4},{4,0},{8,12},{12,8},{16,20},{20,16},{24,28},{28,24},{1,5},{5... | collective-permute-start | bytes 49160 | tf_op jit(solution)/shard_map/ppermute | solution.py:27
  28.9 6.4 %collective-permute-start.3 = (f32[32,128]{1,0:T(8,128)S(1)}, f32[32,128]{1,0:T(8,128)S(1)}, u32[]{:S(2)}, u32[]{:S(2)}) collective-permute-start(f32[32,128]{1,0:T(8,128)S(1)} %add.65), channel_id=1, source_target_pairs={{0,2},{1,3},{2,0},{3,1},{4,6},{5,7},{6,4},{7,5},{8,10},{9,11},{10,... | collective-permute-start | bytes 49160 | tf_op jit(solution)/shard_map/ppermute | solution.py:27
  35.4 1.2 %collective-permute-start.4 = (f32[32,128]{1,0:T(8,128)S(1)}, f32[32,128]{1,0:T(8,128)S(1)}, u32[]{:S(2)}, u32[]{:S(2)}) collective-permute-start(f32[32,128]{1,0:T(8,128)S(1)} %add.66), channel_id=1, source_target_pairs={{0,1},{1,0},{2,3},{3,2},{4,5},{5,4},{6,7},{7,6},{8,9},{9,8},{10,11... | collective-permute-start | bytes 49160 | tf_op jit(solution)/shard_map/ppermute | solution.py:27
  76.2 12.2 %all-to-all-start.1 = ((f32[32,8,128]{2,1,0:T(8,128)}), f32[32,8,128]{2,1,0:T(8,128)S(1)}, u32[]{:S(2)}, u32[]{:S(2)}) async-start(f32[32,8,128]{2,1,0:T(8,128)} %get-tuple-element.16), calls=%async_computation.1 | async-start | bytes 262144 | tf_op jit(solution)/shard_map/all_to_all | solution.py:505
  80.3 8.2 %copy-start.1 = (f32[1,1,4]{2,1,0:T(1,128)S(1)}, f32[1,1,4]{2,1,0:T(1,128)}, u32[]{:S(2)}) copy-start(f32[1,1,4]{2,1,0:T(1,128)} %param.8) | copy-start | bytes 52

commit v5 on v4

--- a/solution.py
+++ b/solution.py
@@ -13,8 +13,8 @@
 LANE = 128
 WIDE = 256
 REACH = 2
-BAND = (2 * REACH + 1) * LANE
-SPAN = 512
+BAND = 2 * REACH * LANE
+SPAN = 256
 GROUP = 16
 HALF_LANE = 64
 VMEM_LARGE = 56 * 1024 * 1024
@@ -28,35 +28,47 @@
 
 
 def gather_far(value):
-    step = 2
-    while step < lax.axis_size("azim"):
-        value = value + exchange(value, "azim", [step])
-        step *= 2
+    return value + exchange(value, "azim", [lax.axis_size("azim") // 2])
+
+
+def gather_near(value):
+    for axis in ("axial", "azim"):
+        step = 1
+        while step < lax.axis_size(axis):
+            if axis == "axial" or step != lax.axis_size("azim") // 2:
+                value = value + exchange(value, axis, [step])
+            step *= 2
     return value
 
 
-def gather_near(value):
-    value = value + exchange(value, "azim", [1])
-    step = lax.axis_size("axial") // 2
-    while step:
-        value = value + exchange(value, "axial", [step])
-        step //= 2
-    return value
-
-
-def tap_values(offset):
+def tap_values(lag, shift):
+    offset = lag.astype(jnp.float32) - shift
     centre = offset == 0.0
-    angle = jnp.where(centre, 1.0, math.pi * offset)
-    sinc = jnp.where(centre, 1.0, jnp.sin(angle) / angle)
+    swing = jnp.sin(math.pi * shift) / math.pi
+    swing = jnp.where((lag & 1) == 1, swing, -swing)
+    sinc = jnp.where(centre, 1.0, swing / jnp.where(centre, 1.0, offset))
     return sinc * jnp.exp(-(offset * offset) / (WINDOW * WINDOW))
 
 
-def wide_matrix(band_ref, s, way):
+def band_of(taps):
+    skewed = pltpu.roll(jnp.broadcast_to(taps, (LANE, BAND)), 0, 1, stride=1, stride_axis=0)
+    return skewed.astype(jnp.bfloat16)
+
+
+def corner_masks():
+    row = lax.broadcasted_iota(jnp.int32, (LANE, LANE), 0)
+    lane = lax.broadcasted_iota(jnp.int32, (LANE, LANE), 1)
+    return [jnp.where(v, 1.0, 0.0).astype(jnp.bfloat16) for v in (lane > row, lane < row)]
+
+
+def wide_matrix(band, mask_ref):
     def block(distance):
         if abs(distance) > REACH:
             return jnp.zeros((LANE, LANE), jnp.bfloat16)
+        if abs(distance) == REACH:
+            return band[:, :LANE] * mask_ref[0 if distance > 0 else 1]
         start = (REACH - distance) * LANE
-        return band_ref[s, way, :, start : start + LANE]
+        return band[:, start : start + LANE]
 
     rows = []
     for row in range(-2, 4):
@@ -79,9 +91,9 @@
     )
 
 
-def mixed(stacked, rows, band_ref, s, way):
+def mixed(stacked, rows, band, mask_ref):
     return jnp.dot(
-        spread(stacked, rows), wide_matrix(band_ref, s, way), preferred_element_type=jnp.float32
+        spread(stacked, rows), wide_matrix(band, mask_ref), preferred_element_type=jnp.float32
     )
 
 
@@ -111,14 +123,14 @@
 
 def prepare_kernel(
     tiles, cols, stride, pair_count, pair_ref, words_ref, table_ref,
-    band_ref, effect_ref, moment_ref, tap_ref, seen_ref, base_ref
+    band_ref, effect_ref, moment_ref, tap_ref, back_ref, seen_ref, base_ref, mask_ref
 ):
     blocks = cols // WIDE
     pair = pair_ref[0]
-    place = lax.broadcasted_iota(jnp.int32, (tiles, 2 * SPAN), 1).astype(jnp.float32) - SPAN
+    place = lax.broadcasted_iota(jnp.int32, (tiles, 2 * SPAN), 1) - SPAN
     shift = table_ref[:, 4:5]
-    tap_ref[0] = tap_values(-place - shift)
-    tap_ref[1] = tap_values(place - shift)
+    tap_ref[...] = tap_values(-place, shift)
+    back_ref[...] = tap_values(place, shift)
     az = axis_terms((8, cols), 1, cols)
     row = lax.broadcasted_iota(jnp.int32, (8, cols), 0)
     base = jnp.where(row == 0, 1.0, jnp.where(row == 1, az, jnp.where(row == 2, az * az, 0.0)))
@@ -126,20 +138,17 @@
     base = jnp.concatenate([high, low], axis=0)
     base_ref[...] = spread(stack_blocks(base).astype(jnp.bfloat16), 16)
     effect_ref[...] = jnp.zeros_like(effect_ref)
+    mask_ref[0], mask_ref[1] = corner_masks()
 
     def build(s, carry):
-        for way in range(2):
-            taps = jnp.broadcast_to(tap_ref[way, pl.ds(s, 1), :], (LANE, 2 * SPAN))
-            skewed = pltpu.roll(taps, 0, 1, stride=1, stride_axis=0)
-            first = SPAN - REACH * LANE
-            band_ref[s, way] = skewed[:, first : first + BAND].astype(jnp.bfloat16)
-        out = jnp.dot(
-            base_ref[...], wide_matrix(band_ref, s, 0), preferred_element_type=jnp.float32
-        )
+        band = band_of(tap_ref[pl.ds(s, 1), :])
+        band_ref[0, s] = band
+        band_ref[1, s] = band_of(back_ref[pl.ds(s, 1), :])
+        out = jnp.dot(base_ref[...], wide_matrix(band, mask_ref), preferred_element_type=jnp.float32)
         seen_ref[s] = jnp.sum(out.reshape(blocks, 2, 8, WIDE), axis=1)
         return carry
 
-    lax.fori_loop(0, tiles, build, 0, unroll=4)
+    lax.fori_loop(0, tiles, build, 0, unroll=8)
     column = lax.broadcasted_iota(jnp.int32, (2, 8, WIDE), 2) + WIDE * lax.broadcasted_iota(
         jnp.int32, (2, 8, WIDE), 0
     )
@@ -168,7 +177,8 @@
         for block in range(blocks):
             for part in parts:
                 rows.extend(two_parts(part[block]))
-        out = mixed(jnp.concatenate(rows, axis=0).astype(jnp.bfloat16), 48, band_ref, s, 1)
+        stacked = jnp.concatenate(rows, axis=0).astype(jnp.bfloat16)
+        out = mixed(stacked, 48, band_ref[1, s], mask_ref)
         out = jnp.sum(out.reshape(blocks, 3, 2, 8, WIDE), axis=2)
         for source, target in enumerate((s, before, after)):
             effect_ref[target] += out[:, source]
@@ -181,7 +191,7 @@
             )
         return carry
 
-    lax.fori_loop(0, tiles, respond, 0, unroll=4)
+    lax.fori_loop(0, tiles, respond, 0, unroll=8)
 
 
 def prepare(pair, table, cols, stride, pair_count):
@@ -192,69 +202,67 @@
     return pl.pallas_call(
         functools.partial(prepare_kernel, tiles, cols, stride, pair_count),
         out_shape=(
-            jax.ShapeDtypeStruct((tiles, 2, LANE, BAND), jnp.bfloat16),
+            jax.ShapeDtypeStruct((2, tiles, LANE, BAND), jnp.bfloat16),
             jax.ShapeDtypeStruct((tiles, blocks, 8, WIDE), jnp.float32),
             jax.ShapeDtypeStruct((tiles, 3, 8, LANE), jnp.float32),
         ),
         in_specs=[smem, smem, vmem],
         out_specs=(vmem, vmem, vmem),
         scratch_shapes=[
-            pltpu.VMEM((2, tiles, 2 * SPAN), jnp.float32),
+            pltpu.VMEM((tiles, 2 * SPAN), jnp.float32),
+            pltpu.VMEM((tiles, 2 * SPAN), jnp.float32),
             pltpu.VMEM((tiles, blocks, 8, WIDE), jnp.float32),
             pltpu.VMEM((16 * blocks, 3 * WIDE), jnp.bfloat16),
+            pltpu.VMEM((2, LANE, LANE), jnp.bfloat16),
         ],
         compiler_params=vmem_params(tiles),
     )(pair, table, table)
 
 
-def band_copies(band_hbm, band_ref, sems, g, way):
+def band_copy(band_hbm, band_ref, sems, way, g):
     part = pl.ds(g * GROUP, GROUP)
-    return pltpu.make_async_copy(band_hbm.at[part, way], band_ref.at[part, way], sems.at[way, g])
+    return pltpu.make_async_copy(band_hbm.at[way, part], band_ref.at[way, part], sems.at[way, g])
 
 
 def one_pass(
     tiles, stride, pair_count, scale, first_row, pair, row_total,
-    words_ref, height_ref, band_hbm, ref_ref, map_ref, band_ref, resampled_ref, total_ref, ref_low_ref, sems, keep
+    words_ref, height_ref, band_hbm, ref_ref, map_ref, band_ref, resampled_ref, total_ref, ref_low_ref, mask_ref, sems, keep
 ):
     rows, cols = ref_ref.shape
     blocks = cols // WIDE
     groups = tiles // GROUP
     for way in range(2):
         for g in range(groups):
-            band_copies(band_hbm, band_ref, sems, g, way).start()
-
+            band_copy(band_hbm, band_ref, sems, way, g).start()
+
+    mask_ref[0], mask_ref[1] = corner_masks()
     az = axis_terms((1, cols), 1, cols)
-    ax = axis_terms((rows, LANE), 0, row_total, first_row)
+    ax = axis_terms((rows, LANE), 0, row_total, first_row)[:, 0:1]
     ax_wide = axis_terms((rows, WIDE), 0, row_total, first_row).reshape(rows // 8, 8, WIDE)
-    column = lax.broadcasted_iota(jnp.int32, (2 * rows, WIDE), 1) + jnp.where(
-        lax.broadcasted_iota(jnp.int32, (2 * rows, WIDE), 0) >= rows, WIDE, 0
-    )
-    column = column.astype(jnp.float32)
+    column = lax.broadcasted_iota(jnp.int32, (1, WIDE), 1).astype(jnp.float32)
 
     def forward(s):
-        tilt = ax[:, 0:1]
-        shape = (
-            words_ref[s, 0]
-            + words_ref[s, 1] * az
-            + words_ref[s, 2] * tilt
-            + words_ref[s, 3] * (az * az + tilt * tilt - 2.0 / 3.0)
-        )
-        corrected = height_ref[s].astype(jnp.float32) - ref_low_ref[...] - shape
-        out = mixed(stack_blocks(corrected).astype(jnp.bfloat16), rows, band_ref, s, 0)
+        steep = words_ref[s, 3]
+        across = words_ref[s, 0] - steep * (2.0 / 3.0) + az * (words_ref[s, 1] + steep * az)
+        along = ax * (words_ref[s, 2] + steep * ax)
+        corrected = height_ref[s].astype(jnp.float32) - ref_low_ref[...] - across - along
+        out = mixed(stack_blocks(corrected).astype(jnp.bfloat16), rows, band_ref[0, s], mask_ref)
         resampled_ref[s] = out.astype(jnp.bfloat16)
-
-    def seam(left, right):
-        difference = resampled_ref[left, 2 * rows :, :].astype(jnp.float32) - resampled_ref[
-            right, : 2 * rows, :
-        ].astype(jnp.float32)
-        start = words_ref[left, 5 + pair]
-        inside = (column >= start) & (column < start + words_ref[left, 5 + pair_count + pair])
-        return jnp.where(inside, difference, 0.0)
 
     def backward(s):
         before, after = neighbours(s, tiles, stride)
-        upstream = jnp.concatenate([-seam(before, s), seam(s, after)], axis=0).astype(jnp.bfloat16)
-        return mixed(upstream, rows, band_ref, s, 1)
+        half = 2 * rows
+        upstream = []
+        for owner, other, mine in ((before, before, 0), (s, after, half)):
+            low = words_ref[owner, 5 + pair]
+            high = low + words_ref[owner, 5 + pair_count + pair]
+            theirs = half - mine
+            difference = resampled_ref[s, mine : mine + half, :] - resampled_ref[other, theirs : theirs + half, :]
+            for block in range(2):
+                place = column + block * WIDE
+                inside = jnp.where((place >= low) & (place < high), 1.0, 0.0).astype(jnp.bfloat16)
+                upstream.append(difference[block * rows : (block + 1) * rows] * inside)
+        return mixed(jnp.concatenate(upstream, axis=0), rows, band_ref[1, s], mask_ref)
 
     def term_sums(pulled):
         plain, tilted, bent = [], [], []
@@ -273,13 +281,13 @@
         return [jnp.sum(v, axis=0, keepdims=True) for v in folded]
 
     def all_forward(g, carry):
-        band_copies(band_hbm, band_ref, sems, g, 0).wait()
+        band_copy(band_hbm, band_ref, sems, 0, g).wait()
         for k in range(GROUP):
             forward(g * GROUP + k)
         return carry
 
     def all_backward(g, carry):
-        band_copies(band_hbm, band_ref, sems, g, 1).wait()
+        band_copy(band_hbm, band_ref, sems, 1, g).wait()
         for k in range(GROUP):
             s = g * GROUP + k
             pulled = backward(s)
@@ -302,12 +310,12 @@
 def first_kernel(
     tiles, row_total, stride, pair_count, scale,
     place_ref, words_ref, height_ref, band_hbm, ref_ref, effect_ref, extra_ref, map_ref, message_ref,
-    band_ref, resampled_ref, total_ref, ref_low_ref, sums_ref, sems
+    band_ref, resampled_ref, total_ref, ref_low_ref, mask_ref, sums_ref, sems
 ):
     rows, cols = ref_ref.shape
     ax_wide = one_pass(
         tiles, stride, pair_count, scale, place_ref[1].astype(jnp.float32), place_ref[0], row_total,
-        words_ref, height_ref, band_hbm, ref_ref, map_ref, band_ref, resampled_ref, total_ref, ref_low_ref, sems, sums_ref
+        words_ref, height_ref, band_hbm, ref_ref, map_ref, band_ref, resampled_ref, total_ref, ref_low_ref, mask_ref, sems, sums_ref
     )
 
     def lanes_dot(left, right):
@@ -343,11 +351,11 @@
 def second_kernel(
     tiles, row_total, stride, pair_count, scale,
     place_ref, words_ref, height_ref, band_hbm, ref_ref, map_ref,
-    band_ref, resampled_ref, total_ref, ref_low_ref, sems
+    band_ref, resampled_ref, total_ref, ref_low_ref, mask_ref, sems
 ):
     one_pass(
         tiles, stride, pair_count, scale, place_ref[1].astype(jnp.float32), place_ref[0], row_total,
-        words_ref, height_ref, band_hbm, ref_ref, map_ref, band_ref, resampled_ref, total_ref, ref_low_ref, sems, None
+        words_ref, height_ref, band_hbm, ref_ref, map_ref, band_ref, resampled_ref, total_ref, ref_low_ref, mask_ref, sems, None
     )
 
 
@@ -362,10 +370,11 @@
     anywhere = pl.BlockSpec(memory_space=pltpu.HBM)
     out_shape = [jax.ShapeDtypeStruct((rows, cols), jnp.float32)]
     scratch = [
-        pltpu.VMEM((tiles, 2, LANE, BAND), jnp.bfloat16),
+        pltpu.VMEM((2, tiles, LANE, BAND), jnp.bfloat16),
         pltpu.VMEM((tiles, 4 * rows, WIDE), jnp.bfloat16),
         pltpu.VMEM((4 * rows, WIDE), jnp.float32),
         pltpu.VMEM((rows, cols), jnp.float32),
+        pltpu.VMEM((2, LANE, LANE), jnp.bfloat16),
     ]
     if more:
         lines = 8 if small(tiles) else 12
@@ -503,7 +512,9 @@
         place, table, heights, bands, ref_map, (effects, extra), row_total, stride, pair_count
     )
     got = in_vmem(lax.all_to_all(message, AXES, 0, 0, tiled=True), tiles)
-    (map_rows,) = run_pass(place, table, heights, bands, map_rows, (), row_total, stride, pair_count)
+    (map_rows,) = run_pass(
+        place, table, heights, bands, map_rows, (), row_total, stride, pair_count
+    )
     new_map, new_coefs = finish(place, got, map_rows, effects, coefs[0], row_total, stride)
     return (new_map, new_coefs[None])
 

time: 90.3 us -> 87.2 us (0.966)
  Pallas kernels: 32.6 us -> 27.5 us
  waiting for transfers between devices: 30.4 us -> 34.7 us
  starting transfers between devices: 22.7 us -> 20.4 us
    ppermute x5, waiting for transfers between devices: 14.4 us -> 31.4 us  [exchange(): lax.ppermute(value, axis, [(i, i ^ k) for i in range(size)])]
    all_to_all x1, waiting for transfers between devices: 14.4 us -> 1.52 us  [local(): lax.all_to_all(own_heights[0, 0].reshape(tiles, rows, cols), AXES, 0, 0,...]
    pallas_call x1, Pallas kernels: 15.7 us -> 11.1 us  [prepare(): pl.pallas_call(functools.partial(prepare_kernel, tiles, cols, stride, pai...]
    ppermute x5, starting transfers between devices: 12.4 us -> 9.23 us  [exchange(): lax.ppermute(value, axis, [(i, i ^ k) for i in range(size)])]
    all_to_all x1, starting transfers between devices: 4.01 us -> 4.94 us  [local(): got = in_vmem(lax.all_to_all(message, AXES, 0, 0, tiled=True), tiles)]
  transfers between devices with their start and end apart: 7 -> 7, of which waited for: 7 -> 7; matrix products, arithmetic and copies ran while one was open for 1% -> 1% of each run, Pallas kernels for 25% -> 20%
where the time goes in v5:
time: 87.2 us; the launch traced here: 86.9 us
  waiting for transfers between devices  34.7 us (40%)
  Pallas kernels  27.5 us (32%)
  starting transfers between devices  20.4 us (23%)
  other arithmetic  2.01 us (2%)
  between operations  1.44 us (2%)
    ppermute x5, waiting for transfers between devices, exchange(): lax.ppermute(value, axis, [(i, i ^ k) for i in range(size)])  31.4 us
    pallas_call x2, Pallas kernels, run_pass(): pl.pallas_call(functools.partial(body, tiles, row_total, stride, pair_cou...  14.8 us
    pallas_call x1, Pallas kernels, prepare(): pl.pallas_call(functools.partial(prepare_kernel, tiles, cols, stride, pai...  11.1 us
    ppermute x5, starting transfers between devices, exchange(): lax.ppermute(value, axis, [(i, i ^ k) for i in range(size)])  9.23 us
    all_to_all x1, starting transfers between devices, local(): lax.all_to_all(own_heights[0, 0].reshape(tiles, rows, cols), AXES, 0, 0,...  6.24 us
    all_to_all x1, starting transfers between devices, local(): got = in_vmem(lax.all_to_all(message, AXES, 0, 0, tiled=True), tiles)  4.94 us
    all_to_all x1, waiting for transfers between devices, local(): got = in_vmem(lax.all_to_all(message, AXES, 0, 0, tiled=True), tiles)  1.78 us
  transfers between devices with their start and end apart: 7, of which 7 were waited for; matrix products, arithmetic and copies ran while one was open for 1% of the time, Pallas kernels for 20%

profile of v5, /device:TPU:0, one launch (start us, length us, event | category | flops | bytes accessed | tf_op | source)
XLA Modules:
  0.0 86.9 jit_solution(13412069471388329685)
XLA Ops:
  1.3 0.7 convert_bitcast_fusion
  2.0 0.7 select_maximum_fusion
  2.7 0.1 broadcast_select_fusion
  2.8 4.0 %collective-permute-start = (f32[32,128]{1,0:T(8,128)S(1)}, f32[32,128]{1,0:T(8,128)S(1)}, u32[]{:S(2)}, u32[]{:S(2)}) collective-permute-start(f32[32,128]{1,0:T(8,128)S(1)} %broadcast_select_fusion), channel_id=1, source_target_pairs={{0,16},{4,20},{8,24},{12,28},{16,0},{20,4},{24,8},{28,12},{1,17},{... | collective-permute-start | bytes 49160 | tf_op jit(solution)/shard_map/ppermute | solution.py:27
  6.8 1.7 %collective-permute-done = f32[32,128]{1,0:T(8,128)S(1)} collective-permute-done((f32[32,128]{1,0:T(8,128)S(1)}, f32[32,128]{1,0:T(8,128)S(1)}, u32[]{:S(2)}, u32[]{:S(2)}) %collective-permute-start) | collective-permute-done | bytes 16416 | tf_op jit(solution)/shard_map/ppermute | solution.py:27
  8.6 6.2 %all-to-all-start = ((bf16[32,32,1024]{2,1,0:T(8,128)(2,1)}), bf16[32,32,1024]{2,1,0:T(8,128)(2,1)S(1)}, u32[]{:S(2)}, u32[]{:S(2)}) async-start(bf16[32,32,1024]{2,1,0:T(8,128)(2,1)} %bitcast.26), calls=%async_computation | async-start | bytes 4194304 | tf_op jit(solution)/shard_map/all_to_all | solution.py:499
  14.9 0.1 pad.16.clone
  15.0 0.1 pad.17.clone
  15.0 0.1 maximum_bitcast_fusion
  15.1 0.3 collective-permute-start.1
  15.4 0.9 %collective-permute-done.1 = f32[32,128]{1,0:T(8,128)S(1)} collective-permute-done((f32[32,128]{1,0:T(8,128)S(1)}, f32[32,128]{1,0:T(8,128)S(1)}, u32[]{:S(2)}, u32[]{:S(2)}) %collective-permute-start.1) | collective-permute-done | bytes 16416 | tf_op jit(solution)/shard_map/ppermute | solution.py:27
  16.3 1.8 %collective-permute-start.2 = (f32[32,128]{1,0:T(8,128)S(1)}, f32[32,128]{1,0:T(8,128)S(1)}, u32[]{:S(2)}, u32[]{:S(2)}) collective-permute-start(f32[32,128]{1,0:T(8,128)S(1)} %add.64), channel_id=1, source_target_pairs={{0,2},{1,3},{2,0},{3,1},{4,6},{5,7},{6,4},{7,5},{8,10},{9,11},{10,... | collective-permute-start | bytes 49160 | tf_op jit(solution)/shard_map/ppermute | solution.py:27
  18.1 10.5 %collective-permute-done.2 = f32[32,128]{1,0:T(8,128)S(1)} collective-permute-done((f32[32,128]{1,0:T(8,128)S(1)}, f32[32,128]{1,0:T(8,128)S(1)}, u32[]{:S(2)}, u32[]{:S(2)}) %collective-permute-start.2) | collective-permute-done | bytes 16416 | tf_op jit(solution)/shard_map/ppermute | solution.py:27
  28.6 2.3 %collective-permute-start.3 = (f32[32,128]{1,0:T(8,128)S(1)}, f32[32,128]{1,0:T(8,128)S(1)}, u32[]{:S(2)}, u32[]{:S(2)}) collective-permute-start(f32[32,128]{1,0:T(8,128)S(1)} %add.65), channel_id=1, source_target_pairs={{0,4},{4,0},{8,12},{12,8},{16,20},{20,16},{24,28},{28,24},{1,5},{5... | collective-permute-start | bytes 49160 | tf_op jit(solution)/shard_map/ppermute | solution.py:27
  30.9 0.1 multiply_reduce_fusion.1
  31.0 2.1 %collective-permute-done.3 = f32[32,128]{1,0:T(8,128)S(1)} collective-permute-done((f32[32,128]{1,0:T(8,128)S(1)}, f32[32,128]{1,0:T(8,128)S(1)}, u32[]{:S(2)}, u32[]{:S(2)}) %collective-permute-start.3) | collective-permute-done | bytes 16416 | tf_op jit(solution)/shard_map/ppermute | solution.py:27
  33.1 0.9 %collective-permute-start.4 = (f32[32,128]{1,0:T(8,128)S(1)}, f32[32,128]{1,0:T(8,128)S(1)}, u32[]{:S(2)}, u32[]{:S(2)}) collective-permute-start(f32[32,128]{1,0:T(8,128)S(1)} %add.66), channel_id=1, source_target_pairs={{0,8},{4,12},{8,0},{12,4},{16,24},{20,28},{24,16},{28,20},{1,9},{5... | collective-permute-start | bytes 49160 | tf_op jit(solution)/shard_map/ppermute | solution.py:27
  34.0 0.1 pad_add_fusion.pair_ref.place_ref
  34.1 16.2 %collective-permute-done.4 = f32[32,128]{1,0:T(8,128)S(1)} collective-permute-done((f32[32,128]{1,0:T(8,128)S(1)}, f32[32,128]{1,0:T(8,128)S(1)}, u32[]{:S(2)}, u32[]{:S(2)}) %collective-permute-start.4) | collective-permute-done | bytes 16416 | tf_op jit(solution)/shard_map/ppermute | solution.py:27
  50.3 11.1 %shard_map.77 = (bf16[2,32,128,512]{3,2,1,0:T(8,128)(2,1)}, f32[32,4,8,256]{3,2,1,0:T(8,128)S(1)}, f32[32,3,8,128]{3,2,1,0:T(8,128)S(1)}) custom-call(s32[3]{0:T(128)S(1)} %pad_add_fusion.pair_ref.place_ref, f32[32,128]{1,0:T(8,128)S(1)} %add.67.words_ref.table_ref, f32[32,128]{1,0:T(8,128)S(1)} %add.67.words_ref.table_ref), custom_call_target="tpu_custom_call" | custom-call | tf_op jit(solution)/shard_map/pallas_call | solution.py:202
  61.4 0.1 slice_bitcast_fusion
  61.5 0.1 copy.11
  61.6 0.2 reshape.40.effect_ref
  61.8 0.1 copy.12
  61.9 0.1 multiply_reduce_fusion
  62.1 0.1 copy.16
  62.2 1.5 %all-to-all-done.height_ref = bf16[32,32,1024]{2,1,0:T(8,128)(2,1)S(1)} async-done(((bf16[32,32,1024]{2,1,0:T(8,128)(2,1)}), bf16[32,32,1024]{2,1,0:T(8,128)(2,1)S(1)}, u32[]{:S(2)}, u32[]{:S(2)}) %all-to-all-start) | async-done | bytes 2097184 | tf_op jit(solution)/shard_map/all_to_all | solution.py:499
  63.8 8.4 %shard_map.78 = (f32[32,1024]{1,0:T(8,128)S(1)}, f32[32,8,128]{2,1,0:T(8,128)}) custom-call(s32[3]{0:T(128)S(1)} %pad_add_fusion.pair_ref.place_ref, f32[32,128]{1,0:T(8,128)S(1)} %add.67.words_ref.table_ref, bf16[32,32,1024]{2,1,0:T(8,128)(2,1)S(1)} %all-to-all-done.height_ref, bf16[2,32,128,512]{3,2,1,0:T(8,128)(2,1)} %get-tuple-element.13.band_hbm, ...), custom_call_target="tpu_custom_call" | custom-call | tf_op jit(solution)/shard_map/pallas_call | solution.py:385
  72.2 4.9 %all-to-all-start.1 = ((f32[32,8,128]{2,1,0:T(8,128)}), f32[32,8,128]{2,1,0:T(8,128)S(1)}, u32[]{:S(2)}, u32[]{:S(2)}) async-start(f32[32,8,128]{2,1,0:T(8,128)} %get-tuple-element.16), calls=%async_computation.1 | async-start | bytes 262144 | tf_op jit(solution)/shard_map/all_to_all | solution.py:514
  77.1 6.4 %shard_map.79.map_ref = f32[32,1024]{1,0:T(8,128)S(1)} custom-call(s32[3]{0:T(128)S(1)} %pad_add_fusion.pair_ref.place_ref, f32[32,128]{1,0:T(8,128)S(1)} %add.67.words_ref.table_ref, bf16[32,32,1024]{2,1,0:T(8,128)(2,1)S(1)} %all-to-all-done.height_ref, bf16[2,32,128,512]{3,2,1,0:T(8,128)(2,1)} %get-tuple-element.13.band_hbm, ...), custom_call_target="tpu_custom_call" | custom-call | tf_op jit(solution)/shard_map/pallas_call | solution.py:385
  83.5 1.8 %all-to-all-done.1.got_ref = f32[32,8,128]{2,1,0:T(8,128)S(1)} async-done(((f32[32,8,128]{2,1,0:T(8,128)}), f32[32,8,128]{2,1,0:T(8,128)S(1)}, u32[]{:S(2)}, u32[]{:S(2)}) %all-to-all-start.1) | async-done | bytes 131104 | tf_op jit(solution)/shard_map/all_to_all | solution.py:514
  85.3 1.6 %shard_map.80 = (f32[32,1024]{1,0:T(8,128)}, f32[1,4]{1,0:T(1,128)}) custom-call(s32[3]{0:T(128)S(1)} %pad_add_fusion.pair_ref.place_ref, f32[32,8,128]{2,1,0:T(8,128)S(1)} %all-to-all-done.1.got_ref, f32[32,1024]{1,0:T(8,128)S(1)} %shard_map.79.map_ref, f32[3,32,1024]{2,1,0:T(8,128)S(1)} %reshape.40.effect_ref, f32[1,4]{1,0:T(1,128)S(1)} %bitcast.25), custom_call_target="tpu_custom_call" | custom-call | tf_op jit(solution)/shard_map/pallas_call | solution.py:447
  (22 shorter events, 0.2 us)
Async XLA Ops:
  2.8 5.8 %collective-permute-start = (f32[32,128]{1,0:T(8,128)S(1)}, f32[32,128]{1,0:T(8,128)S(1)}, u32[]{:S(2)}, u32[]{:S(2)}) collective-permute-start(f32[32,128]{1,0:T(8,128)S(1)} %broadcast_select_fusion), channel_id=1, source_target_pairs={{0,16},{4,20},{8,24},{12,28},{16,0},{20,4},{24,8},{28,12},{1,17},{... | collective-permute-start | bytes 49160 | tf_op jit(solution)/shard_map/ppermute | solution.py:27
  8.6 9.5 %copy-start.2 = (f32[1,3,32]{2,1,0:T(4,128)S(1)}, f32[1,3,32]{2,1,0:T(4,128)}, u32[]{:S(2)}) copy-start(f32[1,3,32]{2,1,0:T(4,128)} %constant.43.clone.1) | copy-start | bytes 1156
  8.6 9.5 %copy-start.3 = (f32[1,3,32]{2,1,0:T(4,128)S(1)}, f32[1,3,32]{2,1,0:T(4,128)}, u32[]{:S(2)}) copy-start(f32[1,3,32]{2,1,0:T(4,128)} %constant.44.clone.1) | copy-start | bytes 1156
  8.6 55.1 %all-to-all-start = ((bf16[32,32,1024]{2,1,0:T(8,128)(2,1)}), bf16[32,32,1024]{2,1,0:T(8,128)(2,1)S(1)}, u32[]{:S(2)}, u32[]{:S(2)}) async-start(bf16[32,32,1024]{2,1,0:T(8,128)(2,1)} %bitcast.26), calls=%async_computation | async-start | bytes 4194304 | tf_op jit(solution)/shard_map/all_to_all | solution.py:499
  14.9 48.9 %copy-start = (f32[32,1024]{1,0:T(8,128)S(1)}, f32[32,1024]{1,0:T(8,128)}, u32[]{:S(2)}) copy-start(f32[32,1024]{1,0:T(8,128)} %ref_ref.1) | copy-start | bytes 393220
  15.1 1.2 %collective-permute-start.1 = (f32[32,128]{1,0:T(8,128)S(1)}, f32[32,128]{1,0:T(8,128)S(1)}, u32[]{:S(2)}, u32[]{:S(2)}) collective-permute-start(f32[32,128]{1,0:T(8,128)S(1)} %fusion), channel_id=1, source_target_pairs={{0,1},{1,0},{2,3},{3,2},{4,5},{5,4},{6,7},{7,6},{8,9},{9,8},{10,11... | collective-permute-start | bytes 49160 | tf_op jit(solution)/shard_map/ppermute | solution.py:27
  16.3 12.3 %collective-permute-start.2 = (f32[32,128]{1,0:T(8,128)S(1)}, f32[32,128]{1,0:T(8,128)S(1)}, u32[]{:S(2)}, u32[]{:S(2)}) collective-permute-start(f32[32,128]{1,0:T(8,128)S(1)} %add.64), channel_id=1, source_target_pairs={{0,2},{1,3},{2,0},{3,1},{4,6},{5,7},{6,4},{7,5},{8,10},{9,11},{10,... | collective-permute-start | bytes 49160 | tf_op jit(solution)/shard_map/ppermute | solution.py:27
  28.6 4.5 %collective-permute-start.3 = (f32[32,128]{1,0:T(8,128)S(1)}, f32[32,128]{1,0:T(8,128)S(1)}, u32[]{:S(2)}, u32[]{:S(2)}) collective-permute-start(f32[32,128]{1,0:T(8,128)S(1)} %add.65), channel_id=1, source_target_pairs={{0,4},{4,0},{8,12},{12,8},{16,20},{20,16},{24,28},{28,24},{1,5},{5... | collective-permute-start | bytes 49160 | tf_op jit(solution)/shard_map/ppermute | solution.py:27
  33.1 17.2 %collective-permute-start.4 = (f32[32,128]{1,0:T(8,128)S(1)}, f32[32,128]{1,0:T(8,128)S(1)}, u32[]{:S(2)}, u32[]{:S(2)}) collective-permute-start(f32[32,128]{1,0:T(8,128)S(1)} %add.66), channel_id=1, source_target_pairs={{0,8},{4,12},{8,0},{12,4},{16,24},{20,28},{24,16},{28,20},{1,9},{5... | collective-permute-start | bytes 49160 | tf_op jit(solution)/shard_map/ppermute | solution.py:27
  72.2 13.2 %all-to-all-start.1 = ((f32[32,8,128]{2,1,0:T(8,128)}), f32[32,8,128]{2,1,0:T(8,128)S(1)}, u32[]{:S(2)}, u32[]{:S(2)}) async-start(f32[32,8,128]{2,1,0:T(8,128)} %get-tuple-element.16), calls=%async_computation.1 | async-start | bytes 262144 | tf_op jit(solution)/shard_map/all_to_all | solution.py:514
  77.1 8.2 %copy-start.1 = (f32[1,1,4]{2,1,0:T(1,128)S(1)}, f32[1,1,4]{2,1,0:T(1,128)}, u32[]{:S(2)}) copy-start(f32[1,1,4]{2,1,0:T(1,128)} %param.8) | copy-start | bytes 52

commit v6 on v5

--- a/solution.py
+++ b/solution.py
@@ -25,10 +25,6 @@
 def exchange(value, axis, steps):
     size = lax.axis_size(axis)
     return sum(lax.ppermute(value, axis, [(i, i ^ k) for i in range(size)]) for k in steps)
-
-
-def gather_far(value):
-    return value + exchange(value, "azim", [lax.axis_size("azim") // 2])
 
 
 def gather_near(value):
@@ -148,7 +144,7 @@
         seen_ref[s] = jnp.sum(out.reshape(blocks, 2, 8, WIDE), axis=1)
         return carry
 
-    lax.fori_loop(0, tiles, build, 0, unroll=8)
+    lax.fori_loop(0, tiles, build, 0, unroll=16)
     column = lax.broadcasted_iota(jnp.int32, (2, 8, WIDE), 2) + WIDE * lax.broadcasted_iota(
         jnp.int32, (2, 8, WIDE), 0
     )
@@ -191,7 +187,7 @@
             )
         return carry
 
-    lax.fori_loop(0, tiles, respond, 0, unroll=8)
+    lax.fori_loop(0, tiles, respond, 0, unroll=16)
 
 
 def prepare(pair, table, cols, stride, pair_count):
@@ -493,9 +489,12 @@
         ]
     )
     words = jnp.pad(words, (0, LANE - words.shape[0]))[None]
-    owner = lax.broadcasted_iota(jnp.int32, (tiles, LANE), 0) == me
-    table = gather_far(jnp.where(owner, words, 0.0))
-    table, own_heights = lax.optimization_barrier((table, observed_heights))
+    far = lax.axis_size("azim") // 2
+    theirs = exchange(words, "azim", [far])
+    theirs, own_heights = lax.optimization_barrier((theirs, observed_heights))
+    line = lax.broadcasted_iota(jnp.int32, (tiles, LANE), 0)
+    them = (lax.axis_index("azim") ^ far) * stride + lax.axis_index("axial")
+    table = jnp.where(line == me, words, jnp.where(line == them, theirs, 0.0))
     heights = lax.all_to_all(
         own_heights[0, 0].reshape(tiles, rows, cols), AXES, 0, 0, tiled=True
     )

time: 87.2 us -> 85.8 us (0.984)
  Pallas kernels: 27.5 us -> 26.5 us
  starting transfers between devices: 20.4 us -> 19.5 us
    all_to_all x1, waiting for transfers between devices: 1.52 us -> 2.45 us  [local(): lax.all_to_all(own_heights[0, 0].reshape(tiles, rows, cols), AXES, 0, 0,...]
    pallas_call x1, Pallas kernels: 11.1 us -> 10.2 us  [prepare(): pl.pallas_call(functools.partial(prepare_kernel, tiles, cols, stride, pai...]
    all_to_all x1, starting transfers between devices: 4.94 us -> 4.02 us  [local(): got = in_vmem(lax.all_to_all(message, AXES, 0, 0, tiled=True), tiles)]
  transfers between devices with their start and end apart: 7 -> 7, of which waited for: 7 -> 7; matrix products, arithmetic and copies ran while one was open for 1% -> 2% of each run, Pallas kernels for 20% -> 19%
where the time goes in v6:
time: 85.8 us; the launch traced here: 85.6 us
  waiting for transfers between devices  35.2 us (41%)
  Pallas kernels  26.5 us (31%)
  starting transfers between devices  19.5 us (23%)
  other arithmetic  2.08 us (2%)
  between operations  1.43 us (2%)
  local copies, waits for them, and re-layouts  0.86 us (1%)
    ppermute x5, waiting for transfers between devices, exchange(): lax.ppermute(value, axis, [(i, i ^ k) for i in range(size)])  30.9 us
    pallas_call x2, Pallas kernels, run_pass(): pl.pallas_call(functools.partial(body, tiles, row_total, stride, pair_cou...  14.8 us
    pallas_call x1, Pallas kernels, prepare(): pl.pallas_call(functools.partial(prepare_kernel, tiles, cols, stride, pai...  10.2 us
    ppermute x5, starting transfers between devices, exchange(): lax.ppermute(value, axis, [(i, i ^ k) for i in range(size)])  9.29 us
    all_to_all x1, starting transfers between devices, local(): lax.all_to_all(own_heights[0, 0].reshape(tiles, rows, cols), AXES, 0, 0,...  6.18 us
    all_to_all x1, starting transfers between devices, local(): got = in_vmem(lax.all_to_all(message, AXES, 0, 0, tiled=True), tiles)  4.02 us
    all_to_all x1, waiting for transfers between devices, local(): lax.all_to_all(own_heights[0, 0].reshape(tiles, rows, cols), AXES, 0, 0,...  2.45 us
    all_to_all x1, waiting for transfers between devices, local(): got = in_vmem(lax.all_to_all(message, AXES, 0, 0, tiled=True), tiles)  1.78 us
  transfers between devices with their start and end apart: 7, of which 7 were waited for; matrix products, arithmetic and copies ran while one was open for 2% of the time, Pallas kernels for 19%

profile of v6, /device:TPU:0, one launch (start us, length us, event | category | flops | bytes accessed | tf_op | source)
XLA Modules:
  0.0 85.6 jit_solution(4468631225582900519)
XLA Ops:
  1.3 0.7 convert_bitcast_fusion
  2.0 0.7 select_maximum_fusion
  2.7 4.0 %collective-permute-start = (f32[1,128]{1,0:T(1,128)S(1)}, f32[1,128]{1,0:T(1,128)S(1)}, u32[]{:S(2)}, u32[]{:S(2)}) collective-permute-start(f32[1,128]{1,0:T(1,128)S(1)} %bitcast.32), channel_id=1, source_target_pairs={{0,16},{4,20},{8,24},{12,28},{16,0},{20,4},{24,8},{28,12},{1,17},{... | collective-permute-start | bytes 1544 | tf_op jit(solution)/shard_map/ppermute | solution.py:27
  6.7 1.5 %collective-permute-done = f32[1,128]{1,0:T(1,128)S(1)} collective-permute-done((f32[1,128]{1,0:T(1,128)S(1)}, f32[1,128]{1,0:T(1,128)S(1)}, u32[]{:S(2)}, u32[]{:S(2)}) %collective-permute-start) | collective-permute-done | bytes 544 | tf_op jit(solution)/shard_map/ppermute | solution.py:27
  8.2 6.2 %all-to-all-start = ((bf16[32,32,1024]{2,1,0:T(8,128)(2,1)}), bf16[32,32,1024]{2,1,0:T(8,128)(2,1)S(1)}, u32[]{:S(2)}, u32[]{:S(2)}) async-start(bf16[32,32,1024]{2,1,0:T(8,128)(2,1)} %bitcast.28), calls=%async_computation | async-start | bytes 4194304 | tf_op jit(solution)/shard_map/all_to_all | solution.py:498
  14.5 0.1 pad.16.clone
  14.6 0.1 maximum_bitcast_fusion
  14.8 0.3 collective-permute-start.1
  15.0 0.9 %collective-permute-done.1 = f32[32,128]{1,0:T(8,128)S(1)} collective-permute-done((f32[32,128]{1,0:T(8,128)S(1)}, f32[32,128]{1,0:T(8,128)S(1)}, u32[]{:S(2)}, u32[]{:S(2)}) %collective-permute-start.1) | collective-permute-done | bytes 16416 | tf_op jit(solution)/shard_map/ppermute | solution.py:27
  16.0 0.1 fusion
  16.0 1.8 %collective-permute-start.2 = (f32[32,128]{1,0:T(8,128)S(1)}, f32[32,128]{1,0:T(8,128)S(1)}, u32[]{:S(2)}, u32[]{:S(2)}) collective-permute-start(f32[32,128]{1,0:T(8,128)S(1)} %fusion), channel_id=1, source_target_pairs={{0,2},{1,3},{2,0},{3,1},{4,6},{5,7},{6,4},{7,5},{8,10},{9,11},{10,... | collective-permute-start | bytes 49160 | tf_op jit(solution)/shard_map/ppermute | solution.py:27
  17.9 10.3 %collective-permute-done.2 = f32[32,128]{1,0:T(8,128)S(1)} collective-permute-done((f32[32,128]{1,0:T(8,128)S(1)}, f32[32,128]{1,0:T(8,128)S(1)}, u32[]{:S(2)}, u32[]{:S(2)}) %collective-permute-start.2) | collective-permute-done | bytes 16416 | tf_op jit(solution)/shard_map/ppermute | solution.py:27
  28.1 0.1 fusion.1
  28.2 2.3 %collective-permute-start.3 = (f32[32,128]{1,0:T(8,128)S(1)}, f32[32,128]{1,0:T(8,128)S(1)}, u32[]{:S(2)}, u32[]{:S(2)}) collective-permute-start(f32[32,128]{1,0:T(8,128)S(1)} %fusion.1), channel_id=1, source_target_pairs={{0,4},{4,0},{8,12},{12,8},{16,20},{20,16},{24,28},{28,24},{1,5},{5... | collective-permute-start | bytes 49160 | tf_op jit(solution)/shard_map/ppermute | solution.py:27
  30.5 0.1 multiply_reduce_fusion.1
  30.7 2.1 %collective-permute-done.3 = f32[32,128]{1,0:T(8,128)S(1)} collective-permute-done((f32[32,128]{1,0:T(8,128)S(1)}, f32[32,128]{1,0:T(8,128)S(1)}, u32[]{:S(2)}, u32[]{:S(2)}) %collective-permute-start.3) | collective-permute-done | bytes 16416 | tf_op jit(solution)/shard_map/ppermute | solution.py:27
  32.8 0.9 %collective-permute-start.4 = (f32[32,128]{1,0:T(8,128)S(1)}, f32[32,128]{1,0:T(8,128)S(1)}, u32[]{:S(2)}, u32[]{:S(2)}) collective-permute-start(f32[32,128]{1,0:T(8,128)S(1)} %add.66), channel_id=1, source_target_pairs={{0,8},{4,12},{8,0},{12,4},{16,24},{20,28},{24,16},{28,20},{1,9},{5... | collective-permute-start | bytes 49160 | tf_op jit(solution)/shard_map/ppermute | solution.py:27
  33.7 0.1 pad_add_fusion.pair_ref.place_ref
  33.8 16.1 %collective-permute-done.4 = f32[32,128]{1,0:T(8,128)S(1)} collective-permute-done((f32[32,128]{1,0:T(8,128)S(1)}, f32[32,128]{1,0:T(8,128)S(1)}, u32[]{:S(2)}, u32[]{:S(2)}) %collective-permute-start.4) | collective-permute-done | bytes 16416 | tf_op jit(solution)/shard_map/ppermute | solution.py:27
  49.9 10.2 %shard_map.77 = (bf16[2,32,128,512]{3,2,1,0:T(8,128)(2,1)}, f32[32,4,8,256]{3,2,1,0:T(8,128)S(1)}, f32[32,3,8,128]{3,2,1,0:T(8,128)S(1)}) custom-call(s32[3]{0:T(128)S(1)} %pad_add_fusion.pair_ref.place_ref, f32[32,128]{1,0:T(8,128)S(1)} %add.67.words_ref.table_ref, f32[32,128]{1,0:T(8,128)S(1)} %add.67.words_ref.table_ref), custom_call_target="tpu_custom_call" | custom-call | tf_op jit(solution)/shard_map/pallas_call | solution.py:198
  60.0 0.1 slice_bitcast_fusion
  60.1 0.1 copy.11
  60.2 0.2 reshape.40.effect_ref
  60.5 0.1 copy.12
  60.6 0.1 multiply_reduce_fusion
  60.7 0.1 copy.16
  60.9 2.5 %all-to-all-done.height_ref = bf16[32,32,1024]{2,1,0:T(8,128)(2,1)S(1)} async-done(((bf16[32,32,1024]{2,1,0:T(8,128)(2,1)}), bf16[32,32,1024]{2,1,0:T(8,128)(2,1)S(1)}, u32[]{:S(2)}, u32[]{:S(2)}) %all-to-all-start) | async-done | bytes 2097184 | tf_op jit(solution)/shard_map/all_to_all | solution.py:498
  63.3 8.4 %shard_map.78 = (f32[32,1024]{1,0:T(8,128)S(1)}, f32[32,8,128]{2,1,0:T(8,128)}) custom-call(s32[3]{0:T(128)S(1)} %pad_add_fusion.pair_ref.place_ref, f32[32,128]{1,0:T(8,128)S(1)} %add.67.words_ref.table_ref, bf16[32,32,1024]{2,1,0:T(8,128)(2,1)S(1)} %all-to-all-done.height_ref, bf16[2,32,128,512]{3,2,1,0:T(8,128)(2,1)} %get-tuple-element.13.band_hbm, ...), custom_call_target="tpu_custom_call" | custom-call | tf_op jit(solution)/shard_map/pallas_call | solution.py:381
  71.7 4.0 %all-to-all-start.1 = ((f32[32,8,128]{2,1,0:T(8,128)}), f32[32,8,128]{2,1,0:T(8,128)S(1)}, u32[]{:S(2)}, u32[]{:S(2)}) async-start(f32[32,8,128]{2,1,0:T(8,128)} %get-tuple-element.16), calls=%async_computation.1 | async-start | bytes 262144 | tf_op jit(solution)/shard_map/all_to_all | solution.py:513
  75.8 6.4 %shard_map.79.map_ref = f32[32,1024]{1,0:T(8,128)S(1)} custom-call(s32[3]{0:T(128)S(1)} %pad_add_fusion.pair_ref.place_ref, f32[32,128]{1,0:T(8,128)S(1)} %add.67.words_ref.table_ref, bf16[32,32,1024]{2,1,0:T(8,128)(2,1)S(1)} %all-to-all-done.height_ref, bf16[2,32,128,512]{3,2,1,0:T(8,128)(2,1)} %get-tuple-element.13.band_hbm, ...), custom_call_target="tpu_custom_call" | custom-call | tf_op jit(solution)/shard_map/pallas_call | solution.py:381
  82.2 1.8 %all-to-all-done.1.got_ref = f32[32,8,128]{2,1,0:T(8,128)S(1)} async-done(((f32[32,8,128]{2,1,0:T(8,128)}), f32[32,8,128]{2,1,0:T(8,128)S(1)}, u32[]{:S(2)}, u32[]{:S(2)}) %all-to-all-start.1) | async-done | bytes 131104 | tf_op jit(solution)/shard_map/all_to_all | solution.py:513
  84.0 1.6 %shard_map.80 = (f32[32,1024]{1,0:T(8,128)}, f32[1,4]{1,0:T(1,128)}) custom-call(s32[3]{0:T(128)S(1)} %pad_add_fusion.pair_ref.place_ref, f32[32,8,128]{2,1,0:T(8,128)S(1)} %all-to-all-done.1.got_ref, f32[32,1024]{1,0:T(8,128)S(1)} %shard_map.79.map_ref, f32[3,32,1024]{2,1,0:T(8,128)S(1)} %reshape.40.effect_ref, f32[1,4]{1,0:T(1,128)S(1)} %bitcast.27), custom_call_target="tpu_custom_call" | custom-call | tf_op jit(solution)/shard_map/pallas_call | solution.py:443
  (21 shorter events, 0.3 us)
Async XLA Ops:
  2.7 5.6 %collective-permute-start = (f32[1,128]{1,0:T(1,128)S(1)}, f32[1,128]{1,0:T(1,128)S(1)}, u32[]{:S(2)}, u32[]{:S(2)}) collective-permute-start(f32[1,128]{1,0:T(1,128)S(1)} %bitcast.32), channel_id=1, source_target_pairs={{0,16},{4,20},{8,24},{12,28},{16,0},{20,4},{24,8},{28,12},{1,17},{... | collective-permute-start | bytes 1544 | tf_op jit(solution)/shard_map/ppermute | solution.py:27
  8.2 9.6 %copy-start.2 = (f32[1,3,32]{2,1,0:T(4,128)S(1)}, f32[1,3,32]{2,1,0:T(4,128)}, u32[]{:S(2)}) copy-start(f32[1,3,32]{2,1,0:T(4,128)} %constant.43.clone.1) | copy-start | bytes 1156
  8.2 9.6 %copy-start.3 = (f32[1,3,32]{2,1,0:T(4,128)S(1)}, f32[1,3,32]{2,1,0:T(4,128)}, u32[]{:S(2)}) copy-start(f32[1,3,32]{2,1,0:T(4,128)} %constant.44.clone.1) | copy-start | bytes 1156
  8.2 55.1 %all-to-all-start = ((bf16[32,32,1024]{2,1,0:T(8,128)(2,1)}), bf16[32,32,1024]{2,1,0:T(8,128)(2,1)S(1)}, u32[]{:S(2)}, u32[]{:S(2)}) async-start(bf16[32,32,1024]{2,1,0:T(8,128)(2,1)} %bitcast.28), calls=%async_computation | async-start | bytes 4194304 | tf_op jit(solution)/shard_map/all_to_all | solution.py:498
  14.4 48.9 %copy-start = (f32[32,1024]{1,0:T(8,128)S(1)}, f32[32,1024]{1,0:T(8,128)}, u32[]{:S(2)}) copy-start(f32[32,1024]{1,0:T(8,128)} %ref_ref.1) | copy-start | bytes 393220
  14.8 1.2 %collective-permute-start.1 = (f32[32,128]{1,0:T(8,128)S(1)}, f32[32,128]{1,0:T(8,128)S(1)}, u32[]{:S(2)}, u32[]{:S(2)}) collective-permute-start(f32[32,128]{1,0:T(8,128)S(1)} %select_select_fusion), channel_id=1, source_target_pairs={{0,1},{1,0},{2,3},{3,2},{4,5},{5,4},{6,7},{7,6},{8,9},{9,8},{10,11... | collective-permute-start | bytes 49160 | tf_op jit(solution)/shard_map/ppermute | solution.py:27
  16.0 12.1 %collective-permute-start.2 = (f32[32,128]{1,0:T(8,128)S(1)}, f32[32,128]{1,0:T(8,128)S(1)}, u32[]{:S(2)}, u32[]{:S(2)}) collective-permute-start(f32[32,128]{1,0:T(8,128)S(1)} %fusion), channel_id=1, source_target_pairs={{0,2},{1,3},{2,0},{3,1},{4,6},{5,7},{6,4},{7,5},{8,10},{9,11},{10,... | collective-permute-start | bytes 49160 | tf_op jit(solution)/shard_map/ppermute | solution.py:27
  28.2 4.5 %collective-permute-start.3 = (f32[32,128]{1,0:T(8,128)S(1)}, f32[32,128]{1,0:T(8,128)S(1)}, u32[]{:S(2)}, u32[]{:S(2)}) collective-permute-start(f32[32,128]{1,0:T(8,128)S(1)} %fusion.1), channel_id=1, source_target_pairs={{0,4},{4,0},{8,12},{12,8},{16,20},{20,16},{24,28},{28,24},{1,5},{5... | collective-permute-start | bytes 49160 | tf_op jit(solution)/shard_map/ppermute | solution.py:27
  32.8 17.1 %collective-permute-start.4 = (f32[32,128]{1,0:T(8,128)S(1)}, f32[32,128]{1,0:T(8,128)S(1)}, u32[]{:S(2)}, u32[]{:S(2)}) collective-permute-start(f32[32,128]{1,0:T(8,128)S(1)} %add.66), channel_id=1, source_target_pairs={{0,8},{4,12},{8,0},{12,4},{16,24},{20,28},{24,16},{28,20},{1,9},{5... | collective-permute-start | bytes 49160 | tf_op jit(solution)/shard_map/ppermute | solution.py:27
  71.7 12.3 %all-to-all-start.1 = ((f32[32,8,128]{2,1,0:T(8,128)}), f32[32,8,128]{2,1,0:T(8,128)S(1)}, u32[]{:S(2)}, u32[]{:S(2)}) async-start(f32[32,8,128]{2,1,0:T(8,128)} %get-tuple-element.16), calls=%async_computation.1 | async-start | bytes 262144 | tf_op jit(solution)/shard_map/all_to_all | solution.py:513
  75.8 8.2 %copy-start.1 = (f32[1,1,4]{2,1,0:T(1,128)S(1)}, f32[1,1,4]{2,1,0:T(1,128)}, u32[]{:S(2)}) copy-start(f32[1,1,4]{2,1,0:T(1,128)} %param.8) | copy-start | bytes 52

commit v7 on v6

--- a/solution.py
+++ b/solution.py
@@ -17,6 +17,7 @@
 SPAN = 256
 GROUP = 16
 HALF_LANE = 64
+LINK_LANE = 96
 VMEM_LARGE = 56 * 1024 * 1024
 VMEM_SMALL = 48 * 1024 * 1024
 EXACT = lax.Precision.HIGHEST
@@ -100,7 +101,7 @@
 
 
 def small(tiles):
-    return tiles <= HALF_LANE
+    return tiles <= LANE - LINK_LANE
 
 
 def vmem_params(tiles):
@@ -144,7 +145,7 @@
         seen_ref[s] = jnp.sum(out.reshape(blocks, 2, 8, WIDE), axis=1)
         return carry
 
-    lax.fori_loop(0, tiles, build, 0, unroll=16)
+    lax.fori_loop(0, tiles, build, 0, unroll=32)
     column = lax.broadcasted_iota(jnp.int32, (2, 8, WIDE), 2) + WIDE * lax.broadcasted_iota(
         jnp.int32, (2, 8, WIDE), 0
     )
@@ -187,7 +188,7 @@
             )
         return carry
 
-    lax.fori_loop(0, tiles, respond, 0, unroll=16)
+    lax.fori_loop(0, tiles, respond, 0, unroll=32)
 
 
 def prepare(pair, table, cols, stride, pair_count):
@@ -341,7 +342,10 @@
     else:
         shared = jnp.concatenate([now, later], axis=0)
     for s in range(tiles):
-        message_ref[s] = jnp.concatenate([shared, extra_ref[s]], axis=0)
+        if small(tiles):
+            message_ref[s] = shared + extra_ref[s]
+        else:
+            message_ref[s] = jnp.concatenate([shared, extra_ref[s]], axis=0)
 
 
 def second_kernel(
@@ -373,7 +377,7 @@
         pltpu.VMEM((2, LANE, LANE), jnp.bfloat16),
     ]
     if more:
-        lines = 8 if small(tiles) else 12
+        lines = 4 if small(tiles) else 12
         out_shape.append(jax.ShapeDtypeStruct((tiles, lines, LANE), jnp.float32))
         scratch.append(pltpu.VMEM((4, tiles, LANE), jnp.float32))
     scratch.append(pltpu.SemaphoreType.DMA((2, tiles // GROUP)))
@@ -395,7 +399,7 @@
     step = total[0:4] / pixels
     if small(tiles):
         later = pltpu.roll(total[0:4], HALF_LANE, 1)
-        links = total[4:8]
+        links = total[0:4]
     else:
         later = total[4:8]
         links = total[8:12]
@@ -428,7 +432,7 @@
     for source, target in enumerate((me, before, after)):
         at = pick(step, target)
         for k in range(4):
-            place = 4 * source + k
+            place = 4 * source + k + (LINK_LANE if small(tiles) else 0)
             reach = reach + at[k : k + 1] * links[:, place : place + 1]
     gain = pick(step, me) + (pick(later, me) - reach) / pixels
     line = lax.broadcasted_iota(jnp.int32, (4, LANE), 0)
@@ -504,7 +508,8 @@
     bands, effects, moments = prepare(place, table, cols, stride, pair_count)
     effects = effects[:, :, :3].transpose(2, 0, 1, 3).reshape(3, tiles, cols)
     extra = response_sums(moments[:, :, :3, :3], ax)
-    extra = jnp.pad(extra, ((0, 0), (0, 0), (0, LANE - 12)))
+    left = LINK_LANE if small(tiles) else 0
+    extra = jnp.pad(extra, ((0, 0), (0, 0), (left, LANE - 12 - left)))
 
     heights = in_vmem(heights, tiles)
     map_rows, message = run_pass(

time: 85.8 us -> 85 us (level)
  no operation moved by 1% of the time
where the time goes in v7:
time: 85 us; the launch traced here: 84.7 us
  waiting for transfers between devices  34.9 us (41%)
  Pallas kernels  25.9 us (30%)
  starting transfers between devices  19.5 us (23%)
  other arithmetic  2.08 us (2%)
  between operations  1.44 us (2%)
  local copies, waits for them, and re-layouts  0.94 us (1%)
    ppermute x5, waiting for transfers between devices, exchange(): lax.ppermute(value, axis, [(i, i ^ k) for i in range(size)])  30.9 us
    pallas_call x2, Pallas kernels, run_pass(): pl.pallas_call(functools.partial(body, tiles, row_total, stride, pair_cou...  14.8 us
    pallas_call x1, Pallas kernels, prepare(): pl.pallas_call(functools.partial(prepare_kernel, tiles, cols, stride, pai...  9.5 us
    ppermute x5, starting transfers between devices, exchange(): lax.ppermute(value, axis, [(i, i ^ k) for i in range(size)])  9.29 us
    all_to_all x1, starting transfers between devices, local(): lax.all_to_all(own_heights[0, 0].reshape(tiles, rows, cols), AXES, 0, 0,...  6.18 us
    all_to_all x1, starting transfers between devices, local(): got = in_vmem(lax.all_to_all(message, AXES, 0, 0, tiled=True), tiles)  4 us
    all_to_all x1, waiting for transfers between devices, local(): lax.all_to_all(own_heights[0, 0].reshape(tiles, rows, cols), AXES, 0, 0,...  3.02 us
  transfers between devices with their start and end apart: 7, of which 7 were waited for; matrix products, arithmetic and copies ran while one was open for 2% of the time, Pallas kernels for 19%

profile of v7, /device:TPU:0, one launch (start us, length us, event | category | flops | bytes accessed | tf_op | source)
XLA Modules:
  0.0 84.7 jit_solution(2787613550923457468)
XLA Ops:
  1.3 0.7 convert_bitcast_fusion
  2.0 0.7 select_maximum_fusion
  2.7 4.0 %collective-permute-start = (f32[1,128]{1,0:T(1,128)S(1)}, f32[1,128]{1,0:T(1,128)S(1)}, u32[]{:S(2)}, u32[]{:S(2)}) collective-permute-start(f32[1,128]{1,0:T(1,128)S(1)} %bitcast.32), channel_id=1, source_target_pairs={{0,16},{4,20},{8,24},{12,28},{16,0},{20,4},{24,8},{28,12},{1,17},{... | collective-permute-start | bytes 1544 | tf_op jit(solution)/shard_map/ppermute | solution.py:28
  6.7 1.5 %collective-permute-done = f32[1,128]{1,0:T(1,128)S(1)} collective-permute-done((f32[1,128]{1,0:T(1,128)S(1)}, f32[1,128]{1,0:T(1,128)S(1)}, u32[]{:S(2)}, u32[]{:S(2)}) %collective-permute-start) | collective-permute-done | bytes 544 | tf_op jit(solution)/shard_map/ppermute | solution.py:28
  8.2 6.2 %all-to-all-start = ((bf16[32,32,1024]{2,1,0:T(8,128)(2,1)}), bf16[32,32,1024]{2,1,0:T(8,128)(2,1)S(1)}, u32[]{:S(2)}, u32[]{:S(2)}) async-start(bf16[32,32,1024]{2,1,0:T(8,128)(2,1)} %bitcast.28), calls=%async_computation | async-start | bytes 4194304 | tf_op jit(solution)/shard_map/all_to_all | solution.py:502
  14.5 0.1 pad.16.clone
  14.6 0.1 maximum_bitcast_fusion
  14.8 0.3 collective-permute-start.1
  15.0 0.9 %collective-permute-done.1 = f32[32,128]{1,0:T(8,128)S(1)} collective-permute-done((f32[32,128]{1,0:T(8,128)S(1)}, f32[32,128]{1,0:T(8,128)S(1)}, u32[]{:S(2)}, u32[]{:S(2)}) %collective-permute-start.1) | collective-permute-done | bytes 16416 | tf_op jit(solution)/shard_map/ppermute | solution.py:28
  16.0 1.8 %collective-permute-start.2 = (f32[32,128]{1,0:T(8,128)S(1)}, f32[32,128]{1,0:T(8,128)S(1)}, u32[]{:S(2)}, u32[]{:S(2)}) collective-permute-start(f32[32,128]{1,0:T(8,128)S(1)} %fusion), channel_id=1, source_target_pairs={{0,2},{1,3},{2,0},{3,1},{4,6},{5,7},{6,4},{7,5},{8,10},{9,11},{10,... | collective-permute-start | bytes 49160 | tf_op jit(solution)/shard_map/ppermute | solution.py:28
  17.9 10.3 %collective-permute-done.2 = f32[32,128]{1,0:T(8,128)S(1)} collective-permute-done((f32[32,128]{1,0:T(8,128)S(1)}, f32[32,128]{1,0:T(8,128)S(1)}, u32[]{:S(2)}, u32[]{:S(2)}) %collective-permute-start.2) | collective-permute-done | bytes 16416 | tf_op jit(solution)/shard_map/ppermute | solution.py:28
  28.1 0.1 fusion.1
  28.2 2.3 %collective-permute-start.3 = (f32[32,128]{1,0:T(8,128)S(1)}, f32[32,128]{1,0:T(8,128)S(1)}, u32[]{:S(2)}, u32[]{:S(2)}) collective-permute-start(f32[32,128]{1,0:T(8,128)S(1)} %fusion.1), channel_id=1, source_target_pairs={{0,4},{4,0},{8,12},{12,8},{16,20},{20,16},{24,28},{28,24},{1,5},{5... | collective-permute-start | bytes 49160 | tf_op jit(solution)/shard_map/ppermute | solution.py:28
  30.5 0.1 multiply_reduce_fusion.1
  30.7 2.1 %collective-permute-done.3 = f32[32,128]{1,0:T(8,128)S(1)} collective-permute-done((f32[32,128]{1,0:T(8,128)S(1)}, f32[32,128]{1,0:T(8,128)S(1)}, u32[]{:S(2)}, u32[]{:S(2)}) %collective-permute-start.3) | collective-permute-done | bytes 16416 | tf_op jit(solution)/shard_map/ppermute | solution.py:28
  32.8 0.9 %collective-permute-start.4 = (f32[32,128]{1,0:T(8,128)S(1)}, f32[32,128]{1,0:T(8,128)S(1)}, u32[]{:S(2)}, u32[]{:S(2)}) collective-permute-start(f32[32,128]{1,0:T(8,128)S(1)} %add.66), channel_id=1, source_target_pairs={{0,8},{4,12},{8,0},{12,4},{16,24},{20,28},{24,16},{28,20},{1,9},{5... | collective-permute-start | bytes 49160 | tf_op jit(solution)/shard_map/ppermute | solution.py:28
  33.7 0.1 pad_add_fusion.pair_ref.place_ref
  33.8 16.1 %collective-permute-done.4 = f32[32,128]{1,0:T(8,128)S(1)} collective-permute-done((f32[32,128]{1,0:T(8,128)S(1)}, f32[32,128]{1,0:T(8,128)S(1)}, u32[]{:S(2)}, u32[]{:S(2)}) %collective-permute-start.4) | collective-permute-done | bytes 16416 | tf_op jit(solution)/shard_map/ppermute | solution.py:28
  49.9 9.5 %shard_map.77 = (bf16[2,32,128,512]{3,2,1,0:T(8,128)(2,1)}, f32[32,4,8,256]{3,2,1,0:T(8,128)S(1)}, f32[32,3,8,128]{3,2,1,0:T(8,128)S(1)}) custom-call(s32[3]{0:T(128)S(1)} %pad_add_fusion.pair_ref.place_ref, f32[32,128]{1,0:T(8,128)S(1)} %add.67.words_ref.table_ref, f32[32,128]{1,0:T(8,128)S(1)} %add.67.words_ref.table_ref), custom_call_target="tpu_custom_call" | custom-call | tf_op jit(solution)/shard_map/pallas_call | solution.py:199
  59.4 0.1 slice_bitcast_fusion
  59.4 0.1 copy.11
  59.6 0.2 reshape.40.effect_ref
  59.8 0.1 copy.12
  59.9 0.1 multiply_reduce_fusion
  60.1 0.1 copy.16
  60.2 0.1 pad.10.extra_ref
  60.3 3.0 %all-to-all-done.height_ref = bf16[32,32,1024]{2,1,0:T(8,128)(2,1)S(1)} async-done(((bf16[32,32,1024]{2,1,0:T(8,128)(2,1)}), bf16[32,32,1024]{2,1,0:T(8,128)(2,1)S(1)}, u32[]{:S(2)}, u32[]{:S(2)}) %all-to-all-start) | async-done | bytes 2097184 | tf_op jit(solution)/shard_map/all_to_all | solution.py:502
  63.3 8.4 %shard_map.78 = (f32[32,1024]{1,0:T(8,128)S(1)}, f32[32,4,128]{2,1,0:T(4,128)}) custom-call(s32[3]{0:T(128)S(1)} %pad_add_fusion.pair_ref.place_ref, f32[32,128]{1,0:T(8,128)S(1)} %add.67.words_ref.table_ref, bf16[32,32,1024]{2,1,0:T(8,128)(2,1)S(1)} %all-to-all-done.height_ref, bf16[2,32,128,512]{3,2,1,0:T(8,128)(2,1)} %get-tuple-element.13.band_hbm, ...), custom_call_target="tpu_custom_call" | custom-call | tf_op jit(solution)/shard_map/pallas_call | solution.py:385
  71.7 4.0 %all-to-all-start.1 = ((f32[32,4,128]{2,1,0:T(4,128)}), f32[32,4,128]{2,1,0:T(4,128)S(1)}, u32[]{:S(2)}, u32[]{:S(2)}) async-start(f32[32,4,128]{2,1,0:T(4,128)} %get-tuple-element.16), calls=%async_computation.1 | async-start | bytes 131072 | tf_op jit(solution)/shard_map/all_to_all | solution.py:518
  75.7 6.4 %shard_map.79.map_ref = f32[32,1024]{1,0:T(8,128)S(1)} custom-call(s32[3]{0:T(128)S(1)} %pad_add_fusion.pair_ref.place_ref, f32[32,128]{1,0:T(8,128)S(1)} %add.67.words_ref.table_ref, bf16[32,32,1024]{2,1,0:T(8,128)(2,1)S(1)} %all-to-all-done.height_ref, bf16[2,32,128,512]{3,2,1,0:T(8,128)(2,1)} %get-tuple-element.13.band_hbm, ...), custom_call_target="tpu_custom_call" | custom-call | tf_op jit(solution)/shard_map/pallas_call | solution.py:385
  82.2 1.0 %all-to-all-done.1.got_ref = f32[32,4,128]{2,1,0:T(4,128)S(1)} async-done(((f32[32,4,128]{2,1,0:T(4,128)}), f32[32,4,128]{2,1,0:T(4,128)S(1)}, u32[]{:S(2)}, u32[]{:S(2)}) %all-to-all-start.1) | async-done | bytes 65568 | tf_op jit(solution)/shard_map/all_to_all | solution.py:518
  83.1 1.6 %shard_map.80 = (f32[32,1024]{1,0:T(8,128)}, f32[1,4]{1,0:T(1,128)}) custom-call(s32[3]{0:T(128)S(1)} %pad_add_fusion.pair_ref.place_ref, f32[32,4,128]{2,1,0:T(4,128)S(1)} %all-to-all-done.1.got_ref, f32[32,1024]{1,0:T(8,128)S(1)} %shard_map.79.map_ref, f32[3,32,1024]{2,1,0:T(8,128)S(1)} %reshape.40.effect_ref, f32[1,4]{1,0:T(1,128)S(1)} %bitcast.27), custom_call_target="tpu_custom_call" | custom-call | tf_op jit(solution)/shard_map/pallas_call | solution.py:447
  (21 shorter events, 0.3 us)
Async XLA Ops:
  2.7 5.6 %collective-permute-start = (f32[1,128]{1,0:T(1,128)S(1)}, f32[1,128]{1,0:T(1,128)S(1)}, u32[]{:S(2)}, u32[]{:S(2)}) collective-permute-start(f32[1,128]{1,0:T(1,128)S(1)} %bitcast.32), channel_id=1, source_target_pairs={{0,16},{4,20},{8,24},{12,28},{16,0},{20,4},{24,8},{28,12},{1,17},{... | collective-permute-start | bytes 1544 | tf_op jit(solution)/shard_map/ppermute | solution.py:28
  8.2 9.6 %copy-start.2 = (f32[1,3,32]{2,1,0:T(4,128)S(1)}, f32[1,3,32]{2,1,0:T(4,128)}, u32[]{:S(2)}) copy-start(f32[1,3,32]{2,1,0:T(4,128)} %constant.43.clone.1) | copy-start | bytes 1156
  8.2 9.6 %copy-start.3 = (f32[1,3,32]{2,1,0:T(4,128)S(1)}, f32[1,3,32]{2,1,0:T(4,128)}, u32[]{:S(2)}) copy-start(f32[1,3,32]{2,1,0:T(4,128)} %constant.44.clone.1) | copy-start | bytes 1156
  8.2 55.1 %all-to-all-start = ((bf16[32,32,1024]{2,1,0:T(8,128)(2,1)}), bf16[32,32,1024]{2,1,0:T(8,128)(2,1)S(1)}, u32[]{:S(2)}, u32[]{:S(2)}) async-start(bf16[32,32,1024]{2,1,0:T(8,128)(2,1)} %bitcast.28), calls=%async_computation | async-start | bytes 4194304 | tf_op jit(solution)/shard_map/all_to_all | solution.py:502
  14.4 48.9 %copy-start = (f32[32,1024]{1,0:T(8,128)S(1)}, f32[32,1024]{1,0:T(8,128)}, u32[]{:S(2)}) copy-start(f32[32,1024]{1,0:T(8,128)} %ref_ref.1) | copy-start | bytes 393220
  14.8 1.2 %collective-permute-start.1 = (f32[32,128]{1,0:T(8,128)S(1)}, f32[32,128]{1,0:T(8,128)S(1)}, u32[]{:S(2)}, u32[]{:S(2)}) collective-permute-start(f32[32,128]{1,0:T(8,128)S(1)} %select_select_fusion), channel_id=1, source_target_pairs={{0,1},{1,0},{2,3},{3,2},{4,5},{5,4},{6,7},{7,6},{8,9},{9,8},{10,11... | collective-permute-start | bytes 49160 | tf_op jit(solution)/shard_map/ppermute | solution.py:28
  16.0 12.1 %collective-permute-start.2 = (f32[32,128]{1,0:T(8,128)S(1)}, f32[32,128]{1,0:T(8,128)S(1)}, u32[]{:S(2)}, u32[]{:S(2)}) collective-permute-start(f32[32,128]{1,0:T(8,128)S(1)} %fusion), channel_id=1, source_target_pairs={{0,2},{1,3},{2,0},{3,1},{4,6},{5,7},{6,4},{7,5},{8,10},{9,11},{10,... | collective-permute-start | bytes 49160 | tf_op jit(solution)/shard_map/ppermute | solution.py:28
  28.2 4.5 %collective-permute-start.3 = (f32[32,128]{1,0:T(8,128)S(1)}, f32[32,128]{1,0:T(8,128)S(1)}, u32[]{:S(2)}, u32[]{:S(2)}) collective-permute-start(f32[32,128]{1,0:T(8,128)S(1)} %fusion.1), channel_id=1, source_target_pairs={{0,4},{4,0},{8,12},{12,8},{16,20},{20,16},{24,28},{28,24},{1,5},{5... | collective-permute-start | bytes 49160 | tf_op jit(solution)/shard_map/ppermute | solution.py:28
  32.8 17.1 %collective-permute-start.4 = (f32[32,128]{1,0:T(8,128)S(1)}, f32[32,128]{1,0:T(8,128)S(1)}, u32[]{:S(2)}, u32[]{:S(2)}) collective-permute-start(f32[32,128]{1,0:T(8,128)S(1)} %add.66), channel_id=1, source_target_pairs={{0,8},{4,12},{8,0},{12,4},{16,24},{20,28},{24,16},{28,20},{1,9},{5... | collective-permute-start | bytes 49160 | tf_op jit(solution)/shard_map/ppermute | solution.py:28
  71.7 11.4 %all-to-all-start.1 = ((f32[32,4,128]{2,1,0:T(4,128)}), f32[32,4,128]{2,1,0:T(4,128)S(1)}, u32[]{:S(2)}, u32[]{:S(2)}) async-start(f32[32,4,128]{2,1,0:T(4,128)} %get-tuple-element.16), calls=%async_computation.1 | async-start | bytes 131072 | tf_op jit(solution)/shard_map/all_to_all | solution.py:518
  75.7 7.4 %copy-start.1 = (f32[1,1,4]{2,1,0:T(1,128)S(1)}, f32[1,1,4]{2,1,0:T(1,128)}, u32[]{:S(2)}) copy-start(f32[1,1,4]{2,1,0:T(1,128)} %param.8) | copy-start | bytes 52
